TPU v7x, 256 devices: a whole 4x4x8 slice. The times are simulated.
256 devices in a mesh: states: 256 (over x, y, z, core).
Axes of the slice: x: 4, y: 4, z: 8, core: 2. Of those that a mesh axis runs over, the one named last changes fastest.
Arguments:
- tiles: float32 [16, 256, 4, 128, 128], P(None, 'states'), may hold values from 0.001 to 1
- counts: int32 [256], P('states'), may hold values from 1 to 4
- col_index: int32 [256, 4], P('states'), may hold values from 0 to 255
- reward: float32 [16, 32768], P(None, 'states'), may hold values from -2.4 to 2.4
- policy: int32 [2, 32768], P(None, 'states'), may hold values from 0 to 15
- start_values: float32 [32768], P('states'), may hold values from -6 to 6
Outputs:
- final_values: float32 [32768], P('states')
- bounds: float32 [2, 2], replicated
Inputs may be any that keep to these rules, and one draw needn't show every extreme that they name: Only the tile slots below counts of a row block enter W_a and row_total; slots at or above it hold arbitrary values that are ignored.
All inputs are finite; a program needn't handle non-finite values.
Results may differ from a plain program's by a relative error of at most 0.00014.
Values sent between devices are 32-bit elements; how exact they have to be, the bound alone decides.
No kernel may reach another device: no remote copies, remote signals or barrier semaphores. Data moves between devices by JAX's collectives and lax.ppermute only.
A program may use at most 64 MiB of HBM per device.

v0:
```python
import jax
import jax.numpy as jnp
from jax import lax
from jax.sharding import Mesh
from jax.sharding import PartitionSpec as P

SWEEPS = 2
EVALS = 2
STATES = ("states_0", "states_1", "states_2", "states_3")


discount = 0.9
precise = lax.Precision.HIGHEST


def sent_to_all(x, axis):
    devices = lax.axis_size(axis)
    return lax.all_to_all(jnp.broadcast_to(x[None], (devices, *x.shape)), axis, 0, 0, tiled=True)


def laid_out(parts, dim):
    parts = jnp.moveaxis(parts, 0, dim)
    shape = parts.shape
    return parts.reshape(*shape[:dim], shape[dim] * shape[dim + 1], *shape[dim + 2 :])


def gather_axes(x, axes, dim):
    far, near = axes
    leading = sent_to_all(x, far)
    parts = jnp.swapaxes(sent_to_all(leading, near), 0, 1)
    return laid_out(parts.reshape(-1, *x.shape), dim)


def apply_tiles(tile_set, blocks, form):
    return jnp.einsum(form, tile_set, blocks, precision=precise)


def local(tiles, counts, col_index, reward, policy, start_values):
    actions, blocks_here, slot_count, tile_width, _ = tiles.shape
    live_mask = (jnp.arange(slot_count)[None, :] < counts[:, None]).astype(jnp.float32)
    row_total = jnp.einsum("abkrc,bk->abr", tiles, live_mask, precision=precise)
    reward_blocks = reward.reshape(actions, blocks_here, tile_width)

    def fetch(gathered):
        blocks = gathered.reshape(-1, tile_width)[col_index]
        return blocks * live_mask[:, :, None]

    values = start_values
    bound_rows = []
    for sweep_index in range(SWEEPS):
        gathered = gather_axes(values, ("states_0", ("states_1", "states_2", "states_3")), 0)
        weighted = apply_tiles(tiles, fetch(gathered), "abkrc,bkc->abr")
        action_values = reward_blocks + discount * (weighted / row_total)
        backup = jnp.max(action_values, axis=0).reshape(-1)
        change = backup - values
        top_bound = jnp.max(change)
        bottom = jnp.min(change)
        gathered, stat_pairs = (
            gather_axes(backup, ("states_0", ("states_1", "states_2", "states_3")), 0),
            gather_axes(
                jnp.stack([top_bound, -bottom]),
                ("states_0", ("states_1", "states_2", "states_3")),
                0,
            ),
        )
        stat_pairs = stat_pairs.reshape(-1, 2)
        top_bound = jnp.max(stat_pairs[:, 0])
        bottom = -jnp.max(stat_pairs[:, 1])
        offset = discount / (1.0 - discount) * 0.5 * (bottom + top_bound)
        gathered = gathered + offset
        bound_rows.append(jnp.stack([bottom, top_bound]))
        onehot = (policy[sweep_index][None, :] == jnp.arange(actions)[:, None]).astype(jnp.float32)
        onehot_blocks = onehot.reshape(actions, blocks_here, tile_width)
        picked = jnp.einsum("abr,abkrc->bkrc", onehot_blocks, tiles, precision=precise)
        picked_total = jnp.sum(onehot_blocks * row_total, axis=0)
        picked_reward = jnp.sum(onehot * reward, axis=0)
        current = backup + offset
        for eval_turn in range(EVALS):
            if eval_turn > 0:
                gathered = gather_axes(
                    current, ("states_0", ("states_1", "states_2", "states_3")), 0
                )
            weighted = apply_tiles(picked, fetch(gathered), "bkrc,bkc->br")
            current = picked_reward + discount * (weighted / picked_total).reshape(-1)
        values = current
    return (values, jnp.stack(bound_rows))


def solution(mesh):
    split = Mesh(mesh.devices.reshape(4, 4, 8, 2), ("states_0", "states_1", "states_2", "states_3"))
    placed = (
        P(None, STATES, None, None, None),
        P(STATES),
        P(STATES, None),
        P(None, STATES),
        P(None, STATES),
        P(STATES),
    )
    return jax.shard_map(
        local, mesh=split, in_specs=placed, out_specs=(P(STATES), P()), check_vma=False
    )
```

profile of v0, /device:TPU:1, one launch (start us, length us, event | category | flops | bytes accessed | tf_op | source)
XLA Modules:
  0.0 227.5 jit_solution(10913317788372415305)
XLA Ops:
  0.6 1.3 broadcast_in_dim.50
  1.9 4.8 %all-to-all-start = ((f32[4,1,128]{2,1,0:T(1,128)}), f32[4,1,128]{2,1,0:T(1,128)S(1)}, u32[]{:S(2)}, u32[]{:S(2)}) async-start(f32[4,1,128]{2,1,0:T(1,128)} %broadcast_in_dim.50), calls=%async_computation | async-start | bytes 4096 | tf_op jit(solution)/shard_map/all_to_all | solution.py:18
  8.8 2.0 all-to-all-done
  11.5 13.6 %all-to-all-start.1 = ((f32[64,4,128]{2,1,0:T(4,128)}), f32[64,4,128]{2,1,0:T(4,128)S(1)}, u32[]{:S(2)}, u32[]{:S(2)}) async-start(f32[64,4,128]{2,1,0:T(4,128)} %broadcast_in_dim.52), calls=%async_computation.1 | async-start | bytes 262144 | tf_op jit(solution)/shard_map/all_to_all | solution.py:18
  25.1 3.4 %reduce_sum.47 = f32[16,4,128]{2,1,0:T(4,128)S(1)} reduce(f32[16,1,4,128,128]{4,3,2,1,0:T(8,128)} %param.6, f32[]{:T(128)} %constant.7.clone.1), dimensions={1,4}, to_apply=%region_2.0 | reduce | flops 1040384 | bytes 4227076 | tf_op jit(solution)/shard_map/abkrc,bk->abr/reduce_sum | solution.py:41
  28.7 6.8 %all-to-all-done.1 = f32[64,4,128]{2,1,0:T(4,128)S(1)} async-done(((f32[64,4,128]{2,1,0:T(4,128)}), f32[64,4,128]{2,1,0:T(4,128)S(1)}, u32[]{:S(2)}, u32[]{:S(2)}) %all-to-all-start.1) | async-done | bytes 131104 | tf_op jit(solution)/shard_map/all_to_all | solution.py:18
  36.1 5.2 %fusion.29 = f32[1,16,128,1]{2,0,3,1:T(1,128)S(1)} fusion(f32[4,128,1,1]{1,2,0,3:T(1,128)S(1)} %bitcast.176, f32[16,1,4,128,128]{4,3,2,1,0:T(8,128)} %param.6), kind=kOutput, calls=%fused_computation.73 | convolution fusion | flops 12582912 | bytes 4204544 | tf_op jit(solution)/shard_map/abkrc,bkc->abr/dot_general | solution.py:35
  43.4 6.4 %all_to_all.88 = f32[4,1,2]{2,1,0:T(1,128)S(1)} all-to-all(f32[4,1,2]{2,1,0:T(1,128)S(1)} %broadcast_in_dim.57), channel_id=1, replica_groups=mesh['states_0'=4,'states_1'=4,'states_2'=8,'states_3'=2] {'states_0'}, dimensions={0} | all-to-all | bytes 64 | tf_op jit(solution)/shard_map/all_to_all | solution.py:18
  50.4 3.2 %all-to-all-start.2 = ((f32[4,1,128]{2,1,0:T(1,128)}), f32[4,1,128]{2,1,0:T(1,128)S(1)}, u32[]{:S(2)}, u32[]{:S(2)}) async-start(f32[4,1,128]{2,1,0:T(1,128)} %broadcast_in_dim.54), calls=%async_computation.2 | async-start | bytes 4096 | tf_op jit(solution)/shard_map/all_to_all | solution.py:18
  53.7 4.0 %all-to-all-done.2 = f32[4,1,128]{2,1,0:T(1,128)S(1)} async-done(((f32[4,1,128]{2,1,0:T(1,128)}), f32[4,1,128]{2,1,0:T(1,128)S(1)}, u32[]{:S(2)}, u32[]{:S(2)}) %all-to-all-start.2) | async-done | bytes 2080 | tf_op jit(solution)/shard_map/all_to_all | solution.py:18
  58.4 7.1 %all-to-all-start.5 = ((f32[64,4,2]{1,2,0:T(2,128)}), f32[64,4,2]{1,2,0:T(2,128)S(1)}, u32[]{:S(2)}, u32[]{:S(2)}) async-start(f32[64,4,2]{1,2,0:T(2,128)} %broadcast_in_dim.59), calls=%async_computation.5 | async-start | bytes 131072 | tf_op jit(solution)/shard_map/all_to_all | solution.py:18
  65.6 9.6 %all-to-all-done.5 = f32[64,4,2]{1,2,0:T(2,128)S(1)} async-done(((f32[64,4,2]{1,2,0:T(2,128)}), f32[64,4,2]{1,2,0:T(2,128)S(1)}, u32[]{:S(2)}, u32[]{:S(2)}) %all-to-all-start.5) | async-done | bytes 2080 | tf_op jit(solution)/shard_map/all_to_all | solution.py:18
  75.9 4.4 %all-to-all-start.3 = ((f32[64,4,128]{2,1,0:T(4,128)}), f32[64,4,128]{2,1,0:T(4,128)S(1)}, u32[]{:S(2)}, u32[]{:S(2)}) async-start(f32[64,4,128]{2,1,0:T(4,128)} %broadcast_in_dim.56), calls=%async_computation.3 | async-start | bytes 262144 | tf_op jit(solution)/shard_map/all_to_all | solution.py:18
  80.3 6.8 %fusion = f32[128,1,4,128]{3,1,2,0:T(1,128)S(1)} fusion(pred[16,128,1,1]{0,2,3,1:T(4,128)(4,1)S(1)} %copy.23, f32[16,4,128,128]{3,2,1,0:T(8,128)} %bitcast.147), kind=kOutput, calls=%fused_computation.6 | convolution fusion | flops 12582912 | bytes 4458496 | tf_op jit(solution)/shard_map/abr,abkrc->bkrc/dot_general | solution.py:74
  89.2 1.6 all-to-all-done.3
  91.8 6.5 %all_to_all.89 = f32[4,1,128]{2,1,0:T(1,128)S(1)} all-to-all(f32[4,1,128]{2,1,0:T(1,128)S(1)} %broadcast_in_dim.60), channel_id=1, replica_groups=mesh['states_0'=4,'states_1'=4,'states_2'=8,'states_3'=2] {'states_0'}, dimensions={0} | all-to-all | bytes 4096 | tf_op jit(solution)/shard_map/all_to_all | solution.py:18
  98.3 20.2 %all_to_all.90 = f32[64,4,128]{2,1,0:T(4,128)S(1)} all-to-all(f32[64,4,128]{2,1,0:T(4,128)S(1)} %broadcast_in_dim.62), channel_id=1, replica_groups=mesh['states_0'=4,'states_1'=4,'states_2'=8,'states_3'=2] {'states_1','s..., dimensions={0} | all-to-all | bytes 262144 | tf_op jit(solution)/shard_map/all_to_all | solution.py:18
  119.5 6.5 %all_to_all.91 = f32[4,1,128]{2,1,0:T(1,128)S(1)} all-to-all(f32[4,1,128]{2,1,0:T(1,128)S(1)} %broadcast_in_dim.63), channel_id=1, replica_groups=mesh['states_0'=4,'states_1'=4,'states_2'=8,'states_3'=2] {'states_0'}, dimensions={0} | all-to-all | bytes 4096 | tf_op jit(solution)/shard_map/all_to_all | solution.py:18
  126.0 16.2 %all_to_all.92 = f32[64,4,128]{2,1,0:T(4,128)S(1)} all-to-all(f32[64,4,128]{2,1,0:T(4,128)S(1)} %broadcast_in_dim.65), channel_id=1, replica_groups=mesh['states_0'=4,'states_1'=4,'states_2'=8,'states_3'=2] {'states_1','s..., dimensions={0} | all-to-all | bytes 262144 | tf_op jit(solution)/shard_map/all_to_all | solution.py:18
  142.8 5.2 %fusion.31 = f32[1,16,128,1]{2,0,3,1:T(1,128)S(1)} fusion(f32[4,128,1,1]{1,2,0,3:T(1,128)S(1)} %bitcast.179, f32[16,1,4,128,128]{4,3,2,1,0:T(8,128)} %param.6), kind=kOutput, calls=%fused_computation.75 | convolution fusion | flops 12582912 | bytes 4204544 | tf_op jit(solution)/shard_map/abkrc,bkc->abr/dot_general | solution.py:35
  150.1 6.4 %all_to_all.93 = f32[4,1,2]{2,1,0:T(1,128)S(1)} all-to-all(f32[4,1,2]{2,1,0:T(1,128)S(1)} %broadcast_in_dim.69), channel_id=1, replica_groups=mesh['states_0'=4,'states_1'=4,'states_2'=8,'states_3'=2] {'states_0'}, dimensions={0} | all-to-all | bytes 64 | tf_op jit(solution)/shard_map/all_to_all | solution.py:18
  157.1 3.2 %all-to-all-start.10 = ((f32[4,1,128]{2,1,0:T(1,128)}), f32[4,1,128]{2,1,0:T(1,128)S(1)}, u32[]{:S(2)}, u32[]{:S(2)}) async-start(f32[4,1,128]{2,1,0:T(1,128)} %broadcast_in_dim.66), calls=%async_computation.10 | async-start | bytes 4096 | tf_op jit(solution)/shard_map/all_to_all | solution.py:18
  160.5 4.0 %all-to-all-done.10 = f32[4,1,128]{2,1,0:T(1,128)S(1)} async-done(((f32[4,1,128]{2,1,0:T(1,128)}), f32[4,1,128]{2,1,0:T(1,128)S(1)}, u32[]{:S(2)}, u32[]{:S(2)}) %all-to-all-start.10) | async-done | bytes 2080 | tf_op jit(solution)/shard_map/all_to_all | solution.py:18
  165.1 7.0 %all-to-all-start.13 = ((f32[64,4,2]{1,2,0:T(2,128)}), f32[64,4,2]{1,2,0:T(2,128)S(1)}, u32[]{:S(2)}, u32[]{:S(2)}) async-start(f32[64,4,2]{1,2,0:T(2,128)} %broadcast_in_dim.71), calls=%async_computation.13 | async-start | bytes 131072 | tf_op jit(solution)/shard_map/all_to_all | solution.py:18
  172.3 9.6 %all-to-all-done.13 = f32[64,4,2]{1,2,0:T(2,128)S(1)} async-done(((f32[64,4,2]{1,2,0:T(2,128)}), f32[64,4,2]{1,2,0:T(2,128)S(1)}, u32[]{:S(2)}, u32[]{:S(2)}) %all-to-all-start.13) | async-done | bytes 2080 | tf_op jit(solution)/shard_map/all_to_all | solution.py:18
  182.6 4.4 %all-to-all-start.11 = ((f32[64,4,128]{2,1,0:T(4,128)}), f32[64,4,128]{2,1,0:T(4,128)S(1)}, u32[]{:S(2)}, u32[]{:S(2)}) async-start(f32[64,4,128]{2,1,0:T(4,128)} %broadcast_in_dim.68), calls=%async_computation.11 | async-start | bytes 262144 | tf_op jit(solution)/shard_map/all_to_all | solution.py:18
  187.0 6.8 %fusion.2 = f32[128,1,4,128]{3,1,2,0:T(1,128)S(1)} fusion(pred[16,128,1,1]{0,2,3,1:T(4,128)(4,1)S(1)} %copy.20, f32[16,4,128,128]{3,2,1,0:T(8,128)} %bitcast.148), kind=kOutput, calls=%fused_computation.8 | convolution fusion | flops 12582912 | bytes 4458496 | tf_op jit(solution)/shard_map/abr,abkrc->bkrc/dot_general | solution.py:74
  195.9 1.6 all-to-all-done.11
  198.4 6.5 %all_to_all.94 = f32[4,1,128]{2,1,0:T(1,128)S(1)} all-to-all(f32[4,1,128]{2,1,0:T(1,128)S(1)} %broadcast_in_dim.72), channel_id=1, replica_groups=mesh['states_0'=4,'states_1'=4,'states_2'=8,'states_3'=2] {'states_0'}, dimensions={0} | all-to-all | bytes 4096 | tf_op jit(solution)/shard_map/all_to_all | solution.py:18
  205.6 10.0 %all-to-all-start.15 = ((f32[64,4,128]{2,1,0:T(4,128)}), f32[64,4,128]{2,1,0:T(4,128)S(1)}, u32[]{:S(2)}, u32[]{:S(2)}) async-start(f32[64,4,128]{2,1,0:T(4,128)} %broadcast_in_dim.74), calls=%async_computation.15 | async-start | bytes 262144 | tf_op jit(solution)/shard_map/all_to_all | solution.py:18
  217.6 8.4 %all-to-all-done.15 = f32[64,4,128]{2,1,0:T(4,128)S(1)} async-done(((f32[64,4,128]{2,1,0:T(4,128)}), f32[64,4,128]{2,1,0:T(4,128)S(1)}, u32[]{:S(2)}, u32[]{:S(2)}) %all-to-all-start.15) | async-done | bytes 131104 | tf_op jit(solution)/shard_map/all_to_all | solution.py:18
  226.6 0.8 fusion.15
  (67 shorter events, 18.4 us)
Async XLA Ops:
  1.9 8.9 %all-to-all-start = ((f32[4,1,128]{2,1,0:T(1,128)}), f32[4,1,128]{2,1,0:T(1,128)S(1)}, u32[]{:S(2)}, u32[]{:S(2)}) async-start(f32[4,1,128]{2,1,0:T(1,128)} %broadcast_in_dim.50), calls=%async_computation | async-start | bytes 4096 | tf_op jit(solution)/shard_map/all_to_all | solution.py:18
  11.5 24.0 %all-to-all-start.1 = ((f32[64,4,128]{2,1,0:T(4,128)}), f32[64,4,128]{2,1,0:T(4,128)S(1)}, u32[]{:S(2)}, u32[]{:S(2)}) async-start(f32[64,4,128]{2,1,0:T(4,128)} %broadcast_in_dim.52), calls=%async_computation.1 | async-start | bytes 262144 | tf_op jit(solution)/shard_map/all_to_all | solution.py:18
  25.1 16.2 %copy-start = (f32[16,128]{1,0:T(8,128)S(1)}, f32[16,128]{1,0:T(8,128)}, u32[]{:S(2)}) copy-start(f32[16,128]{1,0:T(8,128)} %param.9) | copy-start | bytes 24580
  25.1 16.3 %copy-start.1 = (f32[128]{0:T(128)S(1)}, f32[128]{0:T(128)}, u32[]{:S(2)}) copy-start(f32[128]{0:T(128)} %param.11) | copy-start | bytes 1540
  50.4 7.3 %all-to-all-start.2 = ((f32[4,1,128]{2,1,0:T(1,128)}), f32[4,1,128]{2,1,0:T(1,128)S(1)}, u32[]{:S(2)}, u32[]{:S(2)}) async-start(f32[4,1,128]{2,1,0:T(1,128)} %broadcast_in_dim.54), calls=%async_computation.2 | async-start | bytes 4096 | tf_op jit(solution)/shard_map/all_to_all | solution.py:18
  58.4 16.9 %all-to-all-start.5 = ((f32[64,4,2]{1,2,0:T(2,128)}), f32[64,4,2]{1,2,0:T(2,128)S(1)}, u32[]{:S(2)}, u32[]{:S(2)}) async-start(f32[64,4,2]{1,2,0:T(2,128)} %broadcast_in_dim.59), calls=%async_computation.5 | async-start | bytes 131072 | tf_op jit(solution)/shard_map/all_to_all | solution.py:18
  75.9 14.9 %all-to-all-start.3 = ((f32[64,4,128]{2,1,0:T(4,128)}), f32[64,4,128]{2,1,0:T(4,128)S(1)}, u32[]{:S(2)}, u32[]{:S(2)}) async-start(f32[64,4,128]{2,1,0:T(4,128)} %broadcast_in_dim.56), calls=%async_computation.3 | async-start | bytes 262144 | tf_op jit(solution)/shard_map/all_to_all | solution.py:18
  157.1 7.3 %all-to-all-start.10 = ((f32[4,1,128]{2,1,0:T(1,128)}), f32[4,1,128]{2,1,0:T(1,128)S(1)}, u32[]{:S(2)}, u32[]{:S(2)}) async-start(f32[4,1,128]{2,1,0:T(1,128)} %broadcast_in_dim.66), calls=%async_computation.10 | async-start | bytes 4096 | tf_op jit(solution)/shard_map/all_to_all | solution.py:18
  165.1 16.8 %all-to-all-start.13 = ((f32[64,4,2]{1,2,0:T(2,128)}), f32[64,4,2]{1,2,0:T(2,128)S(1)}, u32[]{:S(2)}, u32[]{:S(2)}) async-start(f32[64,4,2]{1,2,0:T(2,128)} %broadcast_in_dim.71), calls=%async_computation.13 | async-start | bytes 131072 | tf_op jit(solution)/shard_map/all_to_all | solution.py:18
  182.6 14.9 %all-to-all-start.11 = ((f32[64,4,128]{2,1,0:T(4,128)}), f32[64,4,128]{2,1,0:T(4,128)S(1)}, u32[]{:S(2)}, u32[]{:S(2)}) async-start(f32[64,4,128]{2,1,0:T(4,128)} %broadcast_in_dim.68), calls=%async_computation.11 | async-start | bytes 262144 | tf_op jit(solution)/shard_map/all_to_all | solution.py:18
  205.6 20.4 %all-to-all-start.15 = ((f32[64,4,128]{2,1,0:T(4,128)}), f32[64,4,128]{2,1,0:T(4,128)S(1)}, u32[]{:S(2)}, u32[]{:S(2)}) async-start(f32[64,4,128]{2,1,0:T(4,128)} %broadcast_in_dim.74), calls=%async_computation.15 | async-start | bytes 262144 | tf_op jit(solution)/shard_map/all_to_all | solution.py:18
where the time goes:
time: 229 us; the launch traced here: 227 us
  blocking collectives  68.8 us (30%)
  starting transfers between devices  57.9 us (25%)
  waiting for transfers between devices  47.6 us (21%)
  matrix products  25.9 us (11%)
  local copies, waits for them, and re-layouts  11.4 us (5%)
  other arithmetic  10.6 us (5%)
  between operations  5.22 us (2%)
    all_to_all x7, blocking collectives, sent_to_all(): lax.all_to_all(jnp.broadcast_to(x[None], (devices, *x.shape)), axis, 0, 0...  68.8 us
    all_to_all x9, starting transfers between devices, sent_to_all(): lax.all_to_all(jnp.broadcast_to(x[None], (devices, *x.shape)), axis, 0, 0...  57.9 us
    all_to_all x9, waiting for transfers between devices, sent_to_all(): lax.all_to_all(jnp.broadcast_to(x[None], (devices, *x.shape)), axis, 0, 0...  47.6 us
    dot_general x2, matrix products, local(): jnp.einsum('abr,abkrc->bkrc', onehot_blocks, tiles, precision=precise)  13.6 us
    dot_general x6, matrix products, apply_tiles(): return jnp.einsum(form, tile_set, blocks, precision=precise)  12.1 us
    broadcast_in_dim x16, local copies, waits for them, and re-layouts, sent_to_all(): jnp.broadcast_to(x[None], (devices, *x.shape))  6.4 us
  transfers between devices with their start and end apart: 9, of which 9 were waited for; matrix products, arithmetic and copies ran while one was open for 10% of the time, Pallas kernels for 0%

commit v1 on v0

v1 whole, which is shorter than its diff:
```python
import functools

import jax
import jax.numpy as jnp
from jax import lax
from jax.experimental import pallas as pl
from jax.experimental.pallas import tpu as pltpu
from jax.sharding import Mesh
from jax.sharding import PartitionSpec as P

SWEEPS = 2
EVALS = 2
AXES = ("x", "y", "z", "c")
discount = 0.9
shift = discount / (1.0 - discount) * 0.5
MIB = 1 << 20


def piece_sums(rows, values):
    high = values.astype(jnp.bfloat16)
    rest = values - high.astype(jnp.float32)
    middle = rest.astype(jnp.bfloat16)
    low = (rest - middle.astype(jnp.float32)).astype(jnp.bfloat16)
    dims = (((1,), (1,)), ((), ()))
    out = lax.dot_general(rows, high, dims, preferred_element_type=jnp.float32)
    out += lax.dot_general(rows, middle, dims, preferred_element_type=jnp.float32)
    return out + lax.dot_general(rows, low, dims, preferred_element_type=jnp.float32)


def row_of(index):
    at = lax.broadcasted_iota(jnp.int32, (16, 128), 0)
    return jnp.where(at == index, 1.0, 0.0).astype(jnp.bfloat16)


def prepare(counts, policy, reward, tiles, scale, picked, picked_scale, picked_reward, sums, columns):
    actions, slots, width, _ = tiles.shape
    for j in range(SWEEPS):
        wide = jnp.broadcast_to(policy[pl.ds(j, 1), :].astype(jnp.float32), (width, width))
        columns[j] = wide.T
    live = [counts[0] > k for k in range(slots)]

    def group(g, _):
        rows = pl.ds(pl.multiple_of(g * 8, 8), 8)
        chosen = [columns[j, rows, :] for j in range(SWEEPS)]
        held = [[jnp.zeros((8, width), jnp.float32) for _ in range(slots)] for _ in range(SWEEPS)]
        for a in range(actions):
            total = jnp.zeros((8, width), jnp.float32)
            for k in range(slots):
                tile = jnp.where(live[k], tiles[a, k, rows, :], 0.0)
                total += tile
                for j in range(SWEEPS):
                    held[j][k] = jnp.where(chosen[j] == float(a), tile, held[j][k])
            sums[a, rows, :] = total
        for j in range(SWEEPS):
            for k in range(slots):
                picked[j, k, rows, :] = held[j][k]
        return 0

    lax.fori_loop(0, width // 8, group, 0)
    totals = jnp.zeros((actions, width), jnp.float32)
    for a in range(actions):
        totals += piece_sums(row_of(a), sums[a])
    inverse = discount / totals
    scale[...] = inverse
    at = lax.broadcasted_iota(jnp.int32, (actions, width), 0)
    for j in range(SWEEPS):
        here = at == policy[pl.ds(j, 1), :]
        picked_scale[pl.ds(j, 1), :] = jnp.sum(jnp.where(here, inverse, 0.0), axis=0, keepdims=True)
        picked_reward[pl.ds(j, 1), :] = jnp.sum(jnp.where(here, reward[...], 0.0), axis=0, keepdims=True)


def fetched(counts, col_index, gathered, slots):
    out = []
    for k in range(slots):
        row = gathered[pl.ds(col_index[0, k], 1), :]
        out.append(jnp.where(counts[0] > k, row, 0.0))
    return out


def back_up(counts, col_index, gathered, tiles, reward, scale, out, sums):
    actions, slots, width, _ = tiles.shape
    blocks = [jnp.broadcast_to(b, (8, width)) for b in fetched(counts, col_index, gathered, slots)]

    def group(g, _):
        rows = pl.ds(pl.multiple_of(g * 8, 8), 8)
        for a in range(actions):
            total = tiles[a, 0, rows, :] * blocks[0]
            for k in range(1, slots):
                total += tiles[a, k, rows, :] * blocks[k]
            sums[a, rows, :] = total
        return 0

    lax.fori_loop(0, width // 8, group, 0)
    weighted = jnp.zeros((actions, width), jnp.float32)
    for a in range(actions):
        weighted += piece_sums(row_of(a), sums[a])
    backup = jnp.max(reward[...] + scale[...] * weighted, axis=0, keepdims=True)
    out[...] = jnp.broadcast_to(backup, out.shape)


def product(counts, col_index, gathered, picked, scale, reward):
    slots, width, _ = picked.shape
    blocks = fetched(counts, col_index, gathered, slots)
    total = picked[0] * blocks[0]
    for k in range(1, slots):
        total += picked[k] * blocks[k]
    weighted = piece_sums(jnp.ones((16, width), jnp.bfloat16), total)[0:1]
    return reward + scale * weighted


def first_evaluation(j, counts, col_index, gathered, before, held, picked, scale, reward, out, bounds):
    change = gathered[...] - before[...]
    top = jnp.max(change)
    bottom = jnp.min(change)
    offset = shift * (bottom + top)
    got = product(counts, col_index, gathered, picked.at[j], scale[pl.ds(j, 1), :], reward[pl.ds(j, 1), :])
    out[...] = jnp.broadcast_to(got + discount * offset, out.shape)
    sweep = lax.broadcasted_iota(jnp.int32, bounds.shape, 0)
    side = lax.broadcasted_iota(jnp.int32, bounds.shape, 1)
    bounds[...] = jnp.where(sweep < j, held[...], jnp.where(side == 0, bottom, top))


def last_evaluation(j, counts, col_index, gathered, picked, scale, reward, bounds, out, bound_rows):
    got = product(counts, col_index, gathered, picked.at[j], scale[pl.ds(j, 1), :], reward[pl.ds(j, 1), :])
    out[...] = jnp.broadcast_to(got, out.shape)
    bound_rows[...] = bounds[...]


def next_evaluation(j, counts, col_index, gathered, picked, scale, reward, out):
    got = product(counts, col_index, gathered, picked.at[j], scale[pl.ds(j, 1), :], reward[pl.ds(j, 1), :])
    out[...] = jnp.broadcast_to(got, out.shape)


SCALARS = pl.BlockSpec(memory_space=pltpu.SMEM)
VECTORS = pl.BlockSpec(memory_space=pltpu.VMEM)


def shaped(*shape):
    return jax.ShapeDtypeStruct(shape, jnp.float32)


def exchange(rows):
    return lax.all_to_all(rows, AXES, 0, 0, tiled=True)


def local(tiles, counts, col_index, reward, policy, start_values):
    actions, _, slots, width, _ = tiles.shape
    devices = lax.axis_size(AXES)
    tiles = tiles.reshape(actions, slots, width, width)
    gathered = exchange(jnp.broadcast_to(start_values[None], (devices, width)))
    params = pltpu.CompilerParams(vmem_limit_bytes=12 * MIB)
    scale, picked, picked_scale, picked_reward = pl.pallas_call(
        prepare,
        out_shape=(shaped(actions, width), shaped(SWEEPS, slots, width, width), shaped(SWEEPS, width), shaped(SWEEPS, width)),
        in_specs=[SCALARS, VECTORS, VECTORS, VECTORS],
        out_specs=(VECTORS,) * 4,
        scratch_shapes=[
            pltpu.VMEM((actions, width, width), jnp.float32),
            pltpu.VMEM((SWEEPS, width, width), jnp.float32),
        ],
        compiler_params=params,
        cost_estimate=pl.CostEstimate(flops=4_000_000, bytes_accessed=6_000_000, transcendentals=0),
        name="prepare",
    )(counts, policy, reward, tiles)

    def called(body, out_shape, scratch, name):
        return pl.pallas_call(
            body,
            out_shape=out_shape,
            in_specs=[SCALARS, SCALARS] + [VECTORS] * (len(given) - 2),
            out_specs=jax.tree.map(lambda _: VECTORS, out_shape),
            scratch_shapes=scratch,
            compiler_params=params,
            name=name,
        )(*given)

    bounds = jnp.zeros((SWEEPS, 2), jnp.float32)
    all_rows = shaped(devices, width)
    for j in range(SWEEPS):
        given = (counts, col_index, gathered, tiles, reward, scale)
        backup = called(back_up, all_rows, [pltpu.VMEM((actions, width, width), jnp.float32)], f"back_up_{j}")
        before, gathered = gathered, exchange(backup)
        given = (counts, col_index, gathered, before, bounds, picked, picked_scale, picked_reward)
        body = functools.partial(first_evaluation, j)
        current, bounds = called(body, (all_rows, shaped(SWEEPS, 2)), [], f"first_evaluation_{j}")
        gathered = exchange(current)
        given = (counts, col_index, gathered, picked, picked_scale, picked_reward)
        if j < SWEEPS - 1:
            gathered = exchange(called(functools.partial(next_evaluation, j), all_rows, [], f"next_evaluation_{j}"))
    given += (bounds,)
    body = functools.partial(last_evaluation, SWEEPS - 1)
    current, bounds = called(body, (shaped(1, width), shaped(SWEEPS, 2)), [], "last_evaluation")
    return current.reshape(width), bounds


def solution(mesh):
    split = Mesh(mesh.devices.reshape(4, 4, 8, 2), AXES)
    placed = (
        P(None, AXES, None, None, None),
        P(AXES),
        P(AXES, None),
        P(None, AXES),
        P(None, AXES),
        P(AXES),
    )
    return jax.shard_map(local, mesh=split, in_specs=placed, out_specs=(P(AXES), P()), check_vma=False)
```

time: 229 us -> 135 us (0.59)
  starting transfers between devices: 57.9 us -> 15.7 us
  waiting for transfers between devices: 47.6 us -> 7.04 us
  matrix products: 25.9 us -> 0 us
  blocking collectives: 68.8 us -> 93.9 us
  other arithmetic: 10.6 us -> 0 us
  Pallas kernels: 0 us -> 9.35 us
  local copies, waits for them, and re-layouts: 11.4 us -> 7.15 us
  between operations: 5.22 us -> 1.36 us
    all_to_all x9 -> x1, starting transfers between devices: 57.9 us -> 15.7 us  [exchange(): return lax.all_to_all(rows, AXES, 0, 0, tiled=True)]
    all_to_all x9 -> x1, waiting for transfers between devices: 47.6 us -> 7.04 us  [exchange(): return lax.all_to_all(rows, AXES, 0, 0, tiled=True)]
    dot_general x8 -> x0, matrix products: 25.7 us -> none  [the longest x2 13.6 us: local(): jnp.einsum('abr,abkrc->bkrc', onehot_blocks, tiles, precision=precise)]
    all_to_all x7 -> x5, blocking collectives: 68.8 us -> 93.9 us  [exchange(): return lax.all_to_all(rows, AXES, 0, 0, tiled=True)]
    pallas_call x0 -> x7, Pallas kernels: none -> 9.35 us  [the longest x6 7.69 us: called(): pl.pallas_call(body, out_shape=out_shape, in_specs=[SCALARS, SCALARS] + [...]
    unnamed x4 -> x14, local copies, waits for them, and re-layouts: 0.01 us -> 5.76 us
    broadcast_in_dim x16 -> x1, local copies, waits for them, and re-layouts: 6.4 us -> 1.38 us  [local(): gathered = exchange(jnp.broadcast_to(start_values[None], (devices, width)))]
    another operation x5 -> x0, other arithmetic: 3.41 us -> none  [the longest x3 1.93 us: local(): return (values, jnp.stack(bound_rows))]
  transfers between devices with their start and end apart: 9 -> 1, of which waited for: 9 -> 1; matrix products, arithmetic and copies ran while one was open for 10% -> 0% of each run, Pallas kernels for 0% -> 1%
where the time goes in v1:
time: 135 us; the launch traced here: 134 us
  blocking collectives  93.9 us (70%)
  starting transfers between devices  15.7 us (12%)
  Pallas kernels  9.35 us (7%)
  local copies, waits for them, and re-layouts  7.15 us (5%)
  waiting for transfers between devices  7.04 us (5%)
  between operations  1.36 us (1%)
    all_to_all x5, blocking collectives, exchange(): return lax.all_to_all(rows, AXES, 0, 0, tiled=True)  93.9 us
    all_to_all x1, starting transfers between devices, exchange(): return lax.all_to_all(rows, AXES, 0, 0, tiled=True)  15.7 us
    pallas_call x6, Pallas kernels, called(): pl.pallas_call(body, out_shape=out_shape, in_specs=[SCALARS, SCALARS] + [...  7.69 us
    all_to_all x1, waiting for transfers between devices, exchange(): return lax.all_to_all(rows, AXES, 0, 0, tiled=True)  7.04 us
    unnamed x14, local copies, waits for them, and re-layouts  5.76 us
  transfers between devices with their start and end apart: 1, of which 1 were waited for; matrix products, arithmetic and copies ran while one was open for 0% of the time, Pallas kernels for 1%

profile of v1, /device:TPU:1, one launch (start us, length us, event | category | flops | bytes accessed | tf_op | source)
XLA Modules:
  0.0 134.5 jit_solution(17753805733482175394)
XLA Ops:
  0.6 0.0 copy-start.4
  0.6 0.0 copy-start.5
  0.7 1.4 %broadcast_in_dim.2 = f32[256,1,128]{2,1,0:T(1,128)} broadcast(f32[128]{0:T(128)} %param.11), dimensions={2} | broadcast | bytes 131584 | tf_op jit(solution)/shard_map/broadcast_in_dim | solution.py:150
  2.0 15.7 %all-to-all-start = ((f32[256,1,128]{2,1,0:T(1,128)}), f32[256,1,128]{2,1,0:T(1,128)S(1)}, u32[]{:S(2)}, u32[]{:S(2)}) async-start(f32[256,1,128]{2,1,0:T(1,128)} %broadcast_in_dim.2), calls=%async_computation | async-start | bytes 262144 | tf_op jit(solution)/shard_map/all_to_all | solution.py:143
  18.3 0.0 copy-start
  18.4 2.2 %copy-done = f32[16,1,4,128,128]{4,3,2,1,0:T(8,128)S(1)} copy-done((f32[16,1,4,128,128]{4,3,2,1,0:T(8,128)S(1)}, f32[16,1,4,128,128]{4,3,2,1,0:T(8,128)}, u32[]{:S(2)}) %copy-start) | copy-done | bytes 4194328
  20.5 0.0 copy-start.3
  20.5 0.7 copy-done.3
  21.2 0.0 copy-start.6
  21.2 0.7 copy-done.6
  21.9 1.7 %prepare.1 = (f32[16,128]{1,0:T(8,128)S(1)}, f32[2,4,128,128]{3,2,1,0:T(8,128)S(1)}, f32[2,128]{1,0:T(2,128)S(1)}, f32[2,128]{1,0:T(2,128)S(1)}) custom-call(s32[1]{0:T(128)S(6)} %copy.13.counts, s32[2,128]{1,0:T(2,128)S(1)} %copy-done.6, f32[16,128]{1,0:T(8,128)S(1)} %copy-done.3, f32[16,4,128,128]{3,2,1,0:T(8,128)S(1)} %bitcast.23), custom_call_target="tpu_custom_call" | custom-call | flops 4000000 | bytes 6000000 | tf_op jit(solution)/shard_map/prepare/pallas_call | solution.py:152
  23.6 7.0 %all-to-all-done = f32[256,1,128]{2,1,0:T(1,128)S(1)} async-done(((f32[256,1,128]{2,1,0:T(1,128)}), f32[256,1,128]{2,1,0:T(1,128)S(1)}, u32[]{:S(2)}, u32[]{:S(2)}) %all-to-all-start) | async-done | bytes 131104 | tf_op jit(solution)/shard_map/all_to_all | solution.py:143
  30.6 0.0 copy-done.4
  30.6 0.0 copy-done.5
  30.6 0.0 copy-start.1
  30.6 2.2 %copy-done.1 = f32[16,1,4,128,128]{4,3,2,1,0:T(8,128)S(1)} copy-done((f32[16,1,4,128,128]{4,3,2,1,0:T(8,128)S(1)}, f32[16,1,4,128,128]{4,3,2,1,0:T(8,128)}, u32[]{:S(2)}) %copy-start.1) | copy-done | bytes 4194328
  32.8 0.0 copy-start.2
  32.8 2.1 %back_up_0.1 = f32[256,128]{1,0:T(8,128)S(1)} custom-call(s32[1]{0:T(128)S(6)} %copy.13.counts, s32[1,4]{1,0:T(1,128)S(1)} %copy-done.5, f32[256,128]{1,0:T(8,128)S(1)} %bitcast.26, f32[16,4,128,128]{3,2,1,0:T(8,128)S(1)} %bitcast.24, f32[16,128]{1,0:T(8,128)S(1)} %copy-done.4, f32[16,128]{1,0:T(8,128)S(1)} %get-tuple-element.12.scale), custom_call_target="tpu_custom_call" | custom-call | tf_op jit(solution)/shard_map/back_up_0/pallas_call | solution.py:167
  34.9 19.4 %all_to_all.63 = f32[256,1,128]{2,1,0:T(1,128)S(1)} all-to-all(f32[256,1,128]{2,1,0:T(1,128)S(1)} %bitcast.32), channel_id=1, replica_groups=mesh['x'=4,'y'=4,'z'=8,'c'=2] {'x','y','z','c'}, dimensions={0} | all-to-all | bytes 262144 | tf_op jit(solution)/shard_map/all_to_all | solution.py:143
  54.4 0.7 first_evaluation_0.1
  55.1 18.6 %all_to_all.64 = f32[256,1,128]{2,1,0:T(1,128)S(1)} all-to-all(f32[256,1,128]{2,1,0:T(1,128)S(1)} %bitcast.37), channel_id=1, replica_groups=mesh['x'=4,'y'=4,'z'=8,'c'=2] {'x','y','z','c'}, dimensions={0} | all-to-all | bytes 262144 | tf_op jit(solution)/shard_map/all_to_all | solution.py:143
  73.8 0.7 next_evaluation_0.1
  74.5 18.6 %all_to_all.65 = f32[256,1,128]{2,1,0:T(1,128)S(1)} all-to-all(f32[256,1,128]{2,1,0:T(1,128)S(1)} %bitcast.36), channel_id=1, replica_groups=mesh['x'=4,'y'=4,'z'=8,'c'=2] {'x','y','z','c'}, dimensions={0} | all-to-all | bytes 262144 | tf_op jit(solution)/shard_map/all_to_all | solution.py:143
  93.1 0.0 copy-done.2
  93.1 2.1 %back_up_1.1 = f32[256,128]{1,0:T(8,128)S(1)} custom-call(s32[1]{0:T(128)S(6)} %copy.13.counts, s32[1,4]{1,0:T(1,128)S(1)} %copy-done.5, f32[256,128]{1,0:T(8,128)S(1)} %bitcast.28, f32[16,4,128,128]{3,2,1,0:T(8,128)S(1)} %bitcast.25, f32[16,128]{1,0:T(8,128)S(1)} %copy-done.4, f32[16,128]{1,0:T(8,128)S(1)} %get-tuple-element.12.scale), custom_call_target="tpu_custom_call" | custom-call | tf_op jit(solution)/shard_map/back_up_1/pallas_call | solution.py:167
  95.2 18.6 %all_to_all.66 = f32[256,1,128]{2,1,0:T(1,128)S(1)} all-to-all(f32[256,1,128]{2,1,0:T(1,128)S(1)} %bitcast.31), channel_id=1, replica_groups=mesh['x'=4,'y'=4,'z'=8,'c'=2] {'x','y','z','c'}, dimensions={0} | all-to-all | bytes 262144 | tf_op jit(solution)/shard_map/all_to_all | solution.py:143
  113.9 0.7 first_evaluation_1.1
  114.6 18.6 %all_to_all.67 = f32[256,1,128]{2,1,0:T(1,128)S(1)} all-to-all(f32[256,1,128]{2,1,0:T(1,128)S(1)} %bitcast.38), channel_id=1, replica_groups=mesh['x'=4,'y'=4,'z'=8,'c'=2] {'x','y','z','c'}, dimensions={0} | all-to-all | bytes 262144 | tf_op jit(solution)/shard_map/all_to_all | solution.py:143
  133.2 1.2 last_evaluation.1
  (1 shorter events, 0.0 us)
Async XLA Ops:
  0.6 30.0 %copy-start.4 = (f32[16,128]{1,0:T(8,128)S(1)}, f32[16,128]{1,0:T(8,128)}, u32[]{:S(2)}) copy-start(f32[16,128]{1,0:T(8,128)} %reward.5) | copy-start | bytes 24580
  0.6 30.0 %copy-start.5 = (s32[1,4]{1,0:T(1,128)S(1)}, s32[1,4]{1,0:T(1,128)}, u32[]{:S(2)}) copy-start(s32[1,4]{1,0:T(1,128)} %col_index.11) | copy-start | bytes 52
  2.0 28.6 %all-to-all-start = ((f32[256,1,128]{2,1,0:T(1,128)}), f32[256,1,128]{2,1,0:T(1,128)S(1)}, u32[]{:S(2)}, u32[]{:S(2)}) async-start(f32[256,1,128]{2,1,0:T(1,128)} %broadcast_in_dim.2), calls=%async_computation | async-start | bytes 262144 | tf_op jit(solution)/shard_map/all_to_all | solution.py:143
  18.3 2.2 %copy-start = (f32[16,1,4,128,128]{4,3,2,1,0:T(8,128)S(1)}, f32[16,1,4,128,128]{4,3,2,1,0:T(8,128)}, u32[]{:S(2)}) copy-start(f32[16,1,4,128,128]{4,3,2,1,0:T(8,128)} %param.6) | copy-start | bytes 12582916
  20.5 0.7 copy-start.3
  21.2 0.7 copy-start.6
  30.6 2.2 %copy-start.1 = (f32[16,1,4,128,128]{4,3,2,1,0:T(8,128)S(1)}, f32[16,1,4,128,128]{4,3,2,1,0:T(8,128)}, u32[]{:S(2)}) copy-start(f32[16,1,4,128,128]{4,3,2,1,0:T(8,128)} %param.6) | copy-start | bytes 12582916
  32.8 60.3 %copy-start.2 = (f32[16,1,4,128,128]{4,3,2,1,0:T(8,128)S(1)}, f32[16,1,4,128,128]{4,3,2,1,0:T(8,128)}, u32[]{:S(2)}) copy-start(f32[16,1,4,128,128]{4,3,2,1,0:T(8,128)} %param.6) | copy-start | bytes 12582916

commit v2 on v1

v2 whole, which is shorter than its diff:
```python
import functools

import jax
import jax.numpy as jnp
from jax import lax
from jax.experimental import pallas as pl
from jax.experimental.pallas import tpu as pltpu
from jax.sharding import Mesh
from jax.sharding import PartitionSpec as P

SWEEPS = 2
EVALS = 2
AXES = ("x", "y", "z", "c")
discount = 0.9
shift = discount / (1.0 - discount) * 0.5
MIB = 1 << 20


def piece_sums(rows, values):
    high = values.astype(jnp.bfloat16)
    rest = values - high.astype(jnp.float32)
    middle = rest.astype(jnp.bfloat16)
    low = (rest - middle.astype(jnp.float32)).astype(jnp.bfloat16)
    dims = (((1,), (1,)), ((), ()))
    out = lax.dot_general(rows, high, dims, preferred_element_type=jnp.float32)
    out += lax.dot_general(rows, middle, dims, preferred_element_type=jnp.float32)
    return out + lax.dot_general(rows, low, dims, preferred_element_type=jnp.float32)


def row_of(index):
    at = lax.broadcasted_iota(jnp.int32, (16, 128), 0)
    return jnp.where(at == index, 1.0, 0.0).astype(jnp.bfloat16)


def spread(counts, col_index, start, out, table):
    for k in range(table.shape[1]):
        table[0, k] = jnp.where(counts[0] > k, col_index[0, k], -1)
    out[...] = jnp.broadcast_to(start[...], out.shape)


def fetched(table, gathered):
    out = []
    for k in range(table.shape[1]):
        at = table[0, k]
        row = gathered[pl.ds(jnp.maximum(at, 0), 1), :]
        out.append(jnp.where(at >= 0, row, 0.0))
    return out


def first_back_up(
    table, gathered, tiles, reward, policy, out, scale, picked, picked_scale, picked_reward, sums, weights, columns
):
    actions, slots, width, _ = tiles.shape
    for j in range(SWEEPS):
        columns[j] = jnp.broadcast_to(policy[pl.ds(j, 1), :].astype(jnp.float32), (width, width)).T
    live = [table[0, k] >= 0 for k in range(slots)]
    blocks = [jnp.broadcast_to(b, (8, width)) for b in fetched(table, gathered)]

    def group(g, _):
        rows = pl.ds(pl.multiple_of(g * 8, 8), 8)
        chosen = [columns[j, rows, :] for j in range(SWEEPS)]
        held = [[jnp.zeros((8, width), jnp.float32) for _ in range(slots)] for _ in range(SWEEPS)]
        for a in range(actions):
            total = jnp.zeros((8, width), jnp.float32)
            weighted = jnp.zeros((8, width), jnp.float32)
            for k in range(slots):
                tile = jnp.where(live[k], tiles[a, k, rows, :], 0.0)
                total += tile
                weighted += tile * blocks[k]
                for j in range(SWEEPS):
                    held[j][k] = jnp.where(chosen[j] == float(a), tile, held[j][k])
            sums[a, rows, :] = total
            weights[a, rows, :] = weighted
        for j in range(SWEEPS):
            for k in range(slots):
                picked[j, k, rows, :] = held[j][k]
        return 0

    lax.fori_loop(0, width // 8, group, 0)
    totals = jnp.zeros((actions, width), jnp.float32)
    weighted = jnp.zeros((actions, width), jnp.float32)
    for a in range(actions):
        totals += piece_sums(row_of(a), sums[a])
        weighted += piece_sums(row_of(a), weights[a])
    inverse = discount / totals
    scale[...] = inverse
    backup = jnp.max(reward[...] + inverse * weighted, axis=0, keepdims=True)
    out[...] = jnp.broadcast_to(backup, out.shape)
    at = lax.broadcasted_iota(jnp.int32, (actions, width), 0)
    for j in range(SWEEPS):
        here = at == policy[pl.ds(j, 1), :]
        picked_scale[pl.ds(j, 1), :] = jnp.sum(jnp.where(here, inverse, 0.0), axis=0, keepdims=True)
        picked_reward[pl.ds(j, 1), :] = jnp.sum(jnp.where(here, reward[...], 0.0), axis=0, keepdims=True)


def back_up(table, gathered, tiles, reward, scale, out, sums):
    actions, slots, width, _ = tiles.shape
    blocks = [jnp.broadcast_to(b, (8, width)) for b in fetched(table, gathered)]

    def group(g, _):
        rows = pl.ds(pl.multiple_of(g * 8, 8), 8)
        for a in range(actions):
            total = tiles[a, 0, rows, :] * blocks[0]
            for k in range(1, slots):
                total += tiles[a, k, rows, :] * blocks[k]
            sums[a, rows, :] = total
        return 0

    lax.fori_loop(0, width // 8, group, 0)
    weighted = jnp.zeros((actions, width), jnp.float32)
    for a in range(actions):
        weighted += piece_sums(row_of(a), sums[a])
    backup = jnp.max(reward[...] + scale[...] * weighted, axis=0, keepdims=True)
    out[...] = jnp.broadcast_to(backup, out.shape)


def product(table, gathered, picked, scale, reward):
    slots, width, _ = picked.shape
    blocks = fetched(table, gathered)
    total = picked[0] * blocks[0]
    for k in range(1, slots):
        total += picked[k] * blocks[k]
    weighted = piece_sums(jnp.ones((16, width), jnp.bfloat16), total)[0:1]
    return reward + scale * weighted


def first_evaluation(j, table, gathered, before, held, picked, scale, reward, out, bounds):
    change = gathered[...] - before[...]
    top = jnp.max(change)
    bottom = jnp.min(change)
    offset = shift * (bottom + top)
    got = product(table, gathered, picked.at[j], scale[pl.ds(j, 1), :], reward[pl.ds(j, 1), :])
    out[...] = jnp.broadcast_to(got + discount * offset, out.shape)
    sweep = lax.broadcasted_iota(jnp.int32, bounds.shape, 0)
    side = lax.broadcasted_iota(jnp.int32, bounds.shape, 1)
    bounds[...] = jnp.where(sweep < j, held[...], jnp.where(side == 0, bottom, top))


def last_evaluation(j, table, gathered, picked, scale, reward, bounds, out, bound_rows):
    got = product(table, gathered, picked.at[j], scale[pl.ds(j, 1), :], reward[pl.ds(j, 1), :])
    out[...] = jnp.broadcast_to(got, out.shape)
    bound_rows[...] = bounds[...]


def next_evaluation(j, table, gathered, picked, scale, reward, out):
    got = product(table, gathered, picked.at[j], scale[pl.ds(j, 1), :], reward[pl.ds(j, 1), :])
    out[...] = jnp.broadcast_to(got, out.shape)


SCALARS = pl.BlockSpec(memory_space=pltpu.SMEM)
VECTORS = pl.BlockSpec(memory_space=pltpu.VMEM)


def shaped(*shape):
    return jax.ShapeDtypeStruct(shape, jnp.float32)


def exchange(rows):
    return lax.all_to_all(rows, AXES, 0, 0, tiled=True)


def local(tiles, counts, col_index, reward, policy, start_values):
    actions, _, slots, width, _ = tiles.shape
    devices = lax.axis_size(AXES)
    tiles = tiles.reshape(actions, slots, width, width)
    rows, table = pl.pallas_call(
        spread,
        out_shape=(shaped(devices, width), jax.ShapeDtypeStruct(col_index.shape, jnp.int32)),
        in_specs=[SCALARS, SCALARS, VECTORS],
        out_specs=(VECTORS, SCALARS),
        compiler_params=pltpu.CompilerParams(vmem_limit_bytes=2 * MIB),
        name="spread",
    )(counts, col_index, start_values.reshape(1, width))
    gathered = exchange(rows)
    params = pltpu.CompilerParams(vmem_limit_bytes=12 * MIB)
    def called(body, out_shape, scratch, name):
        return pl.pallas_call(
            body,
            out_shape=out_shape,
            in_specs=[SCALARS] + [VECTORS] * (len(given) - 1),
            out_specs=jax.tree.map(lambda _: VECTORS, out_shape),
            scratch_shapes=scratch,
            compiler_params=params,
            name=name,
        )(*given)

    bounds = jnp.zeros((SWEEPS, 2), jnp.float32)
    all_rows = shaped(devices, width)
    square = pltpu.VMEM((actions, width, width), jnp.float32)
    for j in range(SWEEPS):
        if j == 0:
            given = (table, gathered, tiles, reward, policy)
            made = (
                all_rows,
                shaped(actions, width),
                shaped(SWEEPS, slots, width, width),
                shaped(SWEEPS, width),
                shaped(SWEEPS, width),
            )
            scratch = [square, square, pltpu.VMEM((SWEEPS, width, width), jnp.float32)]
            backup, scale, picked, picked_scale, picked_reward = called(first_back_up, made, scratch, "first_back_up")
        else:
            given = (table, gathered, tiles, reward, scale)
            backup = called(back_up, all_rows, [square], f"back_up_{j}")
        before, gathered = gathered, exchange(backup)
        given = (table, gathered, before, bounds, picked, picked_scale, picked_reward)
        body = functools.partial(first_evaluation, j)
        current, bounds = called(body, (all_rows, shaped(SWEEPS, 2)), [], f"first_evaluation_{j}")
        gathered = exchange(current)
        given = (table, gathered, picked, picked_scale, picked_reward)
        if j < SWEEPS - 1:
            gathered = exchange(called(functools.partial(next_evaluation, j), all_rows, [], f"next_evaluation_{j}"))
    given += (bounds,)
    body = functools.partial(last_evaluation, SWEEPS - 1)
    current, bounds = called(body, (shaped(1, width), shaped(SWEEPS, 2)), [], "last_evaluation")
    return current.reshape(width), bounds


def solution(mesh):
    split = Mesh(mesh.devices.reshape(4, 4, 8, 2), AXES)
    placed = (
        P(None, AXES, None, None, None),
        P(AXES),
        P(AXES, None),
        P(None, AXES),
        P(None, AXES),
        P(AXES),
    )
    return jax.shard_map(local, mesh=split, in_specs=placed, out_specs=(P(AXES), P()), check_vma=False)
```

time: 135 us -> 138 us (1.022)
  blocking collectives: 93.9 us -> 121 us
  starting transfers between devices: 15.7 us -> 0 us
  waiting for transfers between devices: 7.04 us -> 0 us
  local copies, waits for them, and re-layouts: 7.15 us -> 4.88 us
    all_to_all x5 -> x6, blocking collectives: 93.9 us -> 121 us  [exchange(): return lax.all_to_all(rows, AXES, 0, 0, tiled=True)]
    all_to_all x1 -> x0, starting transfers between devices: 15.7 us -> none  [exchange(): return lax.all_to_all(rows, AXES, 0, 0, tiled=True)]
    all_to_all x1 -> x0, waiting for transfers between devices: 7.04 us -> none  [exchange(): return lax.all_to_all(rows, AXES, 0, 0, tiled=True)]
    broadcast_in_dim x1 -> x0, local copies, waits for them, and re-layouts: 1.38 us -> none  [local(): gathered = exchange(jnp.broadcast_to(start_values[None], (devices, width)))]
  transfers between devices with their start and end apart: 1 -> 0, of which waited for: 1 -> 0; matrix products, arithmetic and copies ran while one was open for 0% -> 0% of each run, Pallas kernels for 1% -> 0%
where the time goes in v2:
time: 138 us
  blocking collectives  121 us (88%)
  Pallas kernels  9.93 us (7%)
  local copies, waits for them, and re-layouts  4.88 us (4%)
    all_to_all x6, blocking collectives, exchange(): return lax.all_to_all(rows, AXES, 0, 0, tiled=True)  121 us
    pallas_call x6, Pallas kernels, called(): pl.pallas_call(body, out_shape=out_shape, in_specs=[SCALARS] + [VECTORS]...  8.79 us
    unnamed x14, local copies, waits for them, and re-layouts  4.88 us

profile of v2, /device:TPU:1, one launch (start us, length us, event | category | flops | bytes accessed | tf_op | source)
XLA Modules:
  0.0 137.7 jit_solution(16046408405003886633)
XLA Ops:
  0.6 0.0 copy-start.3
  1.3 0.0 copy-start.5
  1.3 0.6 copy-done.5
  2.0 0.0 copy-start.6
  2.0 0.7 copy-done.6
  2.6 1.1 spread.1
  3.8 28.4 %all_to_all.66 = f32[256,1,128]{2,1,0:T(1,128)S(1)} all-to-all(f32[256,1,128]{2,1,0:T(1,128)S(1)} %bitcast.42), channel_id=1, replica_groups=mesh['x'=4,'y'=4,'z'=8,'c'=2] {'x','y','z','c'}, dimensions={0} | all-to-all | bytes 262144 | tf_op jit(solution)/shard_map/all_to_all | solution.py:159
  32.2 0.0 copy-start
  32.2 2.2 %copy-done = f32[16,1,4,128,128]{4,3,2,1,0:T(8,128)S(1)} copy-done((f32[16,1,4,128,128]{4,3,2,1,0:T(8,128)S(1)}, f32[16,1,4,128,128]{4,3,2,1,0:T(8,128)}, u32[]{:S(2)}) %copy-start) | copy-done | bytes 4194328
  34.4 0.0 copy-start.2
  34.4 0.7 copy-done.2
  35.0 0.0 copy-start.4
  35.1 0.7 copy-done.4
  35.7 0.0 copy-start.1
  35.7 3.2 %first_back_up.1 = (f32[256,128]{1,0:T(8,128)S(1)}, f32[16,128]{1,0:T(8,128)S(1)}, f32[2,4,128,128]{3,2,1,0:T(8,128)S(1)}, f32[2,128]{1,0:T(2,128)S(1)}, f32[2,128]{1,0:T(2,128)S(1)}) custom-call(s32[1,4]{1,0:T(1,128)S(1)} %get-tuple-element.15.table, f32[256,128]{1,0:T(8,128)S(1)} %bitcast.29, f32[16,4,128,128]{3,2,1,0:T(8,128)S(1)} %bitcast.27, ...), custom_call_target="tpu_custom_call" | custom-call | tf_op jit(solution)/shard_map/first_back_up/pallas_call | solution.py:177
  38.9 18.6 %all_to_all.67 = f32[256,1,128]{2,1,0:T(1,128)S(1)} all-to-all(f32[256,1,128]{2,1,0:T(1,128)S(1)} %bitcast.39), channel_id=1, replica_groups=mesh['x'=4,'y'=4,'z'=8,'c'=2] {'x','y','z','c'}, dimensions={0} | all-to-all | bytes 262144 | tf_op jit(solution)/shard_map/all_to_all | solution.py:159
  57.5 0.7 first_evaluation_0.1
  58.3 18.6 %all_to_all.68 = f32[256,1,128]{2,1,0:T(1,128)S(1)} all-to-all(f32[256,1,128]{2,1,0:T(1,128)S(1)} %bitcast.40), channel_id=1, replica_groups=mesh['x'=4,'y'=4,'z'=8,'c'=2] {'x','y','z','c'}, dimensions={0} | all-to-all | bytes 262144 | tf_op jit(solution)/shard_map/all_to_all | solution.py:159
  76.9 0.7 next_evaluation_0.1
  77.6 18.6 %all_to_all.69 = f32[256,1,128]{2,1,0:T(1,128)S(1)} all-to-all(f32[256,1,128]{2,1,0:T(1,128)S(1)} %bitcast.38), channel_id=1, replica_groups=mesh['x'=4,'y'=4,'z'=8,'c'=2] {'x','y','z','c'}, dimensions={0} | all-to-all | bytes 262144 | tf_op jit(solution)/shard_map/all_to_all | solution.py:159
  96.3 0.0 copy-done.3
  96.3 0.0 copy-done.1
  96.3 2.1 %back_up_1.1 = f32[256,128]{1,0:T(8,128)S(1)} custom-call(s32[1,4]{1,0:T(1,128)S(1)} %get-tuple-element.15.table, f32[256,128]{1,0:T(8,128)S(1)} %bitcast.31, f32[16,4,128,128]{3,2,1,0:T(8,128)S(1)} %bitcast.28, f32[16,128]{1,0:T(8,128)S(1)} %copy-done.3, f32[16,128]{1,0:T(8,128)S(1)} %get-tuple-element.22.scale), custom_call_target="tpu_custom_call" | custom-call | tf_op jit(solution)/shard_map/back_up_1/pallas_call | solution.py:177
  98.4 18.6 %all_to_all.70 = f32[256,1,128]{2,1,0:T(1,128)S(1)} all-to-all(f32[256,1,128]{2,1,0:T(1,128)S(1)} %bitcast.33), channel_id=1, replica_groups=mesh['x'=4,'y'=4,'z'=8,'c'=2] {'x','y','z','c'}, dimensions={0} | all-to-all | bytes 262144 | tf_op jit(solution)/shard_map/all_to_all | solution.py:159
  117.0 0.7 first_evaluation_1.1
  117.8 18.6 %all_to_all.71 = f32[256,1,128]{2,1,0:T(1,128)S(1)} all-to-all(f32[256,1,128]{2,1,0:T(1,128)S(1)} %bitcast.41), channel_id=1, replica_groups=mesh['x'=4,'y'=4,'z'=8,'c'=2] {'x','y','z','c'}, dimensions={0} | all-to-all | bytes 262144 | tf_op jit(solution)/shard_map/all_to_all | solution.py:159
  136.4 1.3 last_evaluation.1
  (1 shorter events, 0.0 us)
Async XLA Ops:
  0.6 95.6 %copy-start.3 = (f32[16,128]{1,0:T(8,128)S(1)}, f32[16,128]{1,0:T(8,128)}, u32[]{:S(2)}) copy-start(f32[16,128]{1,0:T(8,128)} %reward.3) | copy-start | bytes 24580
  1.3 0.7 copy-start.5
  2.0 0.7 copy-start.6
  32.2 2.2 %copy-start = (f32[16,1,4,128,128]{4,3,2,1,0:T(8,128)S(1)}, f32[16,1,4,128,128]{4,3,2,1,0:T(8,128)}, u32[]{:S(2)}) copy-start(f32[16,1,4,128,128]{4,3,2,1,0:T(8,128)} %param.6) | copy-start | bytes 12582916
  34.4 0.7 copy-start.2
  35.0 0.7 copy-start.4
  35.7 60.5 %copy-start.1 = (f32[16,1,4,128,128]{4,3,2,1,0:T(8,128)S(1)}, f32[16,1,4,128,128]{4,3,2,1,0:T(8,128)}, u32[]{:S(2)}) copy-start(f32[16,1,4,128,128]{4,3,2,1,0:T(8,128)} %param.6) | copy-start | bytes 12582916

commit v3 on v1

v3 whole, which is shorter than its diff:
```python
import functools

import jax
import jax.numpy as jnp
from jax import lax
from jax.experimental import pallas as pl
from jax.experimental.pallas import tpu as pltpu
from jax.sharding import Mesh
from jax.sharding import PartitionSpec as P

SWEEPS = 2
AXES = ("x", "y", "z", "c")
ORDER = ("x", "y", "c", "z")
PLANE = ("x", "y", "c")
LINE = "z"
discount = 0.9
shift = discount / (1.0 - discount) * 0.5
MIB = 1 << 20
AUX = 8


def pieces(values):
    high = values.astype(jnp.bfloat16)
    rest = values - high.astype(jnp.float32)
    middle = rest.astype(jnp.bfloat16)
    low = (rest - middle.astype(jnp.float32)).astype(jnp.bfloat16)
    return high, middle, low


def contract(left, right, dims):
    out = None
    for piece in pieces(right):
        term = lax.dot_general(left, piece, (dims, ((), ())), preferred_element_type=jnp.float32)
        out = term if out is None else out + term
    return out


def lane_sums(count, row_values):
    at = lax.broadcasted_iota(jnp.int32, (16, 128), 0)
    out = jnp.zeros((16, 128), jnp.float32)
    for i in range(count):
        row = jnp.where(at == i, 1.0, 0.0).astype(jnp.bfloat16)
        out += contract(row, row_values(i), ((1,), (1,)))
    return out


def stacked(rows, height):
    at = lax.broadcasted_iota(jnp.int32, (height, rows[0].shape[-1]), 0)
    out = jnp.zeros(at.shape, jnp.float32)
    for i, row in enumerate(rows):
        out = jnp.where(at == i, row, out)
    return out


def prepare(counts, col_index, start, policy, reward, tiles, rows_out, table, scale, load_0, load_1, held_tiles, sums, columns, sems):
    actions, slots, width, _ = tiles.shape
    loads = (load_0, load_1)

    def copy(g):
        rows = pl.ds(pl.multiple_of(g * 8, 8), 8)
        return pltpu.make_async_copy(tiles.at[:, :, rows, :], held_tiles.at[:, :, rows, :], sems.at[g])

    for g in range(width // 8):
        copy(g).start()
    columns_of = []
    for k in range(slots):
        block = col_index[0, k]
        place = (block // 16) * 16 + (block % 2) * 8 + (block % 16) // 2
        place = jnp.where(counts[0] > k, place, -1)
        table[0, k] = place
        columns_of.append(jnp.full((1, width), place.astype(jnp.float32)))
    live = [counts[0] > k for k in range(slots)]
    rows_out[...] = jnp.broadcast_to(start[...], rows_out.shape)
    for j in range(SWEEPS):
        columns[j] = jnp.broadcast_to(policy[pl.ds(j, 1), :].astype(jnp.float32), (width, width)).T

    def group(g, _):
        rows = pl.ds(pl.multiple_of(g * 8, 8), 8)
        copy(g).wait()
        chosen = [columns[j, rows, :] for j in range(SWEEPS)]
        held = [[jnp.zeros((8, width), jnp.float32) for _ in range(slots)] for _ in range(SWEEPS)]
        for a in range(actions):
            total = jnp.zeros((8, width), jnp.float32)
            for k in range(slots):
                tile = jnp.where(live[k], held_tiles[a, k, rows, :], 0.0)
                total += tile
                for j in range(SWEEPS):
                    held[j][k] = jnp.where(chosen[j] == float(a), tile, held[j][k])
            sums[a, rows, :] = total
        for j in range(SWEEPS):
            for k in range(slots):
                loads[j][pl.ds(pl.multiple_of(k * width + g * 8, 8), 8), :] = held[j][k]
        return 0

    lax.fori_loop(0, width // 8, group, 0)
    inverse = discount / lane_sums(actions, lambda a: sums[a])
    scale[...] = inverse
    at = lax.broadcasted_iota(jnp.int32, (actions, width), 0)
    for j in range(SWEEPS):
        here = at == policy[pl.ds(j, 1), :]
        picked_scale = jnp.sum(jnp.where(here, inverse, 0.0), axis=0, keepdims=True)
        picked_reward = jnp.sum(jnp.where(here, reward[...], 0.0), axis=0, keepdims=True)
        loads[j][pl.ds(slots * width, AUX), :] = stacked([picked_scale, picked_reward] + columns_of, AUX)


def fetched(table, gathered):
    out = []
    for k in range(table.shape[1]):
        at = table[0, k]
        row = gathered[pl.ds(jnp.maximum(at, 0), 1), :]
        out.append(jnp.where(at >= 0, row, 0.0))
    return out


def back_up(table, gathered, tiles, reward, scale, out, sums):
    actions, slots, width, _ = tiles.shape
    blocks = [jnp.broadcast_to(b, (8, width)) for b in fetched(table, gathered)]

    def group(g, _):
        rows = pl.ds(pl.multiple_of(g * 8, 8), 8)
        for a in range(actions):
            total = tiles[a, 0, rows, :] * blocks[0]
            for k in range(1, slots):
                total += tiles[a, k, rows, :] * blocks[k]
            sums[a, rows, :] = total
        return 0

    lax.fori_loop(0, width // 8, group, 0)
    weighted = lane_sums(actions, lambda a: sums[a])
    backup = jnp.max(reward[...] + scale[...] * weighted, axis=0, keepdims=True)
    out[...] = jnp.broadcast_to(backup, out.shape)


def line_product(gathered, loads):
    states, width = gathered.shape
    high = width * 4 + AUX
    blocks = loads.shape[0] // high
    aux = [loads[pl.ds(b * high + 4 * width, AUX), :] for b in range(blocks)]
    named = jnp.concatenate(aux, axis=0)
    lane = lax.broadcasted_iota(jnp.int32, named.shape, 1).astype(jnp.float32)
    fetched_rows = None
    for h in range(states // width):
        chosen = jnp.where(named == lane + float(h * width), 1.0, 0.0).astype(jnp.bfloat16)
        term = contract(chosen, gathered[pl.ds(h * width, width), :], ((1,), (0,)))
        fetched_rows = term if fetched_rows is None else fetched_rows + term

    def weighted_rows(b):
        total = None
        for k in range(4):
            at = b * AUX + 2 + k
            term = loads[pl.ds(b * high + k * width, width), :] * fetched_rows[at : at + 1]
            total = term if total is None else total + term
        return total

    weighted = lane_sums(blocks, weighted_rows)[:blocks]
    scale = stacked([a[0:1] for a in aux], blocks)
    reward = stacked([a[1:2] for a in aux], blocks)
    return reward + scale * weighted


def spread_out(out, got):
    for i in range(out.shape[0] // got.shape[0]):
        out[pl.ds(i * got.shape[0], got.shape[0]), :] = got


def first_evaluation(j, gathered, before, held, loads, out, bounds):
    change = gathered[...] - before[...]
    top = jnp.max(change)
    bottom = jnp.min(change)
    offset = shift * (bottom + top)
    spread_out(out, line_product(gathered, loads) + discount * offset)
    sweep = lax.broadcasted_iota(jnp.int32, bounds.shape, 0)
    side = lax.broadcasted_iota(jnp.int32, bounds.shape, 1)
    bounds[...] = jnp.where(sweep < j, held[...], jnp.where(side == 0, bottom, top))


def next_evaluation(gathered, loads, out):
    spread_out(out, line_product(gathered, loads))


def last_evaluation(table, gathered, load, held, out, bounds):
    slots, width = table.shape[1], gathered.shape[1]
    blocks = fetched(table, gathered)
    total = load[pl.ds(0, width), :] * blocks[0]
    for k in range(1, slots):
        total += load[pl.ds(k * width, width), :] * blocks[k]
    weighted = lane_sums(1, lambda _: total)[0:1]
    aux = load[pl.ds(slots * width, AUX), :]
    out[...] = aux[1:2] + aux[0:1] * weighted
    bounds[...] = held[...]


SCALARS = pl.BlockSpec(memory_space=pltpu.SMEM)
VECTORS = pl.BlockSpec(memory_space=pltpu.VMEM)
LEFT = pl.BlockSpec(memory_space=pltpu.HBM)


def shaped(*shape):
    return jax.ShapeDtypeStruct(shape, jnp.float32)


def called(body, given, out_shape, name, scratch=(), scalars=0, limit=8):
    return pl.pallas_call(
        body,
        out_shape=out_shape,
        in_specs=[SCALARS] * scalars + [VECTORS] * (len(given) - scalars),
        out_specs=jax.tree.map(lambda _: VECTORS, out_shape),
        scratch_shapes=list(scratch),
        compiler_params=pltpu.CompilerParams(vmem_limit_bytes=limit * MIB),
        name=name,
    )(*given)


def over_all(rows):
    return lax.all_to_all(rows, ORDER, 0, 0, tiled=True)


def over_plane(rows):
    return lax.all_to_all(rows, PLANE, 0, 0, tiled=True)


def over_line(load):
    return lax.all_gather(load, LINE, axis=0, tiled=True)


def local(tiles, counts, col_index, reward, policy, start_values):
    actions, _, slots, width, _ = tiles.shape
    devices = lax.axis_size(AXES)
    tiles = tiles.reshape(actions, slots, width, width)
    all_rows = shaped(devices, width)
    load = shaped(slots * width + AUX, width)
    square = pltpu.VMEM((actions, width, width), jnp.float32)
    rows, table, scale, load_0, load_1, held_tiles = pl.pallas_call(
        prepare,
        out_shape=(
            all_rows,
            jax.ShapeDtypeStruct(col_index.shape, jnp.int32),
            shaped(actions, width),
            load,
            load,
            shaped(*tiles.shape),
        ),
        in_specs=[SCALARS, SCALARS, VECTORS, VECTORS, VECTORS, LEFT],
        out_specs=(VECTORS, SCALARS, VECTORS, VECTORS, VECTORS, VECTORS),
        scratch_shapes=[square, pltpu.VMEM((SWEEPS, width, width), jnp.float32), pltpu.SemaphoreType.DMA((width // 8,))],
        compiler_params=pltpu.CompilerParams(vmem_limit_bytes=12 * MIB),
        name="prepare",
    )(counts, col_index, start_values.reshape(1, width), policy, reward, tiles)

    loads = over_line(load_0)
    gathered = over_all(rows)
    bounds = jnp.zeros((SWEEPS, 2), jnp.float32)
    for j in range(SWEEPS):
        backup = called(back_up, (table, gathered, held_tiles, reward, scale), all_rows, f"back_up_{j}", [square], 1)
        before, gathered = gathered, over_all(backup)
        if j == 0:
            load_1, gathered = lax.optimization_barrier((load_1, gathered))
            later_loads = over_line(load_1)
        body = functools.partial(first_evaluation, j)
        given = (gathered, before, bounds, loads)
        current, bounds = called(body, given, (all_rows, shaped(SWEEPS, 2)), f"first_evaluation_{j}")
        gathered = over_plane(current)
        if j < SWEEPS - 1:
            current = called(next_evaluation, (gathered, loads), all_rows, f"next_evaluation_{j}")
            gathered = over_plane(current)
            loads = later_loads
    given = (table, gathered, load_1, bounds)
    current, bounds = called(last_evaluation, given, (shaped(1, width), shaped(SWEEPS, 2)), "last_evaluation", (), 1)
    return current.reshape(width), bounds


def solution(mesh):
    split = Mesh(mesh.devices.reshape(4, 4, 8, 2), AXES)
    placed = (
        P(None, AXES, None, None, None),
        P(AXES),
        P(AXES, None),
        P(None, AXES),
        P(None, AXES),
        P(AXES),
    )
    return jax.shard_map(local, mesh=split, in_specs=placed, out_specs=(P(AXES), P()), check_vma=False)
```

time: 135 us -> 144 us (1.067)
  starting transfers between devices: 15.7 us -> 0.08 us
  between operations: 1.36 us -> 14.8 us
  blocking collectives: 93.9 us -> 103 us
  waiting for transfers between devices: 7.04 us -> 0.06 us
  local copies, waits for them, and re-layouts: 7.15 us -> 14 us
  Pallas kernels: 9.35 us -> 12.2 us
    all_to_all x1 -> x0, starting transfers between devices: 15.7 us -> none  [exchange(): return lax.all_to_all(rows, AXES, 0, 0, tiled=True)]
    all_to_all x5 -> x6, blocking collectives: 93.9 us -> 103 us  [the longest x3 68.6 us: over_all(): return lax.all_to_all(rows, ORDER, 0, 0, tiled=True)]
    unnamed x14 -> x24, local copies, waits for them, and re-layouts: 5.76 us -> 14 us
    all_to_all x1 -> x0, waiting for transfers between devices: 7.04 us -> none  [exchange(): return lax.all_to_all(rows, AXES, 0, 0, tiled=True)]
    pallas_call x7, Pallas kernels: 9.35 us -> 12.2 us  [the longest x6 8.43 us: called(): pl.pallas_call(body, out_shape=out_shape, in_specs=[SCALARS] * scalars +...]
  transfers between devices with their start and end apart: 1 -> 2, of which waited for: 1 -> 0; matrix products, arithmetic and copies ran while one was open for 0% -> 0% of each run, Pallas kernels for 1% -> 4%
where the time goes in v3:
time: 144 us
  blocking collectives  103 us (72%)
  between operations  14.8 us (10%)
  local copies, waits for them, and re-layouts  14 us (10%)
  Pallas kernels  12.2 us (8%)
    all_to_all x3, blocking collectives, over_all(): return lax.all_to_all(rows, ORDER, 0, 0, tiled=True)  68.6 us
    all_to_all x3, blocking collectives, over_plane(): return lax.all_to_all(rows, PLANE, 0, 0, tiled=True)  34.1 us
    unnamed x24, local copies, waits for them, and re-layouts  14 us
    pallas_call x6, Pallas kernels, called(): pl.pallas_call(body, out_shape=out_shape, in_specs=[SCALARS] * scalars +...  8.43 us
    pallas_call x1, Pallas kernels, local(): pl.pallas_call(prepare, out_shape=(all_rows, jax.ShapeDtypeStruct(col_ind...  3.8 us
  transfers between devices with their start and end apart: 2, of which 0 were waited for; matrix products, arithmetic and copies ran while one was open for 0% of the time, Pallas kernels for 4%

profile of v3, /device:TPU:1, one launch (start us, length us, event | category | flops | bytes accessed | tf_op | source)
XLA Modules:
  0.0 143.8 jit_solution(12519184823777869039)
XLA Ops:
  7.2 0.0 all-gather.3.cloned.1.call-start
  7.9 0.0 copy-start.5
  7.9 2.2 %copy-done.5 = f32[16,1,4,128,128]{4,3,2,1,0:T(8,128)S(1)} copy-done((f32[16,1,4,128,128]{4,3,2,1,0:T(8,128)S(1)}, f32[16,1,4,128,128]{4,3,2,1,0:T(8,128)}, u32[]{:S(2)}) %copy-start.5) | copy-done | bytes 4194328
  10.0 0.7 copy-done.7
  10.7 0.7 copy-done.9
  11.4 0.7 copy-done.10
  12.1 0.7 copy-done.11
  12.7 3.8 %prepare.1 = (f32[256,128]{1,0:T(8,128)S(1)}, s32[1,4]{1,0:T(1,128)S(1)}, f32[16,128]{1,0:T(8,128)S(1)}, f32[520,128]{1,0:T(8,128)}, f32[520,128]{1,0:T(8,128)}, /*index=5*/f32[16,4,128,128]{3,2,1,0:T(8,128)S(1)}) custom-call(s32[1]{0:T(128)S(6)} %copy.11.counts, s32[1,4]{1,0:T(1,128)S(1)} %copy-done.10, f32[1,128]{1,0:T(1,128)S(1)} %bitcast.36, ...), custom_call_target="tpu_custom_call" | custom-call | tf_op jit(solution)/shard_map/prepare/pallas_call | solution.py:233
  16.5 0.0 copy-start
  16.6 1.9 %copy-done = f32[16,4,128,128]{3,2,1,0:T(8,128)} copy-done((f32[16,4,128,128]{3,2,1,0:T(8,128)}, f32[16,4,128,128]{3,2,1,0:T(8,128)S(1)}, u32[]{:S(2)}) %copy-start) | copy-done | bytes 4194328
  18.5 0.0 all-gather.3.cloned.1.call-update
  18.5 0.0 all-gather.5.cloned.1.call-start
  18.6 29.6 %all_to_all.67 = f32[256,1,128]{2,1,0:T(1,128)S(1)} all-to-all(f32[256,1,128]{2,1,0:T(1,128)S(1)} %bitcast.33), channel_id=1, replica_groups=mesh['x'=4,'y'=4,'z'=8,'c'=2] {'x','y','c','z'}, dimensions={0} | all-to-all | bytes 262144 | tf_op jit(solution)/shard_map/all_to_all | solution.py:215
  48.1 0.0 copy-done.8
  48.1 2.2 %copy-done.1 = f32[16,4,128,128]{3,2,1,0:T(8,128)S(1)} copy-done((f32[16,4,128,128]{3,2,1,0:T(8,128)S(1)}, f32[16,4,128,128]{3,2,1,0:T(8,128)}, u32[]{:S(2)}) %copy-start.1) | copy-done | bytes 4194328
  50.4 2.1 %back_up_0.1 = f32[256,128]{1,0:T(8,128)S(1)} custom-call(s32[1,4]{1,0:T(1,128)S(1)} %get-tuple-element.16.table, f32[256,128]{1,0:T(8,128)S(1)} %bitcast.22, f32[16,4,128,128]{3,2,1,0:T(8,128)S(1)} %copy-done.1, f32[16,128]{1,0:T(8,128)S(1)} %copy-done.8, f32[16,128]{1,0:T(8,128)S(1)} %get-tuple-element.20.scale), custom_call_target="tpu_custom_call" | custom-call | tf_op jit(solution)/shard_map/back_up_0/pallas_call | solution.py:203
  52.5 19.1 %all_to_all.68 = f32[256,1,128]{2,1,0:T(1,128)S(1)} all-to-all(f32[256,1,128]{2,1,0:T(1,128)S(1)} %bitcast.31), channel_id=1, replica_groups=mesh['x'=4,'y'=4,'z'=8,'c'=2] {'x','y','c','z'}, dimensions={0} | all-to-all | bytes 262144 | tf_op jit(solution)/shard_map/all_to_all | solution.py:215
  71.5 0.0 all-gather.5.cloned.1.call-update
  71.6 0.0 all-gather.3.cloned.1.call-done.loads
  71.6 0.0 copy-start.2
  71.6 1.7 %copy-done.3 = f32[4160,128]{1,0:T(8,128)S(1)} copy-done((f32[4160,128]{1,0:T(8,128)S(1)}, f32[4160,128]{1,0:T(8,128)}, u32[]{:S(2)}) %copy-start.3) | copy-done | bytes 2129944
  73.4 0.9 first_evaluation_0.1
  74.2 11.4 %all_to_all.69 = f32[32,8,128]{2,1,0:T(8,128)S(1)} all-to-all(f32[32,8,128]{2,1,0:T(8,128)S(1)} %bitcast.35), channel_id=1, replica_groups=mesh['x'=4,'y'=4,'z'=8,'c'=2] {'x','y','c'}, dimensions={0} | all-to-all | bytes 262144 | tf_op jit(solution)/shard_map/all_to_all | solution.py:219
  85.7 1.6 %copy-done.4 = f32[4160,128]{1,0:T(8,128)S(1)} copy-done((f32[4160,128]{1,0:T(8,128)S(1)}, f32[4160,128]{1,0:T(8,128)}, u32[]{:S(2)}) %copy-start.4) | copy-done | bytes 2129944
  87.3 0.8 next_evaluation_0.1
  88.1 11.3 %all_to_all.70 = f32[32,8,128]{2,1,0:T(8,128)S(1)} all-to-all(f32[32,8,128]{2,1,0:T(8,128)S(1)} %bitcast.29), channel_id=1, replica_groups=mesh['x'=4,'y'=4,'z'=8,'c'=2] {'x','y','c'}, dimensions={0} | all-to-all | bytes 262144 | tf_op jit(solution)/shard_map/all_to_all | solution.py:219
  99.4 2.1 %back_up_1.1 = f32[256,128]{1,0:T(8,128)S(1)} custom-call(s32[1,4]{1,0:T(1,128)S(1)} %get-tuple-element.16.table, f32[256,128]{1,0:T(8,128)S(1)} %bitcast.24, f32[16,4,128,128]{3,2,1,0:T(8,128)S(1)} %copy-done.2, f32[16,128]{1,0:T(8,128)S(1)} %copy-done.8, f32[16,128]{1,0:T(8,128)S(1)} %get-tuple-element.20.scale), custom_call_target="tpu_custom_call" | custom-call | tf_op jit(solution)/shard_map/back_up_1/pallas_call | solution.py:203
  101.5 19.9 %all_to_all.71 = f32[256,1,128]{2,1,0:T(1,128)S(1)} all-to-all(f32[256,1,128]{2,1,0:T(1,128)S(1)} %bitcast.30), channel_id=1, replica_groups=mesh['x'=4,'y'=4,'z'=8,'c'=2] {'x','y','c','z'}, dimensions={0} | all-to-all | bytes 262144 | tf_op jit(solution)/shard_map/all_to_all | solution.py:215
  121.4 1.6 %copy-done.6 = f32[4160,128]{1,0:T(8,128)S(1)} copy-done((f32[4160,128]{1,0:T(8,128)S(1)}, f32[4160,128]{1,0:T(8,128)}, u32[]{:S(2)}) %copy-start.6) | copy-done | bytes 2129944
  123.0 0.9 first_evaluation_1.1
  123.9 11.4 %all_to_all.72 = f32[32,8,128]{2,1,0:T(8,128)S(1)} all-to-all(f32[32,8,128]{2,1,0:T(8,128)S(1)} %bitcast.34), channel_id=1, replica_groups=mesh['x'=4,'y'=4,'z'=8,'c'=2] {'x','y','c'}, dimensions={0} | all-to-all | bytes 262144 | tf_op jit(solution)/shard_map/all_to_all | solution.py:219
  135.3 1.7 %last_evaluation.1 = (f32[1,128]{1,0:T(1,128)}, f32[2,2]{1,0:T(2,128)}) custom-call(s32[1,4]{1,0:T(1,128)S(1)} %get-tuple-element.16.table, f32[256,128]{1,0:T(8,128)S(1)} %bitcast.32, f32[520,128]{1,0:T(8,128)} %get-tuple-element.25.load, f32[2,2]{1,0:T(2,128)S(1)} %get-tuple-element.27.held), custom_call_target="tpu_custom_call" | custom-call | tf_op jit(solution)/shard_map/last_evaluation/pallas_call | solution.py:203
  (12 shorter events, 0.0 us)
Async XLA Ops:
  7.2 64.4 %all-gather.3.cloned.1.call-start = ((), (), s32[]{:S(2)}) async-start(), calls=%async_computation.6 | async-start | bytes 2396160 | tf_op jit(solution)/shard_map/all_gather | solution.py:223
  7.9 2.2 %copy-start.5 = (f32[16,1,4,128,128]{4,3,2,1,0:T(8,128)S(1)}, f32[16,1,4,128,128]{4,3,2,1,0:T(8,128)}, u32[]{:S(2)}) copy-start(f32[16,1,4,128,128]{4,3,2,1,0:T(8,128)} %param.6) | copy-start | bytes 12582916
  10.0 0.7 copy-start.7
  10.7 0.7 copy-start.9
  11.4 0.7 copy-start.10
  12.1 0.7 copy-start.11
  12.7 35.4 %copy-start.8 = (f32[16,128]{1,0:T(8,128)S(1)}, f32[16,128]{1,0:T(8,128)}, u32[]{:S(2)}) copy-start(f32[16,128]{1,0:T(8,128)} %reward.5) | copy-start | bytes 24580
  16.5 1.9 %copy-start = (f32[16,4,128,128]{3,2,1,0:T(8,128)}, f32[16,4,128,128]{3,2,1,0:T(8,128)S(1)}, u32[]{:S(2)}) copy-start(f32[16,4,128,128]{3,2,1,0:T(8,128)S(1)} %get-tuple-element.19.tiles) | copy-start | bytes 12582916
  18.5 102.9 %all-gather.5.cloned.1.call-start = ((), (), s32[]{:S(2)}) async-start(), calls=%async_computation.7 | async-start | bytes 2396160 | tf_op jit(solution)/shard_map/all_gather | solution.py:223
  48.1 2.2 %copy-start.1 = (f32[16,4,128,128]{3,2,1,0:T(8,128)S(1)}, f32[16,4,128,128]{3,2,1,0:T(8,128)}, u32[]{:S(2)}) copy-start(f32[16,4,128,128]{3,2,1,0:T(8,128)} %copy-done) | copy-start | bytes 12582916
  71.6 27.8 %copy-start.2 = (f32[16,4,128,128]{3,2,1,0:T(8,128)S(1)}, f32[16,4,128,128]{3,2,1,0:T(8,128)}, u32[]{:S(2)}) copy-start(f32[16,4,128,128]{3,2,1,0:T(8,128)} %copy-done) | copy-start | bytes 12582916
  71.6 1.8 %copy-start.3 = (f32[4160,128]{1,0:T(8,128)S(1)}, f32[4160,128]{1,0:T(8,128)}, u32[]{:S(2)}) copy-start(f32[4160,128]{1,0:T(8,128)} %all-gather.3.cloned.1.call-done.loads) | copy-start | bytes 6389764
  85.6 1.6 %copy-start.4 = (f32[4160,128]{1,0:T(8,128)S(1)}, f32[4160,128]{1,0:T(8,128)}, u32[]{:S(2)}) copy-start(f32[4160,128]{1,0:T(8,128)} %all-gather.3.cloned.1.call-done.loads) | copy-start | bytes 6389764
  121.4 1.6 %copy-start.6 = (f32[4160,128]{1,0:T(8,128)S(1)}, f32[4160,128]{1,0:T(8,128)}, u32[]{:S(2)}) copy-start(f32[4160,128]{1,0:T(8,128)} %all-gather.5.cloned.1.call-done.loads) | copy-start | bytes 6389764
Sparse Core Ops, SparseCore 0:
  18.6 46.6 all-gather.2
  71.7 34.7 all-gather.4

commit v4 on v3

v4 whole, which is shorter than its diff:
```python
import functools

import jax
import jax.numpy as jnp
from jax import lax
from jax.experimental import pallas as pl
from jax.experimental.pallas import tpu as pltpu
from jax.sharding import Mesh
from jax.sharding import PartitionSpec as P

SWEEPS = 2
AXES = ("x", "y", "z", "c")
ORDER = ("x", "y", "c", "z")
PLANE = ("x", "y", "c")
LINE = "z"
discount = 0.9
shift = discount / (1.0 - discount) * 0.5
MIB = 1 << 20
AUX = 8
CHUNK = 16
KEEP = True


def pieces(values, count):
    out = []
    for left in reversed(range(count)):
        piece = values.astype(jnp.bfloat16)
        out.append(piece)
        if left:
            values = values - piece.astype(jnp.float32)
    return out


def contract(left, right, dims, count):
    out = None
    for piece in pieces(right, count):
        term = lax.dot_general(left, piece, (dims, ((), ())), preferred_element_type=jnp.float32)
        out = term if out is None else out + term
    return out


def lane_sums(count, row_values):
    at = lax.broadcasted_iota(jnp.int32, (16, 128), 0)
    out = jnp.zeros((16, 128), jnp.float32)
    for i in range(count):
        row = jnp.where(at == i, 1.0, 0.0).astype(jnp.bfloat16)
        out += contract(row, row_values(i), ((1,), (1,)), 2)
    return out


def stacked(rows, height):
    at = lax.broadcasted_iota(jnp.int32, (height, rows[0].shape[-1]), 0)
    out = jnp.zeros(at.shape, jnp.float32)
    for i, row in enumerate(rows):
        out = jnp.where(at == i, row, out)
    return out


def chunk(g, tiles, held_tiles, sems):
    rows = pl.ds(g * CHUNK, CHUNK)
    return pltpu.make_async_copy(tiles.at[:, :, rows, :], held_tiles.at[:, :, rows, :], sems.at[g])


def prepare(
    counts, columns_in, start_in, policy_in, reward_in, tiles,
    rows_out, table, scale, load_0, load_1,
    col_index, start, policy, reward, held_tiles, sums, columns, sems, small_sems,
):
    actions, slots, width, _ = tiles.shape
    loads = (load_0, load_1)
    given = ((columns_in, col_index), (start_in, start), (policy_in, policy), (reward_in, reward))
    small = [pltpu.make_async_copy(source, target, small_sems.at[i]) for i, (source, target) in enumerate(given)]
    for copy in small:
        copy.start()
    for g in range(width // CHUNK):
        chunk(g, tiles, held_tiles, sems).start()
    for copy in small:
        copy.wait()
    rows_out[...] = jnp.broadcast_to(start[...], rows_out.shape)
    columns_of = []
    for k in range(slots):
        block = col_index[0, k]
        place = (block // 16) * 16 + (block % 2) * 8 + (block % 16) // 2
        place = jnp.where(counts[0] > k, place, -1)
        table[0, k] = place
        columns_of.append(jnp.full((1, width), place.astype(jnp.float32)))
    live = [counts[0] > k for k in range(slots)]
    for j in range(SWEEPS):
        columns[j] = jnp.broadcast_to(policy[pl.ds(j, 1), :].astype(jnp.float32), (width, width)).T
    for g in range(width // CHUNK):
        chunk(g, tiles, held_tiles, sems).wait()
        for r in range(g * CHUNK, (g + 1) * CHUNK, 8):
            rows = pl.ds(r, 8)
            chosen = [columns[j, rows, :] for j in range(SWEEPS)]
            held = [[jnp.zeros((8, width), jnp.float32) for _ in range(slots)] for _ in range(SWEEPS)]
            for a in range(actions):
                total = None
                for k in range(slots):
                    tile = jnp.where(live[k], held_tiles[a, k, rows, :], 0.0)
                    total = tile if total is None else total + tile
                    for j in range(SWEEPS):
                        held[j][k] = jnp.where(chosen[j] == float(a), tile, held[j][k])
                sums[a, rows, :] = total
            for j in range(SWEEPS):
                for k in range(slots):
                    loads[j][pl.ds(k * width + r, 8), :] = held[j][k]
    inverse = discount / lane_sums(actions, lambda a: sums[a])
    scale[...] = inverse
    at = lax.broadcasted_iota(jnp.int32, (actions, width), 0)
    for j in range(SWEEPS):
        here = at == policy[pl.ds(j, 1), :]
        picked_scale = jnp.sum(jnp.where(here, inverse, 0.0), axis=0, keepdims=True)
        picked_reward = jnp.sum(jnp.where(here, reward[...], 0.0), axis=0, keepdims=True)
        loads[j][pl.ds(slots * width, AUX), :] = stacked([picked_scale, picked_reward] + columns_of, AUX)


def fetched(table, gathered):
    out = []
    for k in range(table.shape[1]):
        at = table[0, k]
        row = gathered[pl.ds(jnp.maximum(at, 0), 1), :]
        out.append(jnp.where(at >= 0, row, 0.0))
    return out


def back_up(table, gathered, reward, scale, tiles, out, sums, *stream):
    actions, slots, width, _ = tiles.shape
    if stream:
        held_tiles, sems = stream
        for g in range(width // CHUNK):
            chunk(g, tiles, held_tiles, sems).start()
    else:
        held_tiles = tiles
    blocks = [jnp.broadcast_to(b, (8, width)) for b in fetched(table, gathered)]
    for g in range(width // CHUNK):
        if stream:
            chunk(g, tiles, held_tiles, sems).wait()
        for r in range(g * CHUNK, (g + 1) * CHUNK, 8):
            rows = pl.ds(r, 8)
            for a in range(actions):
                total = held_tiles[a, 0, rows, :] * blocks[0]
                for k in range(1, slots):
                    total += held_tiles[a, k, rows, :] * blocks[k]
                sums[a, rows, :] = total
    weighted = lane_sums(actions, lambda a: sums[a])
    backup = jnp.max(reward[...] + scale[...] * weighted, axis=0, keepdims=True)
    out[...] = jnp.broadcast_to(backup, out.shape)


def parts(loads, held_loads, sems):
    high = held_loads.shape[0] // sems.shape[0]
    rows = [pl.ds(b * high, high) for b in range(sems.shape[0])]
    return [pltpu.make_async_copy(loads.at[r, :], held_loads.at[r, :], sems.at[b]) for b, r in enumerate(rows)]


def line_product(gathered, loads, arriving):
    states, width = gathered.shape
    high = width * 4 + AUX
    blocks = loads.shape[0] // high
    halves = [pieces(gathered[pl.ds(h * width, width), :], 3) for h in range(states // width)]
    lane = lax.broadcasted_iota(jnp.int32, (16, width), 1).astype(jnp.float32)
    aux = []

    def weighted_rows(b):
        if arriving:
            arriving[b].wait()
        aux.append(loads[pl.ds(b * high + 4 * width, AUX), :])
        named = jnp.concatenate([aux[b], aux[b]], axis=0)
        fetched_rows = jnp.zeros((16, width), jnp.float32)
        for h, cut in enumerate(halves):
            chosen = jnp.where(named == lane + float(h * width), 1.0, 0.0).astype(jnp.bfloat16)
            for piece in cut:
                fetched_rows += jnp.dot(chosen, piece, preferred_element_type=jnp.float32)
        total = None
        for k in range(4):
            term = loads[pl.ds(b * high + k * width, width), :] * fetched_rows[2 + k : 3 + k]
            total = term if total is None else total + term
        return total

    weighted = lane_sums(blocks, weighted_rows)[:blocks]
    scale = stacked([a[0:1] for a in aux], blocks)
    reward = stacked([a[1:2] for a in aux], blocks)
    return reward + scale * weighted


def spread_out(out, got):
    for i in range(out.shape[0] // got.shape[0]):
        out[pl.ds(i * got.shape[0], got.shape[0]), :] = got


def first_evaluation(j, gathered, before, held, loads, out, bounds, held_loads, sems):
    arriving = parts(loads, held_loads, sems)
    for copy in arriving:
        copy.start()
    change = gathered[...] - before[...]
    top = jnp.max(change)
    bottom = jnp.min(change)
    offset = shift * (bottom + top)
    spread_out(out, line_product(gathered, held_loads, arriving) + discount * offset)
    sweep = lax.broadcasted_iota(jnp.int32, bounds.shape, 0)
    side = lax.broadcasted_iota(jnp.int32, bounds.shape, 1)
    bounds[...] = jnp.where(sweep < j, held[...], jnp.where(side == 0, bottom, top))


def next_evaluation(gathered, loads, out, *stream):
    arriving = []
    if stream:
        arriving = parts(loads, *stream)
        for copy in arriving:
            copy.start()
        loads = stream[0]
    spread_out(out, line_product(gathered, loads, arriving))


def last_evaluation(table, gathered, load, held, out, bounds):
    slots, width = table.shape[1], gathered.shape[1]
    blocks = fetched(table, gathered)
    total = load[pl.ds(0, width), :] * blocks[0]
    for k in range(1, slots):
        total += load[pl.ds(k * width, width), :] * blocks[k]
    weighted = lane_sums(1, lambda _: total)[0:1]
    aux = load[pl.ds(slots * width, AUX), :]
    out[...] = aux[1:2] + aux[0:1] * weighted
    bounds[...] = held[...]


SCALARS = pl.BlockSpec(memory_space=pltpu.SMEM)
VECTORS = pl.BlockSpec(memory_space=pltpu.VMEM)
LEFT = pl.BlockSpec(memory_space=pltpu.HBM)


def shaped(*shape):
    return jax.ShapeDtypeStruct(shape, jnp.float32)


def called(body, given, out_shape, name, scratch=(), scalars=0, left=0, limit=8):
    inside = len(given) - scalars - left
    given = given[: scalars + inside] + tuple(pltpu.with_memory_space_constraint(x, pltpu.HBM) for x in given[scalars + inside :])
    return pl.pallas_call(
        body,
        out_shape=out_shape,
        in_specs=[SCALARS] * scalars + [VECTORS] * inside + [LEFT] * left,
        out_specs=jax.tree.map(lambda _: VECTORS, out_shape),
        scratch_shapes=list(scratch),
        compiler_params=pltpu.CompilerParams(vmem_limit_bytes=limit * MIB),
        name=name,
    )(*given)


def over_all(rows):
    return lax.all_to_all(rows, ORDER, 0, 0, tiled=True)


def over_plane(rows):
    return lax.all_to_all(rows, PLANE, 0, 0, tiled=True)


def over_line(load):
    return lax.all_gather(load, LINE, axis=0, tiled=True)


def local(tiles, counts, col_index, reward, policy, start_values):
    actions, _, slots, width, _ = tiles.shape
    devices = lax.axis_size(AXES)
    tiles = tiles.reshape(actions, slots, width, width)
    all_rows = shaped(devices, width)
    load = shaped(slots * width + AUX, width)
    square = pltpu.VMEM((actions, width, width), jnp.float32)
    tiles_scratch = pltpu.VMEM(tiles.shape, jnp.float32)
    chunks = pltpu.SemaphoreType.DMA((width // CHUNK,))
    given = (col_index, start_values.reshape(1, width), policy, reward, tiles)
    rows, table, scale, load_0, load_1 = pl.pallas_call(
        prepare,
        out_shape=(all_rows, jax.ShapeDtypeStruct(col_index.shape, jnp.int32), shaped(actions, width), load, load),
        in_specs=[SCALARS] + [LEFT] * 5,
        out_specs=(VECTORS, SCALARS, VECTORS, VECTORS, VECTORS),
        scratch_shapes=[
            pltpu.SMEM(col_index.shape, jnp.int32),
            pltpu.VMEM((1, width), jnp.float32),
            pltpu.VMEM(policy.shape, jnp.int32),
            pltpu.VMEM(reward.shape, jnp.float32),
            tiles_scratch,
            square,
            pltpu.VMEM((SWEEPS, width, width), jnp.float32),
            chunks,
            pltpu.SemaphoreType.DMA((4,)),
        ],
        compiler_params=pltpu.CompilerParams(vmem_limit_bytes=12 * MIB),
        name="prepare",
    )(counts, *(pltpu.with_memory_space_constraint(x, pltpu.HBM) for x in given))

    line = lax.axis_size(LINE)
    arrivals = pltpu.SemaphoreType.DMA((line,))
    line_rows = line * (slots * width + AUX)
    held_shape = shaped(line_rows, width)
    loads = over_line(load_0)
    gathered = over_all(rows)
    bounds = jnp.zeros((SWEEPS, 2), jnp.float32)
    for j in range(SWEEPS):
        given = (table, gathered, reward, scale, tiles)
        scratch = [square] + [tiles_scratch, chunks] * (j == 0)
        backup = called(back_up, given, all_rows, f"back_up_{j}", scratch, 1, int(j == 0), 12)
        before, gathered = gathered, over_all(backup)
        if j == 0:
            load_1, gathered = lax.optimization_barrier((load_1, gathered))
            later_loads = over_line(load_1)
        body = functools.partial(first_evaluation, j)
        given = (gathered, before, bounds, loads)
        made = (all_rows, shaped(SWEEPS, 2))
        if KEEP and j == 0:
            current, bounds, loads = called(body, given, made + (held_shape,), f"first_evaluation_{j}", [arrivals], 0, 1)
        else:
            scratch = [pltpu.VMEM((line_rows, width), jnp.float32), arrivals]
            current, bounds = called(body, given, made, f"first_evaluation_{j}", scratch, 0, 1)
        gathered = over_plane(current)
        if j < SWEEPS - 1:
            scratch = [] if KEEP else scratch
            current = called(next_evaluation, (gathered, loads), all_rows, f"next_evaluation_{j}", scratch, 0, int(not KEEP))
            gathered = over_plane(current)
            loads = later_loads
    given = (table, gathered, load_1, bounds)
    current, bounds = called(last_evaluation, given, (shaped(1, width), shaped(SWEEPS, 2)), "last_evaluation", (), 1)
    return current.reshape(width), bounds


def solution(mesh):
    split = Mesh(mesh.devices.reshape(4, 4, 8, 2), AXES)
    placed = (
        P(None, AXES, None, None, None),
        P(AXES),
        P(AXES, None),
        P(None, AXES),
        P(None, AXES),
        P(AXES),
    )
    return jax.shard_map(local, mesh=split, in_specs=placed, out_specs=(P(AXES), P()), check_vma=False)
```

time: 144 us -> 138 us (0.958)
  local copies, waits for them, and re-layouts: 14 us -> 0.01 us
  Pallas kernels: 12.2 us -> 19.3 us
    unnamed x24 -> x4, local copies, waits for them, and re-layouts: 14 us -> 0.01 us
    pallas_call x6, Pallas kernels: 8.43 us -> 15.1 us  [called(): pl.pallas_call(body, out_shape=out_shape, in_specs=[SCALARS] * scalars +...]
  transfers between devices with their start and end apart: 2 -> 2, of which waited for: 0 -> 0; matrix products, arithmetic and copies ran while one was open for 0% -> 0% of each run, Pallas kernels for 4% -> 7%
where the time goes in v4:
time: 138 us
  blocking collectives  103 us (75%)
  Pallas kernels  19.3 us (14%)
  between operations  14.8 us (11%)
    all_to_all x3, blocking collectives, over_all(): return lax.all_to_all(rows, ORDER, 0, 0, tiled=True)  68.6 us
    all_to_all x3, blocking collectives, over_plane(): return lax.all_to_all(rows, PLANE, 0, 0, tiled=True)  34.9 us
    pallas_call x6, Pallas kernels, called(): pl.pallas_call(body, out_shape=out_shape, in_specs=[SCALARS] * scalars +...  15.1 us
    pallas_call x1, Pallas kernels, local(): pl.pallas_call(prepare, out_shape=(all_rows, jax.ShapeDtypeStruct(col_ind...  4.16 us
  transfers between devices with their start and end apart: 2, of which 0 were waited for; matrix products, arithmetic and copies ran while one was open for 0% of the time, Pallas kernels for 7%

profile of v4, /device:TPU:1, one launch (start us, length us, event | category | flops | bytes accessed | tf_op | source)
XLA Modules:
  0.0 137.7 jit_solution(11813032671309069536)
XLA Ops:
  7.2 0.0 all-gather.3.cloned.1.call-start
  7.9 0.0 copy-start.1
  7.9 4.2 %prepare.1 = (f32[256,128]{1,0:T(8,128)S(1)}, s32[1,4]{1,0:T(1,128)S(1)}, f32[16,128]{1,0:T(8,128)S(1)}, f32[520,128]{1,0:T(8,128)}, f32[520,128]{1,0:T(8,128)}) custom-call(s32[1]{0:T(128)S(6)} %copy.11.counts, s32[1,4]{1,0:T(1,128)} %columns_in.1, f32[1,128]{1,0:T(1,128)} %bitcast.38, s32[2,128]{1,0:T(2,128)} %policy_in.1, f32[16,128]{1,0:T(8,128)} %reward.3, ...), custom_call_target="tpu_custom_call" | custom-call | tf_op jit(solution)/shard_map/prepare/pallas_call | solution.py:272
  12.0 0.0 all-gather.3.cloned.1.call-update
  12.1 0.0 all-gather.5.cloned.1.call-start
  12.1 29.6 %all_to_all.67 = f32[256,1,128]{2,1,0:T(1,128)S(1)} all-to-all(f32[256,1,128]{2,1,0:T(1,128)S(1)} %bitcast.35), channel_id=1, replica_groups=mesh['x'=4,'y'=4,'z'=8,'c'=2] {'x','y','c','z'}, dimensions={0} | all-to-all | bytes 262144 | tf_op jit(solution)/shard_map/all_to_all | solution.py:251
  41.7 0.0 copy-done.1
  41.7 3.5 %back_up_0.1 = f32[256,128]{1,0:T(8,128)S(1)} custom-call(s32[1,4]{1,0:T(1,128)S(1)} %get-tuple-element.16.table, f32[256,128]{1,0:T(8,128)S(1)} %bitcast.24, f32[16,128]{1,0:T(8,128)S(1)} %copy-done.1, f32[16,128]{1,0:T(8,128)S(1)} %get-tuple-element.19.scale, f32[16,4,128,128]{3,2,1,0:T(8,128)} %bitcast.22), custom_call_target="tpu_custom_call" | custom-call | tf_op jit(solution)/shard_map/back_up_0/pallas_call | solution.py:239
  45.2 19.7 %all_to_all.68 = f32[256,1,128]{2,1,0:T(1,128)S(1)} all-to-all(f32[256,1,128]{2,1,0:T(1,128)S(1)} %bitcast.33), channel_id=1, replica_groups=mesh['x'=4,'y'=4,'z'=8,'c'=2] {'x','y','c','z'}, dimensions={0} | all-to-all | bytes 262144 | tf_op jit(solution)/shard_map/all_to_all | solution.py:251
  64.9 0.0 all-gather.5.cloned.1.call-update
  64.9 0.0 all-gather.3.cloned.1.call-done.loads
  64.9 0.0 copy-start
  65.0 3.7 %first_evaluation_0.1 = (f32[256,128]{1,0:T(8,128)S(1)}, f32[2,2]{1,0:T(2,128)S(1)}, f32[4160,128]{1,0:T(8,128)S(1)}) custom-call(f32[256,128]{1,0:T(8,128)S(1)} %bitcast.28, f32[256,128]{1,0:T(8,128)S(1)} %bitcast.25, f32[2,2]{1,0:T(2,128)S(1)} %broadcast_1_held.2.held, f32[4160,128]{1,0:T(8,128)} %all-gather.3.cloned.1.call-done.loads), custom_call_target="tpu_custom_call" | custom-call | tf_op jit(solution)/shard_map/first_evaluation_0/pallas_call | solution.py:239
  68.7 12.2 %all_to_all.69 = f32[32,8,128]{2,1,0:T(8,128)S(1)} all-to-all(f32[32,8,128]{2,1,0:T(8,128)S(1)} %bitcast.36), channel_id=1, replica_groups=mesh['x'=4,'y'=4,'z'=8,'c'=2] {'x','y','c'}, dimensions={0} | all-to-all | bytes 262144 | tf_op jit(solution)/shard_map/all_to_all | solution.py:255
  80.9 1.4 %next_evaluation_0.1 = f32[256,128]{1,0:T(8,128)S(1)} custom-call(f32[256,128]{1,0:T(8,128)S(1)} %bitcast.30, f32[4160,128]{1,0:T(8,128)S(1)} %get-tuple-element.23.loads), custom_call_target="tpu_custom_call" | custom-call | tf_op jit(solution)/shard_map/next_evaluation_0/pallas_call | solution.py:239
  82.3 11.3 %all_to_all.70 = f32[32,8,128]{2,1,0:T(8,128)S(1)} all-to-all(f32[32,8,128]{2,1,0:T(8,128)S(1)} %bitcast.31), channel_id=1, replica_groups=mesh['x'=4,'y'=4,'z'=8,'c'=2] {'x','y','c'}, dimensions={0} | all-to-all | bytes 262144 | tf_op jit(solution)/shard_map/all_to_all | solution.py:255
  93.6 0.0 copy-done
  93.6 1.2 back_up_1.1
  94.9 19.4 %all_to_all.71 = f32[256,1,128]{2,1,0:T(1,128)S(1)} all-to-all(f32[256,1,128]{2,1,0:T(1,128)S(1)} %bitcast.32), channel_id=1, replica_groups=mesh['x'=4,'y'=4,'z'=8,'c'=2] {'x','y','c','z'}, dimensions={0} | all-to-all | bytes 262144 | tf_op jit(solution)/shard_map/all_to_all | solution.py:251
  114.2 0.0 all-gather.5.cloned.1.call-done.loads
  114.2 3.6 %first_evaluation_1.1 = (f32[256,128]{1,0:T(8,128)S(1)}, f32[2,2]{1,0:T(2,128)S(1)}) custom-call(f32[256,128]{1,0:T(8,128)S(1)} %bitcast.29, f32[256,128]{1,0:T(8,128)S(1)} %bitcast.27, f32[2,2]{1,0:T(2,128)S(1)} %get-tuple-element.24.held, f32[4160,128]{1,0:T(8,128)} %all-gather.5.cloned.1.call-done.loads), custom_call_target="tpu_custom_call" | custom-call | tf_op jit(solution)/shard_map/first_evaluation_1/pallas_call | solution.py:239
  117.8 11.4 %all_to_all.72 = f32[32,8,128]{2,1,0:T(8,128)S(1)} all-to-all(f32[32,8,128]{2,1,0:T(8,128)S(1)} %bitcast.37), channel_id=1, replica_groups=mesh['x'=4,'y'=4,'z'=8,'c'=2] {'x','y','c'}, dimensions={0} | all-to-all | bytes 262144 | tf_op jit(solution)/shard_map/all_to_all | solution.py:255
  129.2 1.6 %last_evaluation.1 = (f32[1,128]{1,0:T(1,128)}, f32[2,2]{1,0:T(2,128)}) custom-call(s32[1,4]{1,0:T(1,128)S(1)} %get-tuple-element.16.table, f32[256,128]{1,0:T(8,128)S(1)} %bitcast.34, f32[520,128]{1,0:T(8,128)} %get-tuple-element.25.load, f32[2,2]{1,0:T(2,128)S(1)} %get-tuple-element.27.held), custom_call_target="tpu_custom_call" | custom-call | tf_op jit(solution)/shard_map/last_evaluation/pallas_call | solution.py:239
  (1 shorter events, 0.0 us)
Async XLA Ops:
  7.2 57.8 %all-gather.3.cloned.1.call-start = ((), (), s32[]{:S(2)}) async-start(), calls=%async_computation.6 | async-start | bytes 2396160 | tf_op jit(solution)/shard_map/all_gather | solution.py:259
  7.9 33.8 %copy-start.1 = (f32[16,128]{1,0:T(8,128)S(1)}, f32[16,128]{1,0:T(8,128)}, u32[]{:S(2)}) copy-start(f32[16,128]{1,0:T(8,128)} %reward.3) | copy-start | bytes 24580
  12.1 102.2 %all-gather.5.cloned.1.call-start = ((), (), s32[]{:S(2)}) async-start(), calls=%async_computation.7 | async-start | bytes 2396160 | tf_op jit(solution)/shard_map/all_gather | solution.py:259
  64.9 28.7 %copy-start = (f32[16,1,4,128,128]{4,3,2,1,0:T(8,128)S(1)}, f32[16,1,4,128,128]{4,3,2,1,0:T(8,128)}, u32[]{:S(2)}) copy-start(f32[16,1,4,128,128]{4,3,2,1,0:T(8,128)} %param.6) | copy-start | bytes 12582916
Sparse Core Ops, SparseCore 0:
  12.2 46.9 all-gather.2
  65.0 34.8 all-gather.4

commit v5 on v4

v5 whole, which is shorter than its diff:
```python
import functools

import jax
import jax.numpy as jnp
from jax import lax
from jax.experimental import pallas as pl
from jax.experimental.pallas import tpu as pltpu
from jax.sharding import Mesh
from jax.sharding import PartitionSpec as P

SWEEPS = 2
AXES = ("x", "y", "z", "c")
ORDER = ("y", "z", "c", "x")
PLANE = ("y", "z", "c")
LINE = "x"
discount = 0.9
shift = discount / (1.0 - discount) * 0.5
MIB = 1 << 20
AUX = 8
CHUNK = 32


def pieces(values, count):
    out = []
    for left in reversed(range(count)):
        piece = values.astype(jnp.bfloat16)
        out.append(piece)
        if left:
            values = values - piece.astype(jnp.float32)
    return out


def contract(left, right, dims, count):
    out = None
    for piece in pieces(right, count):
        term = lax.dot_general(left, piece, (dims, ((), ())), preferred_element_type=jnp.float32)
        out = term if out is None else out + term
    return out


def lane_sums(count, row_values, places=None):
    at = lax.broadcasted_iota(jnp.int32, (16, 128), 0)
    out = jnp.zeros((16, 128), jnp.float32)
    for i in range(count):
        row = jnp.where(at == (places[i] if places else i), 1.0, 0.0).astype(jnp.bfloat16)
        out += contract(row, row_values(i), ((1,), (1,)), 2)
    return out


def stacked(rows, height, places=None):
    at = lax.broadcasted_iota(jnp.int32, (height, rows[0].shape[-1]), 0)
    out = jnp.zeros(at.shape, jnp.float32)
    for i, row in enumerate(rows):
        out = jnp.where(at == (places[i] if places else i), row, out)
    return out


def chunk(g, tiles, held_tiles, sems):
    rows = pl.ds(g * CHUNK, CHUNK)
    return pltpu.make_async_copy(tiles.at[:, :, rows, :], held_tiles.at[:, :, rows, :], sems.at[g])


def prepare(
    counts, at, columns_in, policy_in, reward_in, tiles,
    table, scale, load, held_tiles,
    col_index, policy, reward, sums, columns, sems, small_sems,
):
    actions, slots, width, _ = tiles.shape
    high = slots * width + AUX
    given = ((columns_in, col_index), (policy_in, policy), (reward_in, reward))
    small = [pltpu.make_async_copy(source, target, small_sems.at[i]) for i, (source, target) in enumerate(given)]
    for copy in small:
        copy.start()
    for g in range(width // CHUNK):
        chunk(g, tiles, held_tiles, sems).start()
    for copy in small:
        copy.wait()
    table[0, slots] = at[0, 0]
    columns_of = []
    for k in range(slots):
        block = col_index[0, k]
        place = (block % 64) * 4 + block // 64
        place = jnp.where(counts[0] > k, place, -1)
        table[0, k] = place
        columns_of.append(jnp.full((1, width), place.astype(jnp.float32)))
    live = [counts[0] > k for k in range(slots)]
    for j in range(SWEEPS):
        columns[j] = jnp.broadcast_to(policy[pl.ds(j, 1), :].astype(jnp.float32), (width, width)).T
    for g in range(width // CHUNK):
        chunk(g, tiles, held_tiles, sems).wait()
        for r in range(g * CHUNK, (g + 1) * CHUNK, 8):
            rows = pl.ds(r, 8)
            chosen = [columns[j, rows, :] for j in range(SWEEPS)]
            held = [[jnp.zeros((8, width), jnp.float32) for _ in range(slots)] for _ in range(SWEEPS)]
            for a in range(actions):
                total = None
                for k in range(slots):
                    tile = jnp.where(live[k], held_tiles[a, k, rows, :], 0.0)
                    total = tile if total is None else total + tile
                    for j in range(SWEEPS):
                        held[j][k] = jnp.where(chosen[j] == float(a), tile, held[j][k])
                sums[a, rows, :] = total
            for j in range(SWEEPS):
                for k in range(slots):
                    load[pl.ds(j * high + k * width + r, 8), :] = held[j][k]
    inverse = discount / lane_sums(actions, lambda a: sums[a])
    scale[...] = inverse
    at = lax.broadcasted_iota(jnp.int32, (actions, width), 0)
    for j in range(SWEEPS):
        here = at == policy[pl.ds(j, 1), :]
        picked_scale = jnp.sum(jnp.where(here, inverse, 0.0), axis=0, keepdims=True)
        picked_reward = jnp.sum(jnp.where(here, reward[...], 0.0), axis=0, keepdims=True)
        load[pl.ds(j * high + slots * width, AUX), :] = stacked([picked_scale, picked_reward] + columns_of, AUX)


def fetched(table, gathered):
    out = []
    for k in range(table.shape[1] - 1):
        at = table[0, k]
        row = gathered[pl.ds(jnp.maximum(at, 0), 1), :]
        out.append(jnp.where(at >= 0, row, 0.0))
    return out


def back_up(table, gathered, tiles, reward, scale, out, sums):
    actions, slots, width, _ = tiles.shape
    blocks = [jnp.broadcast_to(b, (8, width)) for b in fetched(table, gathered)]
    for r in range(0, width, 8):
        rows = pl.ds(r, 8)
        for a in range(actions):
            total = tiles[a, 0, rows, :] * blocks[0]
            for k in range(1, slots):
                total += tiles[a, k, rows, :] * blocks[k]
            sums[a, rows, :] = total
    weighted = lane_sums(actions, lambda a: sums[a])
    backup = jnp.max(reward[...] + scale[...] * weighted, axis=0, keepdims=True)
    out[...] = jnp.broadcast_to(backup, out.shape)


def line_product(j, at, gathered, loads):
    states, width = gathered.shape
    slots, count = 4, len(loads)
    first = j * (slots * width + AUX)
    aux = [load[pl.ds(first + slots * width, AUX), :] for load in loads]
    named = jnp.concatenate(aux, axis=0)
    lane = lax.broadcasted_iota(jnp.int32, named.shape, 1).astype(jnp.float32)
    fetched_rows = None
    for h in range(states // width):
        chosen = jnp.where(named == lane + float(h * width), 1.0, 0.0).astype(jnp.bfloat16)
        term = contract(chosen, gathered[pl.ds(h * width, width), :], ((1,), (0,)), 3)
        fetched_rows = term if fetched_rows is None else fetched_rows + term

    def weighted_rows(b):
        total = None
        for k in range(slots):
            row = b * AUX + 2 + k
            term = loads[b][pl.ds(first + k * width, width), :] * fetched_rows[row : row + 1]
            total = term if total is None else total + term
        return total

    owners = [lax.rem(at - b + count, count) for b in range(count)]
    weighted = lane_sums(count, weighted_rows, owners)[:8]
    scale = stacked([a[0:1] for a in aux], 8, owners)
    reward = stacked([a[1:2] for a in aux], 8, owners)
    return (reward + scale * weighted)[:count]


def spread_out(out, got):
    got = jnp.concatenate([got] * (8 // got.shape[0]), axis=0)
    for i in range(out.shape[0] // 8):
        out[pl.ds(i * 8, 8), :] = got


def first_evaluation(j, table, gathered, before, held, *refs):
    *loads, out, bounds = refs
    change = gathered[...] - before[...]
    top = jnp.max(change)
    bottom = jnp.min(change)
    offset = shift * (bottom + top)
    spread_out(out, line_product(j, table[0, table.shape[1] - 1], gathered, loads) + discount * offset)
    sweep = lax.broadcasted_iota(jnp.int32, bounds.shape, 0)
    side = lax.broadcasted_iota(jnp.int32, bounds.shape, 1)
    bounds[...] = jnp.where(sweep < j, held[...], jnp.where(side == 0, bottom, top))


def next_evaluation(j, table, gathered, *refs):
    *loads, out = refs
    spread_out(out, line_product(j, table[0, table.shape[1] - 1], gathered, loads))


def last_evaluation(j, table, gathered, load, held, out, bounds):
    slots, width = table.shape[1] - 1, gathered.shape[1]
    first = j * (slots * width + AUX)
    blocks = fetched(table, gathered)
    total = load[pl.ds(first, width), :] * blocks[0]
    for k in range(1, slots):
        total += load[pl.ds(first + k * width, width), :] * blocks[k]
    weighted = lane_sums(1, lambda _: total)[0:1]
    aux = load[pl.ds(first + slots * width, AUX), :]
    out[...] = aux[1:2] + aux[0:1] * weighted
    bounds[...] = held[...]


SCALARS = pl.BlockSpec(memory_space=pltpu.SMEM)
VECTORS = pl.BlockSpec(memory_space=pltpu.VMEM)
LEFT = pl.BlockSpec(memory_space=pltpu.HBM)


def shaped(*shape):
    return jax.ShapeDtypeStruct(shape, jnp.float32)


def called(body, given, out_shape, name, scratch=(), limit=8):
    return pl.pallas_call(
        body,
        out_shape=out_shape,
        in_specs=[SCALARS] + [VECTORS] * (len(given) - 1),
        out_specs=jax.tree.map(lambda _: VECTORS, out_shape),
        scratch_shapes=list(scratch),
        compiler_params=pltpu.CompilerParams(vmem_limit_bytes=limit * MIB),
        name=name,
    )(*given)


def over_all(rows):
    return lax.all_to_all(rows, ORDER, 0, 0, tiled=True)


def over_plane(rows):
    return lax.all_to_all(rows, PLANE, 0, 0, tiled=True)


def local(tiles, counts, col_index, reward, policy, start_values):
    actions, _, slots, width, _ = tiles.shape
    devices, line = lax.axis_size(AXES), lax.axis_size(LINE)
    tiles = tiles.reshape(actions, slots, width, width)
    all_rows = shaped(devices, width)
    square = pltpu.VMEM((actions, width, width), jnp.float32)
    gathered = over_all(jnp.broadcast_to(start_values[None], (devices, width)))
    given = (col_index, policy, reward, tiles)
    table, scale, load, held_tiles = pl.pallas_call(
        prepare,
        out_shape=(
            jax.ShapeDtypeStruct((1, slots + 1), jnp.int32),
            shaped(actions, width),
            shaped(SWEEPS * (slots * width + AUX), width),
            shaped(*tiles.shape),
        ),
        in_specs=[SCALARS] * 2 + [LEFT] * 4,
        out_specs=(SCALARS, VECTORS, VECTORS, VECTORS),
        scratch_shapes=[
            pltpu.SMEM(col_index.shape, jnp.int32),
            pltpu.VMEM(policy.shape, jnp.int32),
            pltpu.VMEM(reward.shape, jnp.float32),
            square,
            pltpu.VMEM((SWEEPS, width, width), jnp.float32),
            pltpu.SemaphoreType.DMA((width // CHUNK,)),
            pltpu.SemaphoreType.DMA((3,)),
        ],
        compiler_params=pltpu.CompilerParams(vmem_limit_bytes=8 * MIB),
        name="prepare",
            cost_estimate=pl.CostEstimate(flops=4_000_000, bytes_accessed=8_000_000, transcendentals=0),
    )(counts, lax.axis_index(LINE).reshape(1, 1), *(pltpu.with_memory_space_constraint(x, pltpu.HBM) for x in given))
    loads = [load] + [lax.ppermute(load, LINE, [(i, (i + k) % line) for i in range(line)]) for k in range(1, line)]

    bounds = jnp.zeros((SWEEPS, 2), jnp.float32)
    for j in range(SWEEPS):
        backup = called(back_up, (table, gathered, held_tiles, reward, scale), all_rows, f"back_up_{j}", [square])
        before, gathered = gathered, over_all(backup)
        body = functools.partial(first_evaluation, j)
        made = (all_rows, shaped(SWEEPS, 2))
        current, bounds = called(body, (table, gathered, before, bounds, *loads), made, f"first_evaluation_{j}")
        gathered = over_plane(current)
        if j < SWEEPS - 1:
            current = called(functools.partial(next_evaluation, j), (table, gathered, *loads), all_rows, f"next_evaluation_{j}")
            gathered = over_plane(current)
    body = functools.partial(last_evaluation, SWEEPS - 1)
    current, bounds = called(body, (table, gathered, load, bounds), (shaped(1, width), shaped(SWEEPS, 2)), "last_evaluation")
    return current.reshape(width), bounds


def solution(mesh):
    split = Mesh(mesh.devices.reshape(4, 4, 8, 2), AXES)
    placed = (
        P(None, AXES, None, None, None),
        P(AXES),
        P(AXES, None),
        P(None, AXES),
        P(None, AXES),
        P(AXES),
    )
    return jax.shard_map(local, mesh=split, in_specs=placed, out_specs=(P(AXES), P()), check_vma=False)
```

time: 138 us -> 132 us (0.957)
  between operations: 14.8 us -> 1.37 us
  blocking collectives: 103 us -> 116 us
  Pallas kernels: 19.3 us -> 10.1 us
  starting transfers between devices: 0.08 us -> 4.51 us
    all_to_all x3, blocking collectives: 34.9 us -> 44.7 us  [over_plane(): return lax.all_to_all(rows, PLANE, 0, 0, tiled=True)]
    pallas_call x7, Pallas kernels: 19.3 us -> 10.1 us  [the longest x6 7.02 us: called(): pl.pallas_call(body, out_shape=out_shape, in_specs=[SCALARS] + [VECTORS]...]
    ppermute x0 -> x3, starting transfers between devices: none -> 4.51 us  [local(): lax.ppermute(load, LINE, [(i, (i + k) % line) for i in range(line)])]
    all_to_all x3, blocking collectives: 68.6 us -> 71 us  [over_all(): return lax.all_to_all(rows, ORDER, 0, 0, tiled=True)]
  transfers between devices with their start and end apart: 2 -> 3, of which waited for: 0 -> 0; matrix products, arithmetic and copies ran while one was open for 0% -> 0% of each run, Pallas kernels for 7% -> 1%
where the time goes in v5:
time: 132 us
  blocking collectives  116 us (88%)
  Pallas kernels  10.1 us (8%)
  starting transfers between devices  4.51 us (3%)
  between operations  1.37 us (1%)
    all_to_all x3, blocking collectives, over_all(): return lax.all_to_all(rows, ORDER, 0, 0, tiled=True)  71 us
    all_to_all x3, blocking collectives, over_plane(): return lax.all_to_all(rows, PLANE, 0, 0, tiled=True)  44.7 us
    pallas_call x6, Pallas kernels, called(): pl.pallas_call(body, out_shape=out_shape, in_specs=[SCALARS] + [VECTORS]...  7.02 us
    ppermute x3, starting transfers between devices, local(): lax.ppermute(load, LINE, [(i, (i + k) % line) for i in range(line)])  4.51 us
    pallas_call x1, Pallas kernels, local(): pl.pallas_call(prepare, out_shape=(jax.ShapeDtypeStruct((1, slots + 1), j...  3.06 us
  transfers between devices with their start and end apart: 3, of which 0 were waited for; matrix products, arithmetic and copies ran while one was open for 0% of the time, Pallas kernels for 1%

profile of v5, /device:TPU:1, one launch (start us, length us, event | category | flops | bytes accessed | tf_op | source)
XLA Modules:
  0.0 131.7 jit_solution(3179621688940012493)
XLA Ops:
  0.6 0.0 copy-start
  0.6 0.0 copy-start.1
  1.3 3.1 %prepare.1 = (s32[1,5]{1,0:T(1,128)S(1)}, f32[16,128]{1,0:T(8,128)S(1)}, f32[1040,128]{1,0:T(8,128)S(1)}, f32[16,4,128,128]{3,2,1,0:T(8,128)S(1)}) custom-call(s32[1]{0:T(128)S(6)} %copy.10.counts, s32[1,1]{1,0:T(1,128)} %bitcast.at, s32[1,4]{1,0:T(1,128)} %columns_in.1, s32[2,128]{1,0:T(2,128)} %policy_in.1, f32[16,128]{1,0:T(8,128)} %reward.3, ...), custom_call_target="tpu_custom_call" | custom-call | flops 4000000 | bytes 8000000 | tf_op jit(solution)/shard_map/prepare/pallas_call | solution.py:241
  4.4 3.4 %collective-permute-start.2 = (f32[1040,128]{1,0:T(8,128)S(1)}, f32[1040,128]{1,0:T(8,128)S(1)}, u32[]{:S(2)}, u32[]{:S(2)}) collective-permute-start(f32[1040,128]{1,0:T(8,128)S(1)} %get-tuple-element.15.refs_0_.load), channel_id=1, source_target_pairs={{0,192},{64,0},{128,64},{192,128},{1,193},{65,1},{129,65},{193,129... | collective-permute-start | bytes 1597448 | tf_op jit(solution)/shard_map/ppermute | solution.py:264
  7.8 0.5 collective-permute-start.1
  8.3 0.6 collective-permute-start
  8.9 0.0 copy-done.1
  8.9 0.1 broadcast_in_dim.2
  9.0 29.6 %all_to_all.63 = f32[256,1,128]{2,1,0:T(1,128)S(1)} all-to-all(f32[256,1,128]{2,1,0:T(1,128)S(1)} %broadcast_in_dim.2), channel_id=1, replica_groups=mesh['x'=4,'y'=4,'z'=8,'c'=2] {'y','z','c','x'}, dimensions={0} | all-to-all | bytes 262144 | tf_op jit(solution)/shard_map/all_to_all | solution.py:226
  38.5 0.0 copy-done
  38.5 1.2 back_up_0.1
  39.8 23.2 %all_to_all.64 = f32[256,1,128]{2,1,0:T(1,128)S(1)} all-to-all(f32[256,1,128]{2,1,0:T(1,128)S(1)} %bitcast.25), channel_id=1, replica_groups=mesh['x'=4,'y'=4,'z'=8,'c'=2] {'y','z','c','x'}, dimensions={0} | all-to-all | bytes 262144 | tf_op jit(solution)/shard_map/all_to_all | solution.py:226
  63.0 0.0 collective-permute-done.2.refs_3_
  63.0 0.0 collective-permute-done.1.refs_2_
  63.0 0.0 collective-permute-done.refs_1_
  63.0 1.1 first_evaluation_0.1
  64.1 14.8 %all_to_all.65 = f32[64,4,128]{2,1,0:T(4,128)S(1)} all-to-all(f32[64,4,128]{2,1,0:T(4,128)S(1)} %bitcast.30), channel_id=1, replica_groups=mesh['x'=4,'y'=4,'z'=8,'c'=2] {'y','z','c'}, dimensions={0} | all-to-all | bytes 262144 | tf_op jit(solution)/shard_map/all_to_all | solution.py:230
  79.0 1.1 next_evaluation_0.1
  80.1 15.0 %all_to_all.66 = f32[64,4,128]{2,1,0:T(4,128)S(1)} all-to-all(f32[64,4,128]{2,1,0:T(4,128)S(1)} %bitcast.28), channel_id=1, replica_groups=mesh['x'=4,'y'=4,'z'=8,'c'=2] {'y','z','c'}, dimensions={0} | all-to-all | bytes 262144 | tf_op jit(solution)/shard_map/all_to_all | solution.py:230
  95.1 1.2 back_up_1.1
  96.4 18.2 %all_to_all.67 = f32[256,1,128]{2,1,0:T(1,128)S(1)} all-to-all(f32[256,1,128]{2,1,0:T(1,128)S(1)} %bitcast.24), channel_id=1, replica_groups=mesh['x'=4,'y'=4,'z'=8,'c'=2] {'y','z','c','x'}, dimensions={0} | all-to-all | bytes 262144 | tf_op jit(solution)/shard_map/all_to_all | solution.py:226
  114.6 1.1 first_evaluation_1.1
  115.7 14.8 %all_to_all.68 = f32[64,4,128]{2,1,0:T(4,128)S(1)} all-to-all(f32[64,4,128]{2,1,0:T(4,128)S(1)} %bitcast.29), channel_id=1, replica_groups=mesh['x'=4,'y'=4,'z'=8,'c'=2] {'y','z','c'}, dimensions={0} | all-to-all | bytes 262144 | tf_op jit(solution)/shard_map/all_to_all | solution.py:230
  130.5 1.2 last_evaluation.1
  (1 shorter events, 0.0 us)
Async XLA Ops:
  0.6 37.9 %copy-start = (f32[16,128]{1,0:T(8,128)S(1)}, f32[16,128]{1,0:T(8,128)}, u32[]{:S(2)}) copy-start(f32[16,128]{1,0:T(8,128)} %reward.3) | copy-start | bytes 24580
  0.6 8.3 %copy-start.1 = (f32[128]{0:T(128)S(1)}, f32[128]{0:T(128)}, u32[]{:S(2)}) copy-start(f32[128]{0:T(128)} %param.11) | copy-start | bytes 1540
  4.4 58.6 %collective-permute-start.2 = (f32[1040,128]{1,0:T(8,128)S(1)}, f32[1040,128]{1,0:T(8,128)S(1)}, u32[]{:S(2)}, u32[]{:S(2)}) collective-permute-start(f32[1040,128]{1,0:T(8,128)S(1)} %get-tuple-element.15.refs_0_.load), channel_id=1, source_target_pairs={{0,192},{64,0},{128,64},{192,128},{1,193},{65,1},{129,65},{193,129... | collective-permute-start | bytes 1597448 | tf_op jit(solution)/shard_map/ppermute | solution.py:264
  7.8 55.2 %collective-permute-start.1 = (f32[1040,128]{1,0:T(8,128)S(1)}, f32[1040,128]{1,0:T(8,128)S(1)}, u32[]{:S(2)}, u32[]{:S(2)}) collective-permute-start(f32[1040,128]{1,0:T(8,128)S(1)} %get-tuple-element.15.refs_0_.load), channel_id=1, source_target_pairs={{0,128},{64,192},{128,0},{192,64},{1,129},{65,193},{129,1},{193,65... | collective-permute-start | bytes 1597448 | tf_op jit(solution)/shard_map/ppermute | solution.py:264
  8.3 54.7 %collective-permute-start = (f32[1040,128]{1,0:T(8,128)S(1)}, f32[1040,128]{1,0:T(8,128)S(1)}, u32[]{:S(2)}, u32[]{:S(2)}) collective-permute-start(f32[1040,128]{1,0:T(8,128)S(1)} %get-tuple-element.15.refs_0_.load), channel_id=1, source_target_pairs={{0,64},{64,128},{128,192},{192,0},{1,65},{65,129},{129,193},{193,1... | collective-permute-start | bytes 1597448 | tf_op jit(solution)/shard_map/ppermute | solution.py:264

commit v6 on v5

v6 whole, which is shorter than its diff:
```python
import functools

import jax
import jax.numpy as jnp
from jax import lax
from jax.experimental import pallas as pl
from jax.experimental.pallas import tpu as pltpu
from jax.sharding import Mesh
from jax.sharding import PartitionSpec as P

SWEEPS = 2
AXES = ("x", "y", "z", "c")
discount = 0.9
shift = discount / (1.0 - discount) * 0.5
MIB = 1 << 20
AUX = 8
CHUNK = 32
KEPT = 10


def pieces(values, count):
    out = []
    for left in reversed(range(count)):
        piece = values.astype(jnp.bfloat16)
        out.append(piece)
        if left:
            values = values - piece.astype(jnp.float32)
    return out


def lane_sums(count, row_values):
    at = lax.broadcasted_iota(jnp.int32, (16, 128), 0)
    out = jnp.zeros((16, 128), jnp.float32)
    for i in range(count):
        row = jnp.where(at == i, 1.0, 0.0).astype(jnp.bfloat16)
        for piece in pieces(row_values(i), 2):
            out += lax.dot_general(row, piece, (((1,), (1,)), ((), ())), preferred_element_type=jnp.float32)
    return out


def stacked(rows, height):
    at = lax.broadcasted_iota(jnp.int32, (height, rows[0].shape[-1]), 0)
    out = jnp.zeros(at.shape, jnp.float32)
    for i, row in enumerate(rows):
        out = jnp.where(at == i, row, out)
    return out


def chunk(g, tiles, kept, others, sems):
    rows = pl.ds(g * CHUNK, CHUNK)
    return [
        pltpu.make_async_copy(tiles.at[pl.ds(0, KEPT), :, rows, :], kept.at[:, :, rows, :], sems.at[g, 0]),
        pltpu.make_async_copy(tiles.at[pl.ds(KEPT, others.shape[0]), :, rows, :], others.at[:, :, rows, :], sems.at[g, 1]),
    ]


def prepare(
    counts, columns_in, policy_in, reward_in, tiles,
    table, scale, load, kept,
    col_index, policy, reward, others, sums, columns, sems, small_sems,
):
    actions, slots, width, _ = tiles.shape
    high = slots * width + AUX
    given = ((columns_in, col_index), (policy_in, policy), (reward_in, reward))
    small = [pltpu.make_async_copy(source, target, small_sems.at[i]) for i, (source, target) in enumerate(given)]
    for copy in small:
        copy.start()
    for g in range(width // CHUNK):
        for copy in chunk(g, tiles, kept, others, sems):
            copy.start()
    for copy in small:
        copy.wait()
    for k in range(slots):
        table[0, k] = jnp.where(counts[0] > k, col_index[0, k], -1)
    live = [counts[0] > k for k in range(slots)]
    for j in range(SWEEPS):
        columns[j] = jnp.broadcast_to(policy[pl.ds(j, 1), :].astype(jnp.float32), (width, width)).T
    for g in range(width // CHUNK):
        for copy in chunk(g, tiles, kept, others, sems):
            copy.wait()
        for r in range(g * CHUNK, (g + 1) * CHUNK, 8):
            rows = pl.ds(r, 8)
            chosen = [columns[j, rows, :] for j in range(SWEEPS)]
            held = [[jnp.zeros((8, width), jnp.float32) for _ in range(slots)] for _ in range(SWEEPS)]
            for a in range(actions):
                total = None
                for k in range(slots):
                    source, place = (kept, a) if a < KEPT else (others, a - KEPT)
                    tile = jnp.where(live[k], source[place, k, rows, :], 0.0)
                    total = tile if total is None else total + tile
                    for j in range(SWEEPS):
                        held[j][k] = jnp.where(chosen[j] == float(a), tile, held[j][k])
                sums[a, rows, :] = total
            for j in range(SWEEPS):
                for k in range(slots):
                    load[pl.ds(j * high + k * width + r, 8), :] = held[j][k]
    inverse = discount / lane_sums(actions, lambda a: sums[a])
    scale[...] = inverse
    at = lax.broadcasted_iota(jnp.int32, (actions, width), 0)
    for j in range(SWEEPS):
        here = at == policy[pl.ds(j, 1), :]
        picked_scale = jnp.sum(jnp.where(here, inverse, 0.0), axis=0, keepdims=True)
        picked_reward = jnp.sum(jnp.where(here, reward[...], 0.0), axis=0, keepdims=True)
        load[pl.ds(j * high + slots * width, AUX), :] = stacked([picked_scale, picked_reward], AUX)


def fetched(table, gathered):
    out = []
    for k in range(table.shape[1]):
        at = table[0, k]
        row = gathered[pl.ds(jnp.maximum(at, 0), 1), :]
        out.append(jnp.where(at >= 0, row, 0.0))
    return out


def back_up(table, gathered, *refs):
    if len(refs) == 5:
        tiles, reward, scale, out, sums = refs
        arriving = []
    else:
        kept, reward, scale, source, out, sums, others, sems = refs
        ends = [pltpu.make_async_copy(source.at[KEPT + i], others.at[i], sems.at[i]) for i in range(others.shape[0])]
        arriving = [None] * KEPT + ends
        for copy in ends:
            copy.start()
    actions, width, _ = sums.shape
    blocks = [jnp.broadcast_to(b, (8, width)) for b in fetched(table, gathered)]
    for a in range(actions):
        held, place = (tiles, a) if not arriving else (kept, a) if a < KEPT else (others, a - KEPT)
        if arriving and arriving[a]:
            arriving[a].wait()
        for r in range(0, width, 8):
            rows = pl.ds(r, 8)
            total = held[place, 0, rows, :] * blocks[0]
            for k in range(1, len(blocks)):
                total += held[place, k, rows, :] * blocks[k]
            sums[a, rows, :] = total
    weighted = lane_sums(actions, lambda a: sums[a])
    backup = jnp.max(reward[...] + scale[...] * weighted, axis=0, keepdims=True)
    out[...] = jnp.broadcast_to(backup, out.shape)


def evaluated(j, table, gathered, load):
    slots, width = table.shape[1], gathered.shape[1]
    first = j * (slots * width + AUX)
    blocks = fetched(table, gathered)
    total = load[pl.ds(first, width), :] * blocks[0]
    for k in range(1, slots):
        total += load[pl.ds(first + k * width, width), :] * blocks[k]
    weighted = lane_sums(1, lambda _: total)[0:1]
    aux = load[pl.ds(first + slots * width, AUX), :]
    return aux[1:2] + aux[0:1] * weighted


def first_evaluation(j, table, gathered, before, held, load, out, bounds):
    change = gathered[...] - before[...]
    top = jnp.max(change)
    bottom = jnp.min(change)
    offset = shift * (bottom + top)
    out[...] = jnp.broadcast_to(evaluated(j, table, gathered, load) + discount * offset, out.shape)
    sweep = lax.broadcasted_iota(jnp.int32, bounds.shape, 0)
    side = lax.broadcasted_iota(jnp.int32, bounds.shape, 1)
    bounds[...] = jnp.where(sweep < j, held[...], jnp.where(side == 0, bottom, top))


def next_evaluation(j, table, gathered, load, out):
    out[...] = jnp.broadcast_to(evaluated(j, table, gathered, load), out.shape)


def last_evaluation(j, table, gathered, load, held, out, bounds):
    out[...] = evaluated(j, table, gathered, load)
    bounds[...] = held[...]


SCALARS = pl.BlockSpec(memory_space=pltpu.SMEM)
VECTORS = pl.BlockSpec(memory_space=pltpu.VMEM)
LEFT = pl.BlockSpec(memory_space=pltpu.HBM)


def shaped(*shape):
    return jax.ShapeDtypeStruct(shape, jnp.float32)


def called(body, given, out_shape, name, scratch=(), limit=8, left=0):
    return pl.pallas_call(
        body,
        out_shape=out_shape,
        in_specs=[SCALARS] + [VECTORS] * (len(given) - 1 - left) + [LEFT] * left,
        out_specs=jax.tree.map(lambda _: VECTORS, out_shape),
        scratch_shapes=list(scratch),
        compiler_params=pltpu.CompilerParams(vmem_limit_bytes=limit * MIB),
        name=name,
    )(*given)


def exchange(rows):
    return lax.all_to_all(rows, AXES, 0, 0, tiled=True)


def local(tiles, counts, col_index, reward, policy, start_values):
    actions, _, slots, width, _ = tiles.shape
    devices = lax.axis_size(AXES)
    tiles = tiles.reshape(actions, slots, width, width)
    all_rows = shaped(devices, width)
    square = pltpu.VMEM((actions, width, width), jnp.float32)
    gathered = exchange(jnp.broadcast_to(start_values[None], (devices, width)))
    given = (col_index, policy, reward, tiles)
    table, scale, load, kept = pl.pallas_call(
        prepare,
        out_shape=(
            jax.ShapeDtypeStruct(col_index.shape, jnp.int32),
            shaped(actions, width),
            shaped(SWEEPS * (slots * width + AUX), width),
            shaped(KEPT, *tiles.shape[1:]),
        ),
        in_specs=[SCALARS] + [LEFT] * 4,
        out_specs=(SCALARS, VECTORS, VECTORS, VECTORS),
        scratch_shapes=[
            pltpu.SMEM(col_index.shape, jnp.int32),
            pltpu.VMEM(policy.shape, jnp.int32),
            pltpu.VMEM(reward.shape, jnp.float32),
            pltpu.VMEM((actions - KEPT, *tiles.shape[1:]), jnp.float32),
            square,
            pltpu.VMEM((SWEEPS, width, width), jnp.float32),
            pltpu.SemaphoreType.DMA((width // CHUNK, 2)),
            pltpu.SemaphoreType.DMA((3,)),
        ],
        compiler_params=pltpu.CompilerParams(vmem_limit_bytes=8 * MIB),
        name="prepare",
            cost_estimate=pl.CostEstimate(flops=4_000_000, bytes_accessed=8_000_000, transcendentals=0),
    )(counts, *(pltpu.with_memory_space_constraint(x, pltpu.HBM) for x in given))
    bounds = jnp.zeros((SWEEPS, 2), jnp.float32)
    for j in range(SWEEPS):
        if j == 0:
            source = pltpu.with_memory_space_constraint(tiles, pltpu.HBM)
            rest = [pltpu.VMEM((actions - KEPT, *tiles.shape[1:]), jnp.float32), pltpu.SemaphoreType.DMA((actions - KEPT,))]
            given = (table, gathered, kept, reward, scale, source)
            backup = called(back_up, given, all_rows, f"back_up_{j}", [square] + rest, left=1)
        else:
            backup = called(back_up, (table, gathered, tiles, reward, scale), all_rows, f"back_up_{j}", [square])
        before, gathered = gathered, exchange(backup)
        if j == 0:
            tiles, gathered = lax.optimization_barrier((tiles, gathered))
        body = functools.partial(first_evaluation, j)
        made = (all_rows, shaped(SWEEPS, 2))
        current, bounds = called(body, (table, gathered, before, bounds, load), made, f"first_evaluation_{j}")
        gathered = exchange(current)
        if j < SWEEPS - 1:
            current = called(functools.partial(next_evaluation, j), (table, gathered, load), all_rows, f"next_evaluation_{j}")
            gathered = exchange(current)
    body = functools.partial(last_evaluation, SWEEPS - 1)
    current, bounds = called(body, (table, gathered, load, bounds), (shaped(1, width), shaped(SWEEPS, 2)), "last_evaluation")
    return current.reshape(width), bounds


def solution(mesh):
    split = Mesh(mesh.devices.reshape(4, 4, 8, 2), AXES)
    placed = (
        P(None, AXES, None, None, None),
        P(AXES),
        P(AXES, None),
        P(None, AXES),
        P(None, AXES),
        P(AXES),
    )
    return jax.shard_map(local, mesh=split, in_specs=placed, out_specs=(P(AXES), P()), check_vma=False)
```

time: 132 us -> 132 us (level)
  blocking collectives: 116 us -> 93.1 us
  starting transfers between devices: 4.51 us -> 15.7 us
  waiting for transfers between devices: 0.01 us -> 8.59 us
    all_to_all x6 -> x5, blocking collectives: 116 us -> 93.1 us  [exchange(): return lax.all_to_all(rows, AXES, 0, 0, tiled=True)]
    all_to_all x0 -> x1, starting transfers between devices: none -> 15.7 us  [exchange(): return lax.all_to_all(rows, AXES, 0, 0, tiled=True)]
    all_to_all x0 -> x1, waiting for transfers between devices: none -> 8.59 us  [exchange(): return lax.all_to_all(rows, AXES, 0, 0, tiled=True)]
    ppermute x3 -> x0, starting transfers between devices: 4.51 us -> none  [local(): lax.ppermute(load, LINE, [(i, (i + k) % line) for i in range(line)])]
  transfers between devices with their start and end apart: 3 -> 1, of which waited for: 0 -> 1; matrix products, arithmetic and copies ran while one was open for 0% -> 0% of each run, Pallas kernels for 1% -> 3%
where the time goes in v6:
time: 132 us; the launch traced here: 131 us
  blocking collectives  93.1 us (71%)
  starting transfers between devices  15.7 us (12%)
  Pallas kernels  11.2 us (8%)
  waiting for transfers between devices  8.59 us (7%)
  local copies, waits for them, and re-layouts  1.39 us (1%)
  between operations  1.34 us (1%)
    all_to_all x5, blocking collectives, exchange(): return lax.all_to_all(rows, AXES, 0, 0, tiled=True)  93.1 us
    all_to_all x1, starting transfers between devices, exchange(): return lax.all_to_all(rows, AXES, 0, 0, tiled=True)  15.7 us
    all_to_all x1, waiting for transfers between devices, exchange(): return lax.all_to_all(rows, AXES, 0, 0, tiled=True)  8.59 us
    pallas_call x6, Pallas kernels, called(): pl.pallas_call(body, out_shape=out_shape, in_specs=[SCALARS] + [VECTORS]...  7.51 us
    pallas_call x1, Pallas kernels, local(): pl.pallas_call(prepare, out_shape=(jax.ShapeDtypeStruct(col_index.shape,...  3.65 us
  transfers between devices with their start and end apart: 1, of which 1 were waited for; matrix products, arithmetic and copies ran while one was open for 0% of the time, Pallas kernels for 3%

profile of v6, /device:TPU:1, one launch (start us, length us, event | category | flops | bytes accessed | tf_op | source)
XLA Modules:
  0.0 131.2 jit_solution(17365168129397143735)
XLA Ops:
  0.6 0.0 copy-start.1
  0.6 1.4 %broadcast_in_dim.2 = f32[256,1,128]{2,1,0:T(1,128)} broadcast(f32[128]{0:T(128)} %param.11), dimensions={2} | broadcast | bytes 131584 | tf_op jit(solution)/shard_map/broadcast_in_dim | solution.py:206
  2.0 15.7 %all-to-all-start = ((f32[256,1,128]{2,1,0:T(1,128)}), f32[256,1,128]{2,1,0:T(1,128)S(1)}, u32[]{:S(2)}, u32[]{:S(2)}) async-start(f32[256,1,128]{2,1,0:T(1,128)} %broadcast_in_dim.2), calls=%async_computation | async-start | bytes 262144 | tf_op jit(solution)/shard_map/all_to_all | solution.py:197
  18.3 3.6 %prepare.1 = (s32[1,4]{1,0:T(1,128)S(1)}, f32[16,128]{1,0:T(8,128)S(1)}, f32[1040,128]{1,0:T(8,128)S(1)}, f32[10,4,128,128]{3,2,1,0:T(8,128)S(1)}) custom-call(s32[1]{0:T(128)S(6)} %copy.13.counts, s32[1,4]{1,0:T(1,128)} %columns_in.1, s32[2,128]{1,0:T(2,128)} %policy_in.1, f32[16,128]{1,0:T(8,128)} %refs_1_.3, f32[16,4,128,128]{3,2,1,0:T(8,128)} %bitcast.23), custom_call_target="tpu_custom_call" | custom-call | flops 4000000 | bytes 8000000 | tf_op jit(solution)/shard_map/prepare/pallas_call | solution.py:208
  22.0 8.6 %all-to-all-done = f32[256,1,128]{2,1,0:T(1,128)S(1)} async-done(((f32[256,1,128]{2,1,0:T(1,128)}), f32[256,1,128]{2,1,0:T(1,128)S(1)}, u32[]{:S(2)}, u32[]{:S(2)}) %all-to-all-start) | async-done | bytes 131104 | tf_op jit(solution)/shard_map/all_to_all | solution.py:197
  30.6 0.0 copy-done.1
  30.6 0.0 copy-start
  30.6 2.9 %back_up_0.1 = f32[256,128]{1,0:T(8,128)S(1)} custom-call(s32[1,4]{1,0:T(1,128)S(1)} %get-tuple-element.14.table, f32[256,128]{1,0:T(8,128)S(1)} %bitcast.26, f32[10,4,128,128]{3,2,1,0:T(8,128)S(1)} %get-tuple-element.15.refs_0_, f32[16,128]{1,0:T(8,128)S(1)} %copy-done.1, f32[16,128]{1,0:T(8,128)S(1)} %get-tuple-element.16.refs_2_, f32[16,4,128,128]{3,2,1,0:T(8,128)} %bitcast.24), custom_call_target="tpu_custom_call" | custom-call | tf_op jit(solution)/shard_map/back_up_0/pallas_call | solution.py:185
  33.5 18.6 %all_to_all.64 = f32[256,1,128]{2,1,0:T(1,128)S(1)} all-to-all(f32[256,1,128]{2,1,0:T(1,128)S(1)} %bitcast.30), channel_id=1, replica_groups=mesh['x'=4,'y'=4,'z'=8,'c'=2] {'x','y','z','c'}, dimensions={0} | all-to-all | bytes 262144 | tf_op jit(solution)/shard_map/all_to_all | solution.py:197
  52.1 0.7 first_evaluation_0.1
  52.8 18.6 %all_to_all.65 = f32[256,1,128]{2,1,0:T(1,128)S(1)} all-to-all(f32[256,1,128]{2,1,0:T(1,128)S(1)} %bitcast.37), channel_id=1, replica_groups=mesh['x'=4,'y'=4,'z'=8,'c'=2] {'x','y','z','c'}, dimensions={0} | all-to-all | bytes 262144 | tf_op jit(solution)/shard_map/all_to_all | solution.py:197
  71.4 0.7 next_evaluation_0.1
  72.2 18.6 %all_to_all.66 = f32[256,1,128]{2,1,0:T(1,128)S(1)} all-to-all(f32[256,1,128]{2,1,0:T(1,128)S(1)} %bitcast.36), channel_id=1, replica_groups=mesh['x'=4,'y'=4,'z'=8,'c'=2] {'x','y','z','c'}, dimensions={0} | all-to-all | bytes 262144 | tf_op jit(solution)/shard_map/all_to_all | solution.py:197
  90.8 0.0 copy-done
  90.8 1.2 back_up_1.1
  92.0 18.6 %all_to_all.67 = f32[256,1,128]{2,1,0:T(1,128)S(1)} all-to-all(f32[256,1,128]{2,1,0:T(1,128)S(1)} %bitcast.31), channel_id=1, replica_groups=mesh['x'=4,'y'=4,'z'=8,'c'=2] {'x','y','z','c'}, dimensions={0} | all-to-all | bytes 262144 | tf_op jit(solution)/shard_map/all_to_all | solution.py:197
  110.7 0.7 first_evaluation_1.1
  111.4 18.6 %all_to_all.68 = f32[256,1,128]{2,1,0:T(1,128)S(1)} all-to-all(f32[256,1,128]{2,1,0:T(1,128)S(1)} %bitcast.38), channel_id=1, replica_groups=mesh['x'=4,'y'=4,'z'=8,'c'=2] {'x','y','z','c'}, dimensions={0} | all-to-all | bytes 262144 | tf_op jit(solution)/shard_map/all_to_all | solution.py:197
  130.0 1.2 last_evaluation.1
  (1 shorter events, 0.0 us)
Async XLA Ops:
  0.6 30.0 %copy-start.1 = (f32[16,128]{1,0:T(8,128)S(1)}, f32[16,128]{1,0:T(8,128)}, u32[]{:S(2)}) copy-start(f32[16,128]{1,0:T(8,128)} %refs_1_.3) | copy-start | bytes 24580
  2.0 28.6 %all-to-all-start = ((f32[256,1,128]{2,1,0:T(1,128)}), f32[256,1,128]{2,1,0:T(1,128)S(1)}, u32[]{:S(2)}, u32[]{:S(2)}) async-start(f32[256,1,128]{2,1,0:T(1,128)} %broadcast_in_dim.2), calls=%async_computation | async-start | bytes 262144 | tf_op jit(solution)/shard_map/all_to_all | solution.py:197
  30.6 60.2 %copy-start = (f32[16,1,4,128,128]{4,3,2,1,0:T(8,128)S(1)}, f32[16,1,4,128,128]{4,3,2,1,0:T(8,128)}, u32[]{:S(2)}) copy-start(f32[16,1,4,128,128]{4,3,2,1,0:T(8,128)} %param.6) | copy-start | bytes 12582916

commit v7 on v6

--- a/solution.py
+++ b/solution.py
@@ -113,22 +113,21 @@
     return out
 
 
-def back_up(table, gathered, *refs):
-    if len(refs) == 5:
-        tiles, reward, scale, out, sums = refs
-        arriving = []
-    else:
-        kept, reward, scale, source, out, sums, others, sems = refs
+def back_up(table, gathered, kept, reward, scale, source, out, *refs):
+    if len(refs) == 3:
+        others, sums, sems = refs
         ends = [pltpu.make_async_copy(source.at[KEPT + i], others.at[i], sems.at[i]) for i in range(others.shape[0])]
-        arriving = [None] * KEPT + ends
         for copy in ends:
             copy.start()
+    else:
+        others, ends = source, []
+        (sums,) = refs
     actions, width, _ = sums.shape
     blocks = [jnp.broadcast_to(b, (8, width)) for b in fetched(table, gathered)]
     for a in range(actions):
-        held, place = (tiles, a) if not arriving else (kept, a) if a < KEPT else (others, a - KEPT)
-        if arriving and arriving[a]:
-            arriving[a].wait()
+        held, place = (kept, a) if a < KEPT else (others, a - KEPT)
+        if ends and a >= KEPT:
+            ends[place].wait()
         for r in range(0, width, 8):
             rows = pl.ds(r, 8)
             total = held[place, 0, rows, :] * blocks[0]
@@ -233,14 +232,13 @@
     for j in range(SWEEPS):
         if j == 0:
             source = pltpu.with_memory_space_constraint(tiles, pltpu.HBM)
-            rest = [pltpu.VMEM((actions - KEPT, *tiles.shape[1:]), jnp.float32), pltpu.SemaphoreType.DMA((actions - KEPT,))]
+            rest = shaped(actions - KEPT, *tiles.shape[1:])
             given = (table, gathered, kept, reward, scale, source)
-            backup = called(back_up, given, all_rows, f"back_up_{j}", [square] + rest, left=1)
+            scratch = [square, pltpu.SemaphoreType.DMA((actions - KEPT,))]
+            backup, others = called(back_up, given, (all_rows, rest), f"back_up_{j}", scratch, left=1)
         else:
-            backup = called(back_up, (table, gathered, tiles, reward, scale), all_rows, f"back_up_{j}", [square])
+            backup = called(back_up, (table, gathered, kept, reward, scale, others), all_rows, f"back_up_{j}", [square])
         before, gathered = gathered, exchange(backup)
-        if j == 0:
-            tiles, gathered = lax.optimization_barrier((tiles, gathered))
         body = functools.partial(first_evaluation, j)
         made = (all_rows, shaped(SWEEPS, 2))
         current, bounds = called(body, (table, gathered, before, bounds, load), made, f"first_evaluation_{j}")

time: 132 us -> 131 us (level)
  no operation moved by 1% of the time
where the time goes in v7:
time: 131 us
  blocking collectives  93.1 us (71%)
  starting transfers between devices  15.7 us (12%)
  Pallas kernels  10.9 us (8%)
  waiting for transfers between devices  8.63 us (7%)
  local copies, waits for them, and re-layouts  1.39 us (1%)
  between operations  1.34 us (1%)
    all_to_all x5, blocking collectives, exchange(): return lax.all_to_all(rows, AXES, 0, 0, tiled=True)  93.1 us
    all_to_all x1, starting transfers between devices, exchange(): return lax.all_to_all(rows, AXES, 0, 0, tiled=True)  15.7 us
    all_to_all x1, waiting for transfers between devices, exchange(): return lax.all_to_all(rows, AXES, 0, 0, tiled=True)  8.63 us
    pallas_call x6, Pallas kernels, called(): pl.pallas_call(body, out_shape=out_shape, in_specs=[SCALARS] + [VECTORS]...  7.27 us
    pallas_call x1, Pallas kernels, local(): pl.pallas_call(prepare, out_shape=(jax.ShapeDtypeStruct(col_index.shape,...  3.61 us
  transfers between devices with their start and end apart: 1, of which 1 were waited for; matrix products, arithmetic and copies ran while one was open for 0% of the time, Pallas kernels for 3%

profile of v7, /device:TPU:1, one launch (start us, length us, event | category | flops | bytes accessed | tf_op | source)
XLA Modules:
  0.0 131.0 jit_solution(17175749265660020292)
XLA Ops:
  0.6 0.0 copy-start
  0.6 1.4 %broadcast_in_dim.2 = f32[256,1,128]{2,1,0:T(1,128)} broadcast(f32[128]{0:T(128)} %param.11), dimensions={2} | broadcast | bytes 131584 | tf_op jit(solution)/shard_map/broadcast_in_dim | solution.py:205
  2.0 15.7 %all-to-all-start = ((f32[256,1,128]{2,1,0:T(1,128)}), f32[256,1,128]{2,1,0:T(1,128)S(1)}, u32[]{:S(2)}, u32[]{:S(2)}) async-start(f32[256,1,128]{2,1,0:T(1,128)} %broadcast_in_dim.2), calls=%async_computation | async-start | bytes 262144 | tf_op jit(solution)/shard_map/all_to_all | solution.py:196
  18.3 3.6 %prepare.1 = (s32[1,4]{1,0:T(1,128)S(1)}, f32[16,128]{1,0:T(8,128)S(1)}, f32[1040,128]{1,0:T(8,128)S(1)}, f32[10,4,128,128]{3,2,1,0:T(8,128)S(1)}) custom-call(s32[1]{0:T(128)S(6)} %copy.13.counts, s32[1,4]{1,0:T(1,128)} %columns_in.1, s32[2,128]{1,0:T(2,128)} %policy_in.1, f32[16,128]{1,0:T(8,128)} %reward.3, f32[16,4,128,128]{3,2,1,0:T(8,128)} %bitcast.36), custom_call_target="tpu_custom_call" | custom-call | flops 4000000 | bytes 8000000 | tf_op jit(solution)/shard_map/prepare/pallas_call | solution.py:207
  22.0 8.6 %all-to-all-done = f32[256,1,128]{2,1,0:T(1,128)S(1)} async-done(((f32[256,1,128]{2,1,0:T(1,128)}), f32[256,1,128]{2,1,0:T(1,128)S(1)}, u32[]{:S(2)}, u32[]{:S(2)}) %all-to-all-start) | async-done | bytes 131104 | tf_op jit(solution)/shard_map/all_to_all | solution.py:196
  30.6 0.0 copy-done
  30.6 2.6 %back_up_0.1 = (f32[256,128]{1,0:T(8,128)S(1)}, f32[6,4,128,128]{3,2,1,0:T(8,128)S(1)}) custom-call(s32[1,4]{1,0:T(1,128)S(1)} %get-tuple-element.14.table, f32[256,128]{1,0:T(8,128)S(1)} %bitcast.23, f32[10,4,128,128]{3,2,1,0:T(8,128)S(1)} %get-tuple-element.15.kept, f32[16,128]{1,0:T(8,128)S(1)} %copy-done, f32[16,128]{1,0:T(8,128)S(1)} %get-tuple-element.16.scale, ...), custom_call_target="tpu_custom_call" | custom-call | tf_op jit(solution)/shard_map/back_up_0/pallas_call | solution.py:184
  33.2 18.6 %all_to_all.63 = f32[256,1,128]{2,1,0:T(1,128)S(1)} all-to-all(f32[256,1,128]{2,1,0:T(1,128)S(1)} %bitcast.35), channel_id=1, replica_groups=mesh['x'=4,'y'=4,'z'=8,'c'=2] {'x','y','z','c'}, dimensions={0} | all-to-all | bytes 262144 | tf_op jit(solution)/shard_map/all_to_all | solution.py:196
  51.8 0.7 first_evaluation_0.1
  52.6 18.6 %all_to_all.64 = f32[256,1,128]{2,1,0:T(1,128)S(1)} all-to-all(f32[256,1,128]{2,1,0:T(1,128)S(1)} %bitcast.33), channel_id=1, replica_groups=mesh['x'=4,'y'=4,'z'=8,'c'=2] {'x','y','z','c'}, dimensions={0} | all-to-all | bytes 262144 | tf_op jit(solution)/shard_map/all_to_all | solution.py:196
  71.2 0.7 next_evaluation_0.1
  71.9 18.6 %all_to_all.65 = f32[256,1,128]{2,1,0:T(1,128)S(1)} all-to-all(f32[256,1,128]{2,1,0:T(1,128)S(1)} %bitcast.32), channel_id=1, replica_groups=mesh['x'=4,'y'=4,'z'=8,'c'=2] {'x','y','z','c'}, dimensions={0} | all-to-all | bytes 262144 | tf_op jit(solution)/shard_map/all_to_all | solution.py:196
  90.5 1.3 back_up_1.1
  91.8 18.6 %all_to_all.66 = f32[256,1,128]{2,1,0:T(1,128)S(1)} all-to-all(f32[256,1,128]{2,1,0:T(1,128)S(1)} %bitcast.27), channel_id=1, replica_groups=mesh['x'=4,'y'=4,'z'=8,'c'=2] {'x','y','z','c'}, dimensions={0} | all-to-all | bytes 262144 | tf_op jit(solution)/shard_map/all_to_all | solution.py:196
  110.4 0.7 first_evaluation_1.1
  111.1 18.6 %all_to_all.67 = f32[256,1,128]{2,1,0:T(1,128)S(1)} all-to-all(f32[256,1,128]{2,1,0:T(1,128)S(1)} %bitcast.34), channel_id=1, replica_groups=mesh['x'=4,'y'=4,'z'=8,'c'=2] {'x','y','z','c'}, dimensions={0} | all-to-all | bytes 262144 | tf_op jit(solution)/shard_map/all_to_all | solution.py:196
  129.8 1.2 last_evaluation.1
  (1 shorter events, 0.0 us)
Async XLA Ops:
  0.6 30.0 %copy-start = (f32[16,128]{1,0:T(8,128)S(1)}, f32[16,128]{1,0:T(8,128)}, u32[]{:S(2)}) copy-start(f32[16,128]{1,0:T(8,128)} %reward.3) | copy-start | bytes 24580
  2.0 28.6 %all-to-all-start = ((f32[256,1,128]{2,1,0:T(1,128)}), f32[256,1,128]{2,1,0:T(1,128)S(1)}, u32[]{:S(2)}, u32[]{:S(2)}) async-start(f32[256,1,128]{2,1,0:T(1,128)} %broadcast_in_dim.2), calls=%async_computation | async-start | bytes 262144 | tf_op jit(solution)/shard_map/all_to_all | solution.py:196

commit v8 on v7

--- a/solution.py
+++ b/solution.py
@@ -14,7 +14,7 @@
 shift = discount / (1.0 - discount) * 0.5
 MIB = 1 << 20
 AUX = 8
-CHUNK = 32
+CHUNKS = ((0, 32), (32, 32), (64, 32), (96, 24), (120, 8))
 KEPT = 10
 
 
@@ -28,13 +28,13 @@
     return out
 
 
-def lane_sums(count, row_values):
-    at = lax.broadcasted_iota(jnp.int32, (16, 128), 0)
+def lane_sums(first, row_values):
+    at = lax.broadcasted_iota(jnp.int32, (16, 256), 0)
     out = jnp.zeros((16, 128), jnp.float32)
-    for i in range(count):
-        row = jnp.where(at == i, 1.0, 0.0).astype(jnp.bfloat16)
-        for piece in pieces(row_values(i), 2):
-            out += lax.dot_general(row, piece, (((1,), (1,)), ((), ())), preferred_element_type=jnp.float32)
+    for i, values in enumerate(row_values):
+        row = jnp.where(at == first + i, 1.0, 0.0).astype(jnp.bfloat16)
+        both = jnp.concatenate(pieces(values, 2), axis=1)
+        out += lax.dot_general(row, both, (((1,), (1,)), ((), ())), preferred_element_type=jnp.float32)
     return out
 
 
@@ -47,7 +47,7 @@
 
 
 def chunk(g, tiles, kept, others, sems):
-    rows = pl.ds(g * CHUNK, CHUNK)
+    rows = pl.ds(*CHUNKS[g])
     return [
         pltpu.make_async_copy(tiles.at[pl.ds(0, KEPT), :, rows, :], kept.at[:, :, rows, :], sems.at[g, 0]),
         pltpu.make_async_copy(tiles.at[pl.ds(KEPT, others.shape[0]), :, rows, :], others.at[:, :, rows, :], sems.at[g, 1]),
@@ -65,7 +65,7 @@
     small = [pltpu.make_async_copy(source, target, small_sems.at[i]) for i, (source, target) in enumerate(given)]
     for copy in small:
         copy.start()
-    for g in range(width // CHUNK):
+    for g in range(len(CHUNKS)):
         for copy in chunk(g, tiles, kept, others, sems):
             copy.start()
     for copy in small:
@@ -75,10 +75,10 @@
     live = [counts[0] > k for k in range(slots)]
     for j in range(SWEEPS):
         columns[j] = jnp.broadcast_to(policy[pl.ds(j, 1), :].astype(jnp.float32), (width, width)).T
-    for g in range(width // CHUNK):
+    for g in range(len(CHUNKS)):
         for copy in chunk(g, tiles, kept, others, sems):
             copy.wait()
-        for r in range(g * CHUNK, (g + 1) * CHUNK, 8):
+        for r in range(CHUNKS[g][0], sum(CHUNKS[g]), 8):
             rows = pl.ds(r, 8)
             chosen = [columns[j, rows, :] for j in range(SWEEPS)]
             held = [[jnp.zeros((8, width), jnp.float32) for _ in range(slots)] for _ in range(SWEEPS)]
@@ -94,7 +94,7 @@
             for j in range(SWEEPS):
                 for k in range(slots):
                     load[pl.ds(j * high + k * width + r, 8), :] = held[j][k]
-    inverse = discount / lane_sums(actions, lambda a: sums[a])
+    inverse = discount / lane_sums(0, [sums[a] for a in range(actions)])
     scale[...] = inverse
     at = lax.broadcasted_iota(jnp.int32, (actions, width), 0)
     for j in range(SWEEPS):
@@ -124,17 +124,18 @@
         (sums,) = refs
     actions, width, _ = sums.shape
     blocks = [jnp.broadcast_to(b, (8, width)) for b in fetched(table, gathered)]
-    for a in range(actions):
-        held, place = (kept, a) if a < KEPT else (others, a - KEPT)
-        if ends and a >= KEPT:
-            ends[place].wait()
-        for r in range(0, width, 8):
-            rows = pl.ds(r, 8)
-            total = held[place, 0, rows, :] * blocks[0]
-            for k in range(1, len(blocks)):
-                total += held[place, k, rows, :] * blocks[k]
-            sums[a, rows, :] = total
-    weighted = lane_sums(actions, lambda a: sums[a])
+    weighted = jnp.zeros((actions, width), jnp.float32)
+    for start, count, held in ((0, KEPT, kept), (KEPT, actions - KEPT, others)):
+        for i in range(count):
+            if ends and held is others:
+                ends[i].wait()
+            for r in range(0, width, 8):
+                rows = pl.ds(r, 8)
+                total = held[i, 0, rows, :] * blocks[0]
+                for k in range(1, len(blocks)):
+                    total += held[i, k, rows, :] * blocks[k]
+                sums[start + i, rows, :] = total
+        weighted += lane_sums(start, [sums[start + i] for i in range(count)])
     backup = jnp.max(reward[...] + scale[...] * weighted, axis=0, keepdims=True)
     out[...] = jnp.broadcast_to(backup, out.shape)
 
@@ -146,7 +147,7 @@
     total = load[pl.ds(first, width), :] * blocks[0]
     for k in range(1, slots):
         total += load[pl.ds(first + k * width, width), :] * blocks[k]
-    weighted = lane_sums(1, lambda _: total)[0:1]
+    weighted = lane_sums(0, [total])[0:1]
     aux = load[pl.ds(first + slots * width, AUX), :]
     return aux[1:2] + aux[0:1] * weighted
 
@@ -221,7 +222,7 @@
             pltpu.VMEM((actions - KEPT, *tiles.shape[1:]), jnp.float32),
             square,
             pltpu.VMEM((SWEEPS, width, width), jnp.float32),
-            pltpu.SemaphoreType.DMA((width // CHUNK, 2)),
+            pltpu.SemaphoreType.DMA((len(CHUNKS), 2)),
             pltpu.SemaphoreType.DMA((3,)),
         ],
         compiler_params=pltpu.CompilerParams(vmem_limit_bytes=8 * MIB),

time: 131 us -> 131 us (level)
  no operation moved by 1% of the time
where the time goes in v8:
time: 131 us; the launch traced here: 130 us
  blocking collectives  93.1 us (71%)
  starting transfers between devices  15.7 us (12%)
  Pallas kernels  10.1 us (8%)
  waiting for transfers between devices  8.92 us (7%)
  local copies, waits for them, and re-layouts  1.39 us (1%)
  between operations  1.34 us (1%)
    all_to_all x5, blocking collectives, exchange(): return lax.all_to_all(rows, AXES, 0, 0, tiled=True)  93.1 us
    all_to_all x1, starting transfers between devices, exchange(): return lax.all_to_all(rows, AXES, 0, 0, tiled=True)  15.7 us
    all_to_all x1, waiting for transfers between devices, exchange(): return lax.all_to_all(rows, AXES, 0, 0, tiled=True)  8.92 us
    pallas_call x6, Pallas kernels, called(): pl.pallas_call(body, out_shape=out_shape, in_specs=[SCALARS] + [VECTORS]...  6.74 us
    pallas_call x1, Pallas kernels, local(): pl.pallas_call(prepare, out_shape=(jax.ShapeDtypeStruct(col_index.shape,...  3.32 us
  transfers between devices with their start and end apart: 1, of which 1 were waited for; matrix products, arithmetic and copies ran while one was open for 0% of the time, Pallas kernels for 3%

profile of v8, /device:TPU:1, one launch (start us, length us, event | category | flops | bytes accessed | tf_op | source)
XLA Modules:
  0.0 130.5 jit_solution(1761909757045008237)
XLA Ops:
  0.6 0.0 copy-start
  0.6 1.4 %broadcast_in_dim.2 = f32[256,1,128]{2,1,0:T(1,128)} broadcast(f32[128]{0:T(128)} %param.11), dimensions={2} | broadcast | bytes 131584 | tf_op jit(solution)/shard_map/broadcast_in_dim | solution.py:206
  2.0 15.7 %all-to-all-start = ((f32[256,1,128]{2,1,0:T(1,128)}), f32[256,1,128]{2,1,0:T(1,128)S(1)}, u32[]{:S(2)}, u32[]{:S(2)}) async-start(f32[256,1,128]{2,1,0:T(1,128)} %broadcast_in_dim.2), calls=%async_computation | async-start | bytes 262144 | tf_op jit(solution)/shard_map/all_to_all | solution.py:197
  18.3 3.3 %prepare.1 = (s32[1,4]{1,0:T(1,128)S(1)}, f32[16,128]{1,0:T(8,128)S(1)}, f32[1040,128]{1,0:T(8,128)S(1)}, f32[10,4,128,128]{3,2,1,0:T(8,128)S(1)}) custom-call(s32[1]{0:T(128)S(6)} %copy.13.counts, s32[1,4]{1,0:T(1,128)} %columns_in.1, s32[2,128]{1,0:T(2,128)} %policy_in.1, f32[16,128]{1,0:T(8,128)} %reward.3, f32[16,4,128,128]{3,2,1,0:T(8,128)} %bitcast.36), custom_call_target="tpu_custom_call" | custom-call | flops 4000000 | bytes 8000000 | tf_op jit(solution)/shard_map/prepare/pallas_call | solution.py:208
  21.7 8.9 %all-to-all-done = f32[256,1,128]{2,1,0:T(1,128)S(1)} async-done(((f32[256,1,128]{2,1,0:T(1,128)}), f32[256,1,128]{2,1,0:T(1,128)S(1)}, u32[]{:S(2)}, u32[]{:S(2)}) %all-to-all-start) | async-done | bytes 131104 | tf_op jit(solution)/shard_map/all_to_all | solution.py:197
  30.6 0.0 copy-done
  30.6 2.3 %back_up_0.1 = (f32[256,128]{1,0:T(8,128)S(1)}, f32[6,4,128,128]{3,2,1,0:T(8,128)S(1)}) custom-call(s32[1,4]{1,0:T(1,128)S(1)} %get-tuple-element.14.table, f32[256,128]{1,0:T(8,128)S(1)} %bitcast.23, f32[10,4,128,128]{3,2,1,0:T(8,128)S(1)} %get-tuple-element.15.kept, f32[16,128]{1,0:T(8,128)S(1)} %copy-done, f32[16,128]{1,0:T(8,128)S(1)} %get-tuple-element.16.scale, ...), custom_call_target="tpu_custom_call" | custom-call | tf_op jit(solution)/shard_map/back_up_0/pallas_call | solution.py:185
  32.9 18.6 %all_to_all.63 = f32[256,1,128]{2,1,0:T(1,128)S(1)} all-to-all(f32[256,1,128]{2,1,0:T(1,128)S(1)} %bitcast.35), channel_id=1, replica_groups=mesh['x'=4,'y'=4,'z'=8,'c'=2] {'x','y','z','c'}, dimensions={0} | all-to-all | bytes 262144 | tf_op jit(solution)/shard_map/all_to_all | solution.py:197
  51.5 0.7 first_evaluation_0.1
  52.2 18.6 %all_to_all.64 = f32[256,1,128]{2,1,0:T(1,128)S(1)} all-to-all(f32[256,1,128]{2,1,0:T(1,128)S(1)} %bitcast.33), channel_id=1, replica_groups=mesh['x'=4,'y'=4,'z'=8,'c'=2] {'x','y','z','c'}, dimensions={0} | all-to-all | bytes 262144 | tf_op jit(solution)/shard_map/all_to_all | solution.py:197
  70.8 0.7 next_evaluation_0.1
  71.6 18.6 %all_to_all.65 = f32[256,1,128]{2,1,0:T(1,128)S(1)} all-to-all(f32[256,1,128]{2,1,0:T(1,128)S(1)} %bitcast.32), channel_id=1, replica_groups=mesh['x'=4,'y'=4,'z'=8,'c'=2] {'x','y','z','c'}, dimensions={0} | all-to-all | bytes 262144 | tf_op jit(solution)/shard_map/all_to_all | solution.py:197
  90.2 1.1 back_up_1.1
  91.3 18.6 %all_to_all.66 = f32[256,1,128]{2,1,0:T(1,128)S(1)} all-to-all(f32[256,1,128]{2,1,0:T(1,128)S(1)} %bitcast.27), channel_id=1, replica_groups=mesh['x'=4,'y'=4,'z'=8,'c'=2] {'x','y','z','c'}, dimensions={0} | all-to-all | bytes 262144 | tf_op jit(solution)/shard_map/all_to_all | solution.py:197
  109.9 0.7 first_evaluation_1.1
  110.6 18.6 %all_to_all.67 = f32[256,1,128]{2,1,0:T(1,128)S(1)} all-to-all(f32[256,1,128]{2,1,0:T(1,128)S(1)} %bitcast.34), channel_id=1, replica_groups=mesh['x'=4,'y'=4,'z'=8,'c'=2] {'x','y','z','c'}, dimensions={0} | all-to-all | bytes 262144 | tf_op jit(solution)/shard_map/all_to_all | solution.py:197
  129.2 1.2 last_evaluation.1
  (1 shorter events, 0.0 us)
Async XLA Ops:
  0.6 30.0 %copy-start = (f32[16,128]{1,0:T(8,128)S(1)}, f32[16,128]{1,0:T(8,128)}, u32[]{:S(2)}) copy-start(f32[16,128]{1,0:T(8,128)} %reward.3) | copy-start | bytes 24580
  2.0 28.6 %all-to-all-start = ((f32[256,1,128]{2,1,0:T(1,128)}), f32[256,1,128]{2,1,0:T(1,128)S(1)}, u32[]{:S(2)}, u32[]{:S(2)}) async-start(f32[256,1,128]{2,1,0:T(1,128)} %broadcast_in_dim.2), calls=%async_computation | async-start | bytes 262144 | tf_op jit(solution)/shard_map/all_to_all | solution.py:197

commit v9 on v8

--- a/solution.py
+++ b/solution.py
@@ -16,6 +16,7 @@
 AUX = 8
 CHUNKS = ((0, 32), (32, 32), (64, 32), (96, 24), (120, 8))
 KEPT = 10
+SLOTS = 4
 
 
 def pieces(values, count):
@@ -56,7 +57,7 @@
 
 def prepare(
     counts, columns_in, policy_in, reward_in, tiles,
-    table, scale, load, kept,
+    named, scale, load, kept,
     col_index, policy, reward, others, sums, columns, sems, small_sems,
 ):
     actions, slots, width, _ = tiles.shape
@@ -70,8 +71,8 @@
             copy.start()
     for copy in small:
         copy.wait()
-    for k in range(slots):
-        table[0, k] = jnp.where(counts[0] > k, col_index[0, k], -1)
+    blocks = [jnp.where(counts[0] > k, col_index[0, k], -1) for k in range(slots)]
+    named[...] = stacked([jnp.full((1, width), block.astype(jnp.float32)) for block in blocks], AUX)
     live = [counts[0] > k for k in range(slots)]
     for j in range(SWEEPS):
         columns[j] = jnp.broadcast_to(policy[pl.ds(j, 1), :].astype(jnp.float32), (width, width)).T
@@ -104,16 +105,19 @@
         load[pl.ds(j * high + slots * width, AUX), :] = stacked([picked_scale, picked_reward], AUX)
 
 
-def fetched(table, gathered):
-    out = []
-    for k in range(table.shape[1]):
-        at = table[0, k]
-        row = gathered[pl.ds(jnp.maximum(at, 0), 1), :]
-        out.append(jnp.where(at >= 0, row, 0.0))
-    return out
-
-
-def back_up(table, gathered, kept, reward, scale, source, out, *refs):
+def fetched(named, gathered):
+    states, width = gathered.shape
+    wide = jnp.concatenate([named[...]] * 2, axis=0)
+    lane = lax.broadcasted_iota(jnp.int32, wide.shape, 1).astype(jnp.float32)
+    chosen = [jnp.where(wide == lane + float(h), 1.0, 0.0).astype(jnp.bfloat16) for h in range(0, states, width)]
+    chosen = jnp.concatenate(chosen, axis=1)
+    rows = jnp.zeros(wide.shape, jnp.float32)
+    for piece in pieces(gathered[...], 3):
+        rows += jnp.dot(chosen, piece, preferred_element_type=jnp.float32)
+    return [rows[k : k + 1] for k in range(SLOTS)]
+
+
+def back_up(named, gathered, kept, reward, scale, source, out, *refs):
     if len(refs) == 3:
         others, sums, sems = refs
         ends = [pltpu.make_async_copy(source.at[KEPT + i], others.at[i], sems.at[i]) for i in range(others.shape[0])]
@@ -123,7 +127,7 @@
         others, ends = source, []
         (sums,) = refs
     actions, width, _ = sums.shape
-    blocks = [jnp.broadcast_to(b, (8, width)) for b in fetched(table, gathered)]
+    blocks = [jnp.broadcast_to(b, (8, width)) for b in fetched(named, gathered)]
     weighted = jnp.zeros((actions, width), jnp.float32)
     for start, count, held in ((0, KEPT, kept), (KEPT, actions - KEPT, others)):
         for i in range(count):
@@ -140,10 +144,10 @@
     out[...] = jnp.broadcast_to(backup, out.shape)
 
 
-def evaluated(j, table, gathered, load):
-    slots, width = table.shape[1], gathered.shape[1]
+def evaluated(j, named, gathered, load):
+    slots, width = SLOTS, gathered.shape[1]
     first = j * (slots * width + AUX)
-    blocks = fetched(table, gathered)
+    blocks = fetched(named, gathered)
     total = load[pl.ds(first, width), :] * blocks[0]
     for k in range(1, slots):
         total += load[pl.ds(first + k * width, width), :] * blocks[k]
@@ -152,23 +156,23 @@
     return aux[1:2] + aux[0:1] * weighted
 
 
-def first_evaluation(j, table, gathered, before, held, load, out, bounds):
+def first_evaluation(j, named, gathered, before, held, load, out, bounds):
     change = gathered[...] - before[...]
     top = jnp.max(change)
     bottom = jnp.min(change)
     offset = shift * (bottom + top)
-    out[...] = jnp.broadcast_to(evaluated(j, table, gathered, load) + discount * offset, out.shape)
+    out[...] = jnp.broadcast_to(evaluated(j, named, gathered, load) + discount * offset, out.shape)
     sweep = lax.broadcasted_iota(jnp.int32, bounds.shape, 0)
     side = lax.broadcasted_iota(jnp.int32, bounds.shape, 1)
     bounds[...] = jnp.where(sweep < j, held[...], jnp.where(side == 0, bottom, top))
 
 
-def next_evaluation(j, table, gathered, load, out):
-    out[...] = jnp.broadcast_to(evaluated(j, table, gathered, load), out.shape)
-
-
-def last_evaluation(j, table, gathered, load, held, out, bounds):
-    out[...] = evaluated(j, table, gathered, load)
+def next_evaluation(j, named, gathered, load, out):
+    out[...] = jnp.broadcast_to(evaluated(j, named, gathered, load), out.shape)
+
+
+def last_evaluation(j, named, gathered, load, held, out, bounds):
+    out[...] = evaluated(j, named, gathered, load)
     bounds[...] = held[...]
 
 
@@ -185,7 +189,7 @@
     return pl.pallas_call(
         body,
         out_shape=out_shape,
-        in_specs=[SCALARS] + [VECTORS] * (len(given) - 1 - left) + [LEFT] * left,
+        in_specs=[VECTORS] * (len(given) - left) + [LEFT] * left,
         out_specs=jax.tree.map(lambda _: VECTORS, out_shape),
         scratch_shapes=list(scratch),
         compiler_params=pltpu.CompilerParams(vmem_limit_bytes=limit * MIB),
@@ -205,16 +209,16 @@
     square = pltpu.VMEM((actions, width, width), jnp.float32)
     gathered = exchange(jnp.broadcast_to(start_values[None], (devices, width)))
     given = (col_index, policy, reward, tiles)
-    table, scale, load, kept = pl.pallas_call(
+    named, scale, load, kept = pl.pallas_call(
         prepare,
         out_shape=(
-            jax.ShapeDtypeStruct(col_index.shape, jnp.int32),
+            shaped(AUX, width),
             shaped(actions, width),
             shaped(SWEEPS * (slots * width + AUX), width),
             shaped(KEPT, *tiles.shape[1:]),
         ),
         in_specs=[SCALARS] + [LEFT] * 4,
-        out_specs=(SCALARS, VECTORS, VECTORS, VECTORS),
+        out_specs=(VECTORS,) * 4,
         scratch_shapes=[
             pltpu.SMEM(col_index.shape, jnp.int32),
             pltpu.VMEM(policy.shape, jnp.int32),
@@ -234,21 +238,21 @@
         if j == 0:
             source = pltpu.with_memory_space_constraint(tiles, pltpu.HBM)
             rest = shaped(actions - KEPT, *tiles.shape[1:])
-            given = (table, gathered, kept, reward, scale, source)
+            given = (named, gathered, kept, reward, scale, source)
             scratch = [square, pltpu.SemaphoreType.DMA((actions - KEPT,))]
             backup, others = called(back_up, given, (all_rows, rest), f"back_up_{j}", scratch, left=1)
         else:
-            backup = called(back_up, (table, gathered, kept, reward, scale, others), all_rows, f"back_up_{j}", [square])
+            backup = called(back_up, (named, gathered, kept, reward, scale, others), all_rows, f"back_up_{j}", [square])
         before, gathered = gathered, exchange(backup)
         body = functools.partial(first_evaluation, j)
         made = (all_rows, shaped(SWEEPS, 2))
-        current, bounds = called(body, (table, gathered, before, bounds, load), made, f"first_evaluation_{j}")
+        current, bounds = called(body, (named, gathered, before, bounds, load), made, f"first_evaluation_{j}")
         gathered = exchange(current)
         if j < SWEEPS - 1:
-            current = called(functools.partial(next_evaluation, j), (table, gathered, load), all_rows, f"next_evaluation_{j}")
+            current = called(functools.partial(next_evaluation, j), (named, gathered, load), all_rows, f"next_evaluation_{j}")
             gathered = exchange(current)
     body = functools.partial(last_evaluation, SWEEPS - 1)
-    current, bounds = called(body, (table, gathered, load, bounds), (shaped(1, width), shaped(SWEEPS, 2)), "last_evaluation")
+    current, bounds = called(body, (named, gathered, load, bounds), (shaped(1, width), shaped(SWEEPS, 2)), "last_evaluation")
     return current.reshape(width), bounds
 
 

time: 131 us -> 128 us (0.977)
  Pallas kernels: 10.1 us -> 7.4 us
    pallas_call x7, Pallas kernels: 10.1 us -> 7.4 us  [the longest x6 4.26 us: called(): pl.pallas_call(body, out_shape=out_shape, in_specs=[VECTORS] * (len(given...]
  transfers between devices with their start and end apart: 1 -> 1, of which waited for: 1 -> 1; matrix products, arithmetic and copies ran while one was open for 0% -> 0% of each run, Pallas kernels for 3% -> 2%
where the time goes in v9:
time: 128 us
  blocking collectives  93.1 us (73%)
  starting transfers between devices  15.7 us (12%)
  waiting for transfers between devices  9.11 us (7%)
  Pallas kernels  7.4 us (6%)
  local copies, waits for them, and re-layouts  1.39 us (1%)
  between operations  1.33 us (1%)
    all_to_all x5, blocking collectives, exchange(): return lax.all_to_all(rows, AXES, 0, 0, tiled=True)  93.1 us
    all_to_all x1, starting transfers between devices, exchange(): return lax.all_to_all(rows, AXES, 0, 0, tiled=True)  15.7 us
    all_to_all x1, waiting for transfers between devices, exchange(): return lax.all_to_all(rows, AXES, 0, 0, tiled=True)  9.11 us
    pallas_call x6, Pallas kernels, called(): pl.pallas_call(body, out_shape=out_shape, in_specs=[VECTORS] * (len(given...  4.26 us
    pallas_call x1, Pallas kernels, local(): pl.pallas_call(prepare, out_shape=(shaped(AUX, width), shaped(actions, wi...  3.13 us
  transfers between devices with their start and end apart: 1, of which 1 were waited for; matrix products, arithmetic and copies ran while one was open for 0% of the time, Pallas kernels for 2%

profile of v9, /device:TPU:1, one launch (start us, length us, event | category | flops | bytes accessed | tf_op | source)
XLA Modules:
  0.0 128.0 jit_solution(14742854313946213395)
XLA Ops:
  0.6 0.0 copy-start
  0.6 1.4 %broadcast_in_dim.2 = f32[256,1,128]{2,1,0:T(1,128)} broadcast(f32[128]{0:T(128)} %param.11), dimensions={2} | broadcast | bytes 131584 | tf_op jit(solution)/shard_map/broadcast_in_dim | solution.py:210
  2.0 15.7 %all-to-all-start = ((f32[256,1,128]{2,1,0:T(1,128)}), f32[256,1,128]{2,1,0:T(1,128)S(1)}, u32[]{:S(2)}, u32[]{:S(2)}) async-start(f32[256,1,128]{2,1,0:T(1,128)} %broadcast_in_dim.2), calls=%async_computation | async-start | bytes 262144 | tf_op jit(solution)/shard_map/all_to_all | solution.py:201
  18.3 3.1 %prepare.1 = (f32[8,128]{1,0:T(8,128)S(1)}, f32[16,128]{1,0:T(8,128)S(1)}, f32[1040,128]{1,0:T(8,128)S(1)}, f32[10,4,128,128]{3,2,1,0:T(8,128)S(1)}) custom-call(s32[1]{0:T(128)S(6)} %copy.13.counts, s32[1,4]{1,0:T(1,128)} %columns_in.1, s32[2,128]{1,0:T(2,128)} %policy_in.1, f32[16,128]{1,0:T(8,128)} %reward.3, f32[16,4,128,128]{3,2,1,0:T(8,128)} %bitcast.36), custom_call_target="tpu_custom_call" | custom-call | flops 4000000 | bytes 8000000 | tf_op jit(solution)/shard_map/prepare/pallas_call | solution.py:212
  21.5 9.1 %all-to-all-done = f32[256,1,128]{2,1,0:T(1,128)S(1)} async-done(((f32[256,1,128]{2,1,0:T(1,128)}), f32[256,1,128]{2,1,0:T(1,128)S(1)}, u32[]{:S(2)}, u32[]{:S(2)}) %all-to-all-start) | async-done | bytes 131104 | tf_op jit(solution)/shard_map/all_to_all | solution.py:201
  30.6 0.0 copy-done
  30.6 1.7 %back_up_0.1 = (f32[256,128]{1,0:T(8,128)S(1)}, f32[6,4,128,128]{3,2,1,0:T(8,128)S(1)}) custom-call(f32[8,128]{1,0:T(8,128)S(1)} %get-tuple-element.14.named, f32[256,128]{1,0:T(8,128)S(1)} %bitcast.23, f32[10,4,128,128]{3,2,1,0:T(8,128)S(1)} %get-tuple-element.15.kept, f32[16,128]{1,0:T(8,128)S(1)} %copy-done, f32[16,128]{1,0:T(8,128)S(1)} %get-tuple-element.16.scale, ...), custom_call_target="tpu_custom_call" | custom-call | tf_op jit(solution)/shard_map/back_up_0/pallas_call | solution.py:189
  32.3 18.6 %all_to_all.63 = f32[256,1,128]{2,1,0:T(1,128)S(1)} all-to-all(f32[256,1,128]{2,1,0:T(1,128)S(1)} %bitcast.35), channel_id=1, replica_groups=mesh['x'=4,'y'=4,'z'=8,'c'=2] {'x','y','z','c'}, dimensions={0} | all-to-all | bytes 262144 | tf_op jit(solution)/shard_map/all_to_all | solution.py:201
  51.0 0.3 first_evaluation_0.1
  51.3 18.6 %all_to_all.64 = f32[256,1,128]{2,1,0:T(1,128)S(1)} all-to-all(f32[256,1,128]{2,1,0:T(1,128)S(1)} %bitcast.33), channel_id=1, replica_groups=mesh['x'=4,'y'=4,'z'=8,'c'=2] {'x','y','z','c'}, dimensions={0} | all-to-all | bytes 262144 | tf_op jit(solution)/shard_map/all_to_all | solution.py:201
  69.9 0.3 next_evaluation_0.1
  70.2 18.6 %all_to_all.65 = f32[256,1,128]{2,1,0:T(1,128)S(1)} all-to-all(f32[256,1,128]{2,1,0:T(1,128)S(1)} %bitcast.31), channel_id=1, replica_groups=mesh['x'=4,'y'=4,'z'=8,'c'=2] {'x','y','z','c'}, dimensions={0} | all-to-all | bytes 262144 | tf_op jit(solution)/shard_map/all_to_all | solution.py:201
  88.8 0.7 back_up_1.1
  89.6 18.6 %all_to_all.66 = f32[256,1,128]{2,1,0:T(1,128)S(1)} all-to-all(f32[256,1,128]{2,1,0:T(1,128)S(1)} %bitcast.29), channel_id=1, replica_groups=mesh['x'=4,'y'=4,'z'=8,'c'=2] {'x','y','z','c'}, dimensions={0} | all-to-all | bytes 262144 | tf_op jit(solution)/shard_map/all_to_all | solution.py:201
  108.2 0.3 first_evaluation_1.1
  108.5 18.6 %all_to_all.67 = f32[256,1,128]{2,1,0:T(1,128)S(1)} all-to-all(f32[256,1,128]{2,1,0:T(1,128)S(1)} %bitcast.34), channel_id=1, replica_groups=mesh['x'=4,'y'=4,'z'=8,'c'=2] {'x','y','z','c'}, dimensions={0} | all-to-all | bytes 262144 | tf_op jit(solution)/shard_map/all_to_all | solution.py:201
  127.1 0.8 last_evaluation.1
  (1 shorter events, 0.0 us)
Async XLA Ops:
  0.6 30.0 %copy-start = (f32[16,128]{1,0:T(8,128)S(1)}, f32[16,128]{1,0:T(8,128)}, u32[]{:S(2)}) copy-start(f32[16,128]{1,0:T(8,128)} %reward.3) | copy-start | bytes 24580
  2.0 28.6 %all-to-all-start = ((f32[256,1,128]{2,1,0:T(1,128)}), f32[256,1,128]{2,1,0:T(1,128)S(1)}, u32[]{:S(2)}, u32[]{:S(2)}) async-start(f32[256,1,128]{2,1,0:T(1,128)} %broadcast_in_dim.2), calls=%async_computation | async-start | bytes 262144 | tf_op jit(solution)/shard_map/all_to_all | solution.py:201

commit v10 on v5

v10 whole, which is shorter than its diff:
```python
import functools

import jax
import jax.numpy as jnp
from jax import lax
from jax.experimental import pallas as pl
from jax.experimental.pallas import tpu as pltpu
from jax.sharding import Mesh
from jax.sharding import PartitionSpec as P

SWEEPS = 2
AXES = ("x", "y", "z", "c")
ORDER = ("y", "z", "x", "c")
PLANE = ("y", "z")
LINE = ("x", "c")
discount = 0.9
shift = discount / (1.0 - discount) * 0.5
MIB = 1 << 20
AUX = 8
CHUNKS = ((0, 32), (32, 32), (64, 32), (96, 24), (120, 8))
SLOTS = 4


def pieces(values, count):
    out = []
    for left in reversed(range(count)):
        piece = values.astype(jnp.bfloat16)
        out.append(piece)
        if left:
            values = values - piece.astype(jnp.float32)
    return out


def contract(left, right):
    out = jnp.zeros((left.shape[0], right.shape[1]), jnp.float32)
    for piece in pieces(right, 3):
        out += jnp.dot(left, piece, preferred_element_type=jnp.float32)
    return out


def lane_sums(row_values, places=None):
    at = lax.broadcasted_iota(jnp.int32, (16, 256), 0).astype(jnp.float32)
    out = jnp.zeros((16, 128), jnp.float32)
    for i, values in enumerate(row_values):
        place = jnp.concatenate([places[i]] * 2, axis=1) if places else float(i)
        row = jnp.where(at == place, 1.0, 0.0).astype(jnp.bfloat16)
        both = jnp.concatenate(pieces(values, 2), axis=1)
        out += lax.dot_general(row, both, (((1,), (1,)), ((), ())), preferred_element_type=jnp.float32)
    return out


def stacked(rows, height, places=None):
    at = lax.broadcasted_iota(jnp.int32, (height, rows[0].shape[-1]), 0).astype(jnp.float32)
    out = jnp.zeros(at.shape, jnp.float32)
    for i, row in enumerate(rows):
        out = jnp.where(at == (places[i] if places else float(i)), row, out)
    return out


def chunk(g, tiles, kept, sems):
    rows = pl.ds(*CHUNKS[g])
    return pltpu.make_async_copy(tiles.at[:, :, rows, :], kept.at[:, :, rows, :], sems.at[g])


def prepare(
    counts, at, columns_in, policy_in, reward_in, tiles,
    named, scale, load, kept,
    col_index, policy, reward, sums, columns, sems, small_sems,
):
    actions, slots, width, _ = tiles.shape
    high = slots * width + AUX
    given = ((columns_in, col_index), (policy_in, policy), (reward_in, reward))
    small = [pltpu.make_async_copy(source, target, small_sems.at[i]) for i, (source, target) in enumerate(given)]
    for copy in small:
        copy.start()
    for g in range(len(CHUNKS)):
        chunk(g, tiles, kept, sems).start()
    for copy in small:
        copy.wait()
    columns_of = []
    for k in range(slots):
        block = col_index[0, k]
        place = (block % 64) // 2 * 8 + block // 64 * 2 + block % 2
        place = jnp.where(counts[0] > k, place, -1)
        columns_of.append(jnp.full((1, width), place.astype(jnp.float32)))
    named[...] = stacked(columns_of, AUX)
    columns_of.append(jnp.full((1, width), at[0, 0].astype(jnp.float32)))
    live = [counts[0] > k for k in range(slots)]
    for j in range(SWEEPS):
        columns[j] = jnp.broadcast_to(policy[pl.ds(j, 1), :].astype(jnp.float32), (width, width)).T
    for g in range(len(CHUNKS)):
        chunk(g, tiles, kept, sems).wait()
        for r in range(CHUNKS[g][0], sum(CHUNKS[g]), 8):
            rows = pl.ds(r, 8)
            chosen = [columns[j, rows, :] for j in range(SWEEPS)]
            held = [[jnp.zeros((8, width), jnp.float32) for _ in range(slots)] for _ in range(SWEEPS)]
            for a in range(actions):
                total = None
                for k in range(slots):
                    tile = jnp.where(live[k], kept[a, k, rows, :], 0.0)
                    total = tile if total is None else total + tile
                    for j in range(SWEEPS):
                        held[j][k] = jnp.where(chosen[j] == float(a), tile, held[j][k])
                sums[a, rows, :] = total
            for j in range(SWEEPS):
                for k in range(slots):
                    load[pl.ds(j * high + k * width + r, 8), :] = held[j][k]
    inverse = discount / lane_sums([sums[a] for a in range(actions)])
    scale[...] = inverse
    action = lax.broadcasted_iota(jnp.int32, (actions, width), 0)
    for j in range(SWEEPS):
        here = action == policy[pl.ds(j, 1), :]
        picked_scale = jnp.sum(jnp.where(here, inverse, 0.0), axis=0, keepdims=True)
        picked_reward = jnp.sum(jnp.where(here, reward[...], 0.0), axis=0, keepdims=True)
        load[pl.ds(j * high + slots * width, AUX), :] = stacked([picked_scale, picked_reward] + columns_of, AUX)


def fetched(named, gathered):
    states, width = gathered.shape
    lane = lax.broadcasted_iota(jnp.int32, named.shape, 1).astype(jnp.float32)
    chosen = [jnp.where(named == lane + float(h), 1.0, 0.0).astype(jnp.bfloat16) for h in range(0, states, width)]
    return contract(jnp.concatenate(chosen, axis=1), gathered[...])


def back_up(named, gathered, tiles, reward, scale, out, sums):
    actions, width, _ = sums.shape
    rows_of = fetched(jnp.concatenate([named[...]] * 2, axis=0), gathered)
    blocks = [jnp.broadcast_to(rows_of[k : k + 1], (8, width)) for k in range(SLOTS)]
    for a in range(actions):
        for r in range(0, width, 8):
            rows = pl.ds(r, 8)
            total = tiles[a, 0, rows, :] * blocks[0]
            for k in range(1, SLOTS):
                total += tiles[a, k, rows, :] * blocks[k]
            sums[a, rows, :] = total
    weighted = lane_sums([sums[a] for a in range(actions)])
    backup = jnp.max(reward[...] + scale[...] * weighted, axis=0, keepdims=True)
    out[...] = jnp.broadcast_to(backup, out.shape)


def products(load, first, rows_of, start):
    width = load.shape[1]
    total = load[pl.ds(first, width), :] * rows_of[start : start + 1]
    for k in range(1, SLOTS):
        total += load[pl.ds(first + k * width, width), :] * rows_of[start + k : start + k + 1]
    return total


def line_product(j, gathered, loads):
    width = gathered.shape[1]
    first = j * (SLOTS * width + AUX)
    aux = [load[pl.ds(first + SLOTS * width, AUX), :] for load in loads]
    rows_of = fetched(jnp.concatenate(aux, axis=0), gathered)
    owners = [a[2 + SLOTS : 3 + SLOTS] for a in aux]
    weighted = lane_sums([products(load, first, rows_of, b * AUX + 2) for b, load in enumerate(loads)], owners)[:8]
    return stacked([a[1:2] for a in aux], 8, owners) + stacked([a[0:1] for a in aux], 8, owners) * weighted


def spread_out(out, got):
    for i in range(out.shape[0] // 8):
        out[pl.ds(i * 8, 8), :] = got


def first_evaluation(j, gathered, before, held, *refs):
    *loads, out, bounds = refs
    change = gathered[...] - before[...]
    top = jnp.max(change)
    bottom = jnp.min(change)
    offset = shift * (bottom + top)
    spread_out(out, line_product(j, gathered, loads) + discount * offset)
    sweep = lax.broadcasted_iota(jnp.int32, bounds.shape, 0)
    side = lax.broadcasted_iota(jnp.int32, bounds.shape, 1)
    bounds[...] = jnp.where(sweep < j, held[...], jnp.where(side == 0, bottom, top))


def next_evaluation(j, gathered, *refs):
    *loads, out = refs
    spread_out(out, line_product(j, gathered, loads))


def last_evaluation(j, named, gathered, load, held, out, bounds):
    width = gathered.shape[1]
    first = j * (SLOTS * width + AUX)
    rows_of = fetched(jnp.concatenate([named[...]] * 2, axis=0), gathered)
    weighted = lane_sums([products(load, first, rows_of, 0)])[0:1]
    aux = load[pl.ds(first + SLOTS * width, AUX), :]
    out[...] = aux[1:2] + aux[0:1] * weighted
    bounds[...] = held[...]


SCALARS = pl.BlockSpec(memory_space=pltpu.SMEM)
VECTORS = pl.BlockSpec(memory_space=pltpu.VMEM)
LEFT = pl.BlockSpec(memory_space=pltpu.HBM)


def shaped(*shape):
    return jax.ShapeDtypeStruct(shape, jnp.float32)


def called(body, given, out_shape, name, scratch=(), limit=8, left=0):
    return pl.pallas_call(
        body,
        out_shape=out_shape,
        in_specs=[VECTORS] * (len(given) - left) + [LEFT] * left,
        out_specs=jax.tree.map(lambda _: VECTORS, out_shape),
        scratch_shapes=list(scratch),
        compiler_params=pltpu.CompilerParams(vmem_limit_bytes=limit * MIB),
        name=name,
    )(*given)


def over_all(rows):
    return lax.all_to_all(rows, ORDER, 0, 0, tiled=True)


def over_plane(rows):
    return lax.all_to_all(rows, PLANE, 0, 0, tiled=True)


def local(tiles, counts, col_index, reward, policy, start_values):
    actions, _, slots, width, _ = tiles.shape
    devices = lax.axis_size(AXES)
    tiles = tiles.reshape(actions, slots, width, width)
    all_rows = shaped(devices, width)
    square = pltpu.VMEM((actions, width, width), jnp.float32)
    gathered = over_all(jnp.broadcast_to(start_values[None], (devices, width)))
    given = (col_index, policy, reward, tiles)
    named, scale, load, kept = pl.pallas_call(
        prepare,
        out_shape=(
            shaped(AUX, width),
            shaped(actions, width),
            shaped(SWEEPS * (slots * width + AUX), width),
            shaped(*tiles.shape),
        ),
        in_specs=[SCALARS] * 2 + [LEFT] * 4,
        out_specs=(VECTORS,) * 4,
        scratch_shapes=[
            pltpu.SMEM(col_index.shape, jnp.int32),
            pltpu.VMEM(policy.shape, jnp.int32),
            pltpu.VMEM(reward.shape, jnp.float32),
            square,
            pltpu.VMEM((SWEEPS, width, width), jnp.float32),
            pltpu.SemaphoreType.DMA((len(CHUNKS),)),
            pltpu.SemaphoreType.DMA((3,)),
        ],
        compiler_params=pltpu.CompilerParams(vmem_limit_bytes=8 * MIB),
        name="prepare",
            cost_estimate=pl.CostEstimate(flops=4_000_000, bytes_accessed=8_000_000, transcendentals=0),
    )(counts, lax.axis_index(LINE).reshape(1, 1), *(pltpu.with_memory_space_constraint(x, pltpu.HBM) for x in given))
    far = lax.axis_size(LINE[0])
    loads = [load] + [lax.ppermute(load, LINE[0], [(i, (i + k) % far) for i in range(far)]) for k in range(1, far)]
    bounds = jnp.zeros((SWEEPS, 2), jnp.float32)
    all_rows = shaped(devices, width)
    for j in range(SWEEPS):
        backup = called(back_up, (named, gathered, kept, reward, scale), all_rows, f"back_up_{j}", [square])
        before, gathered = gathered, over_all(backup)
        if j == 0:
            *loads, gathered = lax.optimization_barrier((*loads, gathered))
            loads += [lax.ppermute(held, LINE[1], [(0, 1), (1, 0)]) for held in loads]
        body = functools.partial(first_evaluation, j)
        made = (all_rows, shaped(SWEEPS, 2))
        current, bounds = called(body, (gathered, before, bounds, *loads), made, f"first_evaluation_{j}")
        gathered = over_plane(current)
        if j < SWEEPS - 1:
            current = called(functools.partial(next_evaluation, j), (gathered, *loads), all_rows, f"next_evaluation_{j}")
            gathered = over_plane(current)
    body = functools.partial(last_evaluation, SWEEPS - 1)
    current, bounds = called(body, (named, gathered, load, bounds), (shaped(1, width), shaped(SWEEPS, 2)), "last_evaluation")
    return current.reshape(width), bounds


def solution(mesh):
    split = Mesh(mesh.devices.reshape(4, 4, 8, 2), AXES)
    placed = (
        P(None, AXES, None, None, None),
        P(AXES),
        P(AXES, None),
        P(None, AXES),
        P(None, AXES),
        P(AXES),
    )
    return jax.shard_map(local, mesh=split, in_specs=placed, out_specs=(P(AXES), P()), check_vma=False)
```

time: 132 us -> 129 us (0.977)
  blocking collectives: 116 us -> 112 us
  Pallas kernels: 10.1 us -> 6.8 us
  waiting for transfers between devices: 0.01 us -> 3.23 us
    all_to_all x3, blocking collectives: 44.7 us -> 38.5 us  [over_plane(): return lax.all_to_all(rows, PLANE, 0, 0, tiled=True)]
    pallas_call x7, Pallas kernels: 10.1 us -> 6.8 us  [the longest x6 3.75 us: called(): pl.pallas_call(body, out_shape=out_shape, in_specs=[VECTORS] * (len(given...]
    ppermute x3 -> x7, waiting for transfers between devices: 0.01 us -> 3.23 us  [the longest x4 3.22 us: local(): loads += [lax.ppermute(held, LINE[1], [(0, 1), (1, 0)]) for held in loads]]
    all_to_all x3, blocking collectives: 71 us -> 73.2 us  [over_all(): return lax.all_to_all(rows, ORDER, 0, 0, tiled=True)]
    ppermute x3 -> x7, starting transfers between devices: 4.51 us -> 5.71 us  [the longest x3 4.51 us: local(): lax.ppermute(load, LINE[0], [(i, (i + k) % far) for i in range(far)])]
  transfers between devices with their start and end apart: 3 -> 7, of which waited for: 0 -> 4; matrix products, arithmetic and copies ran while one was open for 0% -> 0% of each run, Pallas kernels for 1% -> 1%
where the time goes in v10:
time: 129 us
  blocking collectives  112 us (87%)
  Pallas kernels  6.8 us (5%)
  starting transfers between devices  5.71 us (4%)
  waiting for transfers between devices  3.23 us (3%)
  between operations  1.37 us (1%)
    all_to_all x3, blocking collectives, over_all(): return lax.all_to_all(rows, ORDER, 0, 0, tiled=True)  73.2 us
    all_to_all x3, blocking collectives, over_plane(): return lax.all_to_all(rows, PLANE, 0, 0, tiled=True)  38.5 us
    ppermute x3, starting transfers between devices, local(): lax.ppermute(load, LINE[0], [(i, (i + k) % far) for i in range(far)])  4.51 us
    pallas_call x6, Pallas kernels, called(): pl.pallas_call(body, out_shape=out_shape, in_specs=[VECTORS] * (len(given...  3.75 us
    ppermute x4, waiting for transfers between devices, local(): loads += [lax.ppermute(held, LINE[1], [(0, 1), (1, 0)]) for held in loads]  3.22 us
    pallas_call x1, Pallas kernels, local(): pl.pallas_call(prepare, out_shape=(shaped(AUX, width), shaped(actions, wi...  3.05 us
  transfers between devices with their start and end apart: 7, of which 4 were waited for; matrix products, arithmetic and copies ran while one was open for 0% of the time, Pallas kernels for 1%

profile of v10, /device:TPU:1, one launch (start us, length us, event | category | flops | bytes accessed | tf_op | source)
XLA Modules:
  0.0 128.9 jit_solution(4287525743138690556)
XLA Ops:
  0.6 0.0 copy-start
  0.6 0.0 copy-start.1
  1.3 3.0 %prepare.1 = (f32[8,128]{1,0:T(8,128)S(1)}, f32[16,128]{1,0:T(8,128)S(1)}, f32[1040,128]{1,0:T(8,128)S(1)}, f32[16,4,128,128]{3,2,1,0:T(8,128)S(1)}) custom-call(s32[1]{0:T(128)S(6)} %copy.10.counts, s32[1,1]{1,0:T(1,128)} %bitcast.at, s32[1,4]{1,0:T(1,128)} %columns_in.1, s32[2,128]{1,0:T(2,128)} %policy_in.1, f32[16,128]{1,0:T(8,128)} %reward.3, ...), custom_call_target="tpu_custom_call" | custom-call | flops 4000000 | bytes 8000000 | tf_op jit(solution)/shard_map/prepare/pallas_call | solution.py:228
  4.4 3.4 %collective-permute-start.2 = (f32[1040,128]{1,0:T(8,128)S(1)}, f32[1040,128]{1,0:T(8,128)S(1)}, u32[]{:S(2)}, u32[]{:S(2)}) collective-permute-start(f32[1040,128]{1,0:T(8,128)S(1)} %get-tuple-element.22.refs_0_.load), channel_id=1, source_target_pairs={{0,192},{64,0},{128,64},{192,128},{1,193},{65,1},{129,65},{193,129... | collective-permute-start | bytes 1597448 | tf_op jit(solution)/shard_map/ppermute | solution.py:252
  7.8 0.5 collective-permute-start.1
  8.3 0.6 collective-permute-start
  8.9 0.0 copy-done.1
  8.9 0.1 broadcast_in_dim.2
  9.0 29.6 %all_to_all.64 = f32[256,1,128]{2,1,0:T(1,128)S(1)} all-to-all(f32[256,1,128]{2,1,0:T(1,128)S(1)} %broadcast_in_dim.2), channel_id=1, replica_groups=mesh['x'=4,'y'=4,'z'=8,'c'=2] {'y','z','x','c'}, dimensions={0} | all-to-all | bytes 262144 | tf_op jit(solution)/shard_map/all_to_all | solution.py:213
  38.6 0.0 copy-done
  38.6 0.7 back_up_0.1
  39.2 23.2 %all_to_all.65 = f32[256,1,128]{2,1,0:T(1,128)S(1)} all-to-all(f32[256,1,128]{2,1,0:T(1,128)S(1)} %bitcast.27), channel_id=1, replica_groups=mesh['x'=4,'y'=4,'z'=8,'c'=2] {'y','z','x','c'}, dimensions={0} | all-to-all | bytes 262144 | tf_op jit(solution)/shard_map/all_to_all | solution.py:213
  62.5 0.0 collective-permute-done.2.refs_3_
  62.5 0.0 collective-permute-done.1.refs_2_
  62.5 0.0 collective-permute-done.refs_1_
  62.5 0.6 collective-permute-start.3
  63.1 0.1 collective-permute-start.4
  63.2 0.4 collective-permute-start.5
  63.6 0.1 collective-permute-start.6
  63.7 0.9 collective-permute-done.3.refs_4_
  64.6 0.8 collective-permute-done.4.refs_5_
  65.4 0.8 collective-permute-done.5.refs_6_
  66.1 0.8 collective-permute-done.6.refs_7_
  66.9 0.5 first_evaluation_0.1
  67.4 12.6 %all_to_all.66 = f32[32,8,128]{2,1,0:T(8,128)S(1)} all-to-all(f32[32,8,128]{2,1,0:T(8,128)S(1)} %bitcast.30), channel_id=1, replica_groups=mesh['x'=4,'y'=4,'z'=8,'c'=2] {'y','z'}, dimensions={0} | all-to-all | bytes 262144 | tf_op jit(solution)/shard_map/all_to_all | solution.py:217
  80.0 0.5 next_evaluation_0.1
  80.5 13.3 %all_to_all.67 = f32[32,8,128]{2,1,0:T(8,128)S(1)} all-to-all(f32[32,8,128]{2,1,0:T(8,128)S(1)} %bitcast.26), channel_id=1, replica_groups=mesh['x'=4,'y'=4,'z'=8,'c'=2] {'y','z'}, dimensions={0} | all-to-all | bytes 262144 | tf_op jit(solution)/shard_map/all_to_all | solution.py:217
  93.9 0.7 back_up_1.1
  94.6 20.4 %all_to_all.68 = f32[256,1,128]{2,1,0:T(1,128)S(1)} all-to-all(f32[256,1,128]{2,1,0:T(1,128)S(1)} %bitcast.24), channel_id=1, replica_groups=mesh['x'=4,'y'=4,'z'=8,'c'=2] {'y','z','x','c'}, dimensions={0} | all-to-all | bytes 262144 | tf_op jit(solution)/shard_map/all_to_all | solution.py:213
  114.9 0.5 first_evaluation_1.1
  115.5 12.6 %all_to_all.69 = f32[32,8,128]{2,1,0:T(8,128)S(1)} all-to-all(f32[32,8,128]{2,1,0:T(8,128)S(1)} %bitcast.29), channel_id=1, replica_groups=mesh['x'=4,'y'=4,'z'=8,'c'=2] {'y','z'}, dimensions={0} | all-to-all | bytes 262144 | tf_op jit(solution)/shard_map/all_to_all | solution.py:217
  128.0 0.8 last_evaluation.1
  (1 shorter events, 0.0 us)
Async XLA Ops:
  0.6 37.9 %copy-start = (f32[16,128]{1,0:T(8,128)S(1)}, f32[16,128]{1,0:T(8,128)}, u32[]{:S(2)}) copy-start(f32[16,128]{1,0:T(8,128)} %reward.3) | copy-start | bytes 24580
  0.6 8.2 %copy-start.1 = (f32[128]{0:T(128)S(1)}, f32[128]{0:T(128)}, u32[]{:S(2)}) copy-start(f32[128]{0:T(128)} %param.11) | copy-start | bytes 1540
  4.4 58.1 %collective-permute-start.2 = (f32[1040,128]{1,0:T(8,128)S(1)}, f32[1040,128]{1,0:T(8,128)S(1)}, u32[]{:S(2)}, u32[]{:S(2)}) collective-permute-start(f32[1040,128]{1,0:T(8,128)S(1)} %get-tuple-element.22.refs_0_.load), channel_id=1, source_target_pairs={{0,192},{64,0},{128,64},{192,128},{1,193},{65,1},{129,65},{193,129... | collective-permute-start | bytes 1597448 | tf_op jit(solution)/shard_map/ppermute | solution.py:252
  7.8 54.7 %collective-permute-start.1 = (f32[1040,128]{1,0:T(8,128)S(1)}, f32[1040,128]{1,0:T(8,128)S(1)}, u32[]{:S(2)}, u32[]{:S(2)}) collective-permute-start(f32[1040,128]{1,0:T(8,128)S(1)} %get-tuple-element.22.refs_0_.load), channel_id=1, source_target_pairs={{0,128},{64,192},{128,0},{192,64},{1,129},{65,193},{129,1},{193,65... | collective-permute-start | bytes 1597448 | tf_op jit(solution)/shard_map/ppermute | solution.py:252
  8.3 54.2 %collective-permute-start = (f32[1040,128]{1,0:T(8,128)S(1)}, f32[1040,128]{1,0:T(8,128)S(1)}, u32[]{:S(2)}, u32[]{:S(2)}) collective-permute-start(f32[1040,128]{1,0:T(8,128)S(1)} %get-tuple-element.22.refs_0_.load), channel_id=1, source_target_pairs={{0,64},{64,128},{128,192},{192,0},{1,65},{65,129},{129,193},{193,1... | collective-permute-start | bytes 1597448 | tf_op jit(solution)/shard_map/ppermute | solution.py:252
  62.5 2.1 %collective-permute-start.3 = (f32[1040,128]{1,0:T(8,128)S(1)}, f32[1040,128]{1,0:T(8,128)S(1)}, u32[]{:S(2)}, u32[]{:S(2)}) collective-permute-start(f32[1040,128]{1,0:T(8,128)S(1)} %get-tuple-element.22.refs_0_.load), channel_id=1, source_target_pairs={{0,1},{1,0},{2,3},{3,2},{4,5},{5,4},{6,7},{7,6},{8,9},{9,8},{10,11... | collective-permute-start | bytes 1597448 | tf_op jit(solution)/shard_map/ppermute | solution.py:260
  63.1 2.3 %collective-permute-start.4 = (f32[1040,128]{1,0:T(8,128)S(1)}, f32[1040,128]{1,0:T(8,128)S(1)}, u32[]{:S(2)}, u32[]{:S(2)}) collective-permute-start(f32[1040,128]{1,0:T(8,128)S(1)} %collective-permute-done.refs_1_), channel_id=1, source_target_pairs={{0,1},{1,0},{2,3},{3,2},{4,5},{5,4},{6,7},{7,6},{8,9},{9,8},{10,11... | collective-permute-start | bytes 1597448 | tf_op jit(solution)/shard_map/ppermute | solution.py:260
  63.2 3.0 %collective-permute-start.5 = (f32[1040,128]{1,0:T(8,128)S(1)}, f32[1040,128]{1,0:T(8,128)S(1)}, u32[]{:S(2)}, u32[]{:S(2)}) collective-permute-start(f32[1040,128]{1,0:T(8,128)S(1)} %collective-permute-done.1.refs_2_), channel_id=1, source_target_pairs={{0,1},{1,0},{2,3},{3,2},{4,5},{5,4},{6,7},{7,6},{8,9},{9,8},{10,11... | collective-permute-start | bytes 1597448 | tf_op jit(solution)/shard_map/ppermute | solution.py:260
  63.6 3.3 %collective-permute-start.6 = (f32[1040,128]{1,0:T(8,128)S(1)}, f32[1040,128]{1,0:T(8,128)S(1)}, u32[]{:S(2)}, u32[]{:S(2)}) collective-permute-start(f32[1040,128]{1,0:T(8,128)S(1)} %collective-permute-done.2.refs_3_), channel_id=1, source_target_pairs={{0,1},{1,0},{2,3},{3,2},{4,5},{5,4},{6,7},{7,6},{8,9},{9,8},{10,11... | collective-permute-start | bytes 1597448 | tf_op jit(solution)/shard_map/ppermute | solution.py:260

commit v11 on v10

--- a/solution.py
+++ b/solution.py
@@ -250,14 +250,14 @@
     )(counts, lax.axis_index(LINE).reshape(1, 1), *(pltpu.with_memory_space_constraint(x, pltpu.HBM) for x in given))
     far = lax.axis_size(LINE[0])
     loads = [load] + [lax.ppermute(load, LINE[0], [(i, (i + k) % far) for i in range(far)]) for k in range(1, far)]
+    near = lax.ppermute(load, LINE[1], [(0, 1), (1, 0)])
+    *others, gathered = lax.optimization_barrier((*loads[1:], gathered))
+    loads = [load, *others, near] + [lax.ppermute(held, LINE[1], [(0, 1), (1, 0)]) for held in others]
     bounds = jnp.zeros((SWEEPS, 2), jnp.float32)
     all_rows = shaped(devices, width)
     for j in range(SWEEPS):
         backup = called(back_up, (named, gathered, kept, reward, scale), all_rows, f"back_up_{j}", [square])
         before, gathered = gathered, over_all(backup)
-        if j == 0:
-            *loads, gathered = lax.optimization_barrier((*loads, gathered))
-            loads += [lax.ppermute(held, LINE[1], [(0, 1), (1, 0)]) for held in loads]
         body = functools.partial(first_evaluation, j)
         made = (all_rows, shaped(SWEEPS, 2))
         current, bounds = called(body, (gathered, before, bounds, *loads), made, f"first_evaluation_{j}")

time: 129 us -> 134 us (1.039)
  blocking collectives: 112 us -> 58.7 us
  starting transfers between devices: 5.71 us -> 33 us
  waiting for transfers between devices: 3.23 us -> 24.5 us
  local copies, waits for them, and re-layouts: 0.08 us -> 5.54 us
  Pallas kernels: 6.8 us -> 10.5 us
    all_to_all x3 -> x1, blocking collectives: 73.2 us -> 20.8 us  [over_all(): return lax.all_to_all(rows, ORDER, 0, 0, tiled=True)]
    all_to_all x0 -> x2, starting transfers between devices: none -> 25.1 us  [over_all(): return lax.all_to_all(rows, ORDER, 0, 0, tiled=True)]
    all_to_all x0 -> x2, waiting for transfers between devices: none -> 24.5 us  [over_all(): return lax.all_to_all(rows, ORDER, 0, 0, tiled=True)]
    unnamed x4 -> x12, local copies, waits for them, and re-layouts: 0.01 us -> 4.81 us
    pallas_call x6, Pallas kernels: 3.75 us -> 7.5 us  [called(): pl.pallas_call(body, out_shape=out_shape, in_specs=[VECTORS] * (len(given...]
    ppermute x4, waiting for transfers between devices: 3.22 us -> 0.01 us  [the longest x3 0.01 us: local(): lax.ppermute(held, LINE[1], [(0, 1), (1, 0)])]
    ppermute x4, starting transfers between devices: 1.2 us -> 3.48 us  [the longest x1 2.23 us: local(): near = lax.ppermute(load, LINE[1], [(0, 1), (1, 0)])]
  transfers between devices with their start and end apart: 7 -> 9, of which waited for: 4 -> 2; matrix products, arithmetic and copies ran while one was open for 0% -> 1% of each run, Pallas kernels for 1% -> 1%
where the time goes in v11:
time: 134 us
  blocking collectives  58.7 us (44%)
  starting transfers between devices  33 us (25%)
  waiting for transfers between devices  24.5 us (18%)
  Pallas kernels  10.5 us (8%)
  local copies, waits for them, and re-layouts  5.54 us (4%)
  between operations  1.43 us (1%)
    all_to_all x3, blocking collectives, over_plane(): return lax.all_to_all(rows, PLANE, 0, 0, tiled=True)  38 us
    all_to_all x2, starting transfers between devices, over_all(): return lax.all_to_all(rows, ORDER, 0, 0, tiled=True)  25.1 us
    all_to_all x2, waiting for transfers between devices, over_all(): return lax.all_to_all(rows, ORDER, 0, 0, tiled=True)  24.5 us
    all_to_all x1, blocking collectives, over_all(): return lax.all_to_all(rows, ORDER, 0, 0, tiled=True)  20.8 us
    pallas_call x6, Pallas kernels, called(): pl.pallas_call(body, out_shape=out_shape, in_specs=[VECTORS] * (len(given...  7.5 us
    unnamed x12, local copies, waits for them, and re-layouts  4.81 us
    ppermute x3, starting transfers between devices, local(): lax.ppermute(load, LINE[0], [(i, (i + k) % far) for i in range(far)])  4.43 us
    pallas_call x1, Pallas kernels, local(): pl.pallas_call(prepare, out_shape=(shaped(AUX, width), shaped(actions, wi...  3.05 us
  transfers between devices with their start and end apart: 9, of which 2 were waited for; matrix products, arithmetic and copies ran while one was open for 1% of the time, Pallas kernels for 1%

profile of v11, /device:TPU:1, one launch (start us, length us, event | category | flops | bytes accessed | tf_op | source)
XLA Modules:
  0.0 133.7 jit_solution(13104372973536502668)
XLA Ops:
  1.3 3.0 %prepare.1 = (f32[8,128]{1,0:T(8,128)S(1)}, f32[16,128]{1,0:T(8,128)S(1)}, f32[1040,128]{1,0:T(8,128)S(1)}, f32[16,4,128,128]{3,2,1,0:T(8,128)S(1)}) custom-call(s32[1]{0:T(128)S(6)} %copy.10.counts, s32[1,1]{1,0:T(1,128)} %bitcast.at, s32[1,4]{1,0:T(1,128)} %columns_in.1, s32[2,128]{1,0:T(2,128)} %policy_in.1, f32[16,128]{1,0:T(8,128)} %reward.3, ...), custom_call_target="tpu_custom_call" | custom-call | flops 4000000 | bytes 8000000 | tf_op jit(solution)/shard_map/prepare/pallas_call | solution.py:228
  4.4 1.9 %copy-done = f32[16,4,128,128]{3,2,1,0:T(8,128)} copy-done((f32[16,4,128,128]{3,2,1,0:T(8,128)}, f32[16,4,128,128]{3,2,1,0:T(8,128)S(1)}, u32[]{:S(2)}) %copy-start) | copy-done | bytes 4194328
  6.3 3.3 %collective-permute-start.2 = (f32[1040,128]{1,0:T(8,128)S(1)}, f32[1040,128]{1,0:T(8,128)S(1)}, u32[]{:S(2)}, u32[]{:S(2)}) collective-permute-start(f32[1040,128]{1,0:T(8,128)S(1)} %get-tuple-element.17.refs_0_.load), channel_id=1, source_target_pairs={{0,192},{64,0},{128,64},{192,128},{1,193},{65,1},{129,65},{193,129... | collective-permute-start | bytes 1597448 | tf_op jit(solution)/shard_map/ppermute | solution.py:252
  9.6 0.5 collective-permute-start.1
  10.1 0.6 collective-permute-start
  10.8 0.7 broadcast_in_dim.2
  11.5 15.0 %all-to-all-start = ((f32[256,1,128]{2,1,0:T(1,128)}), f32[256,1,128]{2,1,0:T(1,128)S(1)}, u32[]{:S(2)}, u32[]{:S(2)}) async-start(f32[256,1,128]{2,1,0:T(1,128)} %broadcast_in_dim.2), calls=%async_computation | async-start | bytes 262144 | tf_op jit(solution)/shard_map/all_to_all | solution.py:213
  26.5 2.2 %collective-permute-start.3 = (f32[1040,128]{1,0:T(8,128)S(1)}, f32[1040,128]{1,0:T(8,128)S(1)}, u32[]{:S(2)}, u32[]{:S(2)}) collective-permute-start(f32[1040,128]{1,0:T(8,128)S(1)} %get-tuple-element.17.refs_0_.load), channel_id=1, source_target_pairs={{0,1},{1,0},{2,3},{3,2},{4,5},{5,4},{6,7},{7,6},{8,9},{9,8},{10,11... | collective-permute-start | bytes 1597448 | tf_op jit(solution)/shard_map/ppermute | solution.py:253
  28.7 11.7 %all-to-all-done = f32[256,1,128]{2,1,0:T(1,128)S(1)} async-done(((f32[256,1,128]{2,1,0:T(1,128)}), f32[256,1,128]{2,1,0:T(1,128)S(1)}, u32[]{:S(2)}, u32[]{:S(2)}) %all-to-all-start) | async-done | bytes 131104 | tf_op jit(solution)/shard_map/all_to_all | solution.py:213
  40.4 0.0 collective-permute-done.2.refs_3_
  40.4 0.0 collective-permute-done.1.refs_2_
  40.4 0.0 collective-permute-done.refs_1_
  40.4 0.7 collective-permute-start.4
  41.2 0.1 collective-permute-start.5
  41.3 0.4 collective-permute-start.6
  41.7 2.2 %copy-done.1 = f32[16,4,128,128]{3,2,1,0:T(8,128)S(1)} copy-done((f32[16,4,128,128]{3,2,1,0:T(8,128)S(1)}, f32[16,4,128,128]{3,2,1,0:T(8,128)}, u32[]{:S(2)}) %copy-start.1) | copy-done | bytes 4194328
  43.9 0.7 back_up_0.1
  44.6 0.7 copy-done.3
  45.2 10.1 %all-to-all-start.1 = ((f32[256,1,128]{2,1,0:T(1,128)}), f32[256,1,128]{2,1,0:T(1,128)S(1)}, u32[]{:S(2)}, u32[]{:S(2)}) async-start(f32[256,1,128]{2,1,0:T(1,128)} %bitcast.24), calls=%async_computation.1 | async-start | bytes 262144 | tf_op jit(solution)/shard_map/all_to_all | solution.py:213
  55.4 12.8 %all-to-all-done.1 = f32[256,1,128]{2,1,0:T(1,128)S(1)} async-done(((f32[256,1,128]{2,1,0:T(1,128)}), f32[256,1,128]{2,1,0:T(1,128)S(1)}, u32[]{:S(2)}, u32[]{:S(2)}) %all-to-all-start.1) | async-done | bytes 131104 | tf_op jit(solution)/shard_map/all_to_all | solution.py:213
  68.1 0.0 collective-permute-done.4.refs_5_
  68.1 0.0 collective-permute-done.5.refs_6_
  68.1 0.0 collective-permute-done.6.refs_7_
  68.2 1.9 %first_evaluation_0.1 = (f32[256,128]{1,0:T(8,128)S(1)}, f32[2,2]{1,0:T(2,128)S(1)}) custom-call(f32[256,128]{1,0:T(8,128)S(1)} %bitcast.22, f32[256,128]{1,0:T(8,128)S(1)} %bitcast.19, f32[2,2]{1,0:T(2,128)S(1)} %broadcast_1_held.2.held, f32[1040,128]{1,0:T(8,128)S(1)} %get-tuple-element.17.refs_0_.load, f32[1040,128]{1,0:T(8,128)S(1)} %collective-permute-done.refs_1_, ...), custom_call_target="tpu_custom_call" | custom-call | tf_op jit(solution)/shard_map/first_evaluation_0/pallas_call | solution.py:201
  70.0 12.6 %all_to_all.64 = f32[32,8,128]{2,1,0:T(8,128)S(1)} all-to-all(f32[32,8,128]{2,1,0:T(8,128)S(1)} %bitcast.30), channel_id=1, replica_groups=mesh['x'=4,'y'=4,'z'=8,'c'=2] {'y','z'}, dimensions={0} | all-to-all | bytes 262144 | tf_op jit(solution)/shard_map/all_to_all | solution.py:217
  82.6 1.7 %next_evaluation_0.1 = f32[256,128]{1,0:T(8,128)S(1)} custom-call(f32[256,128]{1,0:T(8,128)S(1)} %bitcast.26, f32[1040,128]{1,0:T(8,128)S(1)} %get-tuple-element.17.refs_0_.load, f32[1040,128]{1,0:T(8,128)S(1)} %collective-permute-done.refs_1_, f32[1040,128]{1,0:T(8,128)S(1)} %collective-permute-done.1.refs_2_, ...), custom_call_target="tpu_custom_call" | custom-call | tf_op jit(solution)/shard_map/next_evaluation_0/pallas_call | solution.py:201
  84.4 12.8 %all_to_all.65 = f32[32,8,128]{2,1,0:T(8,128)S(1)} all-to-all(f32[32,8,128]{2,1,0:T(8,128)S(1)} %bitcast.27), channel_id=1, replica_groups=mesh['x'=4,'y'=4,'z'=8,'c'=2] {'y','z'}, dimensions={0} | all-to-all | bytes 262144 | tf_op jit(solution)/shard_map/all_to_all | solution.py:217
  97.2 0.7 back_up_1.1
  97.8 20.8 %all_to_all.66 = f32[256,1,128]{2,1,0:T(1,128)S(1)} all-to-all(f32[256,1,128]{2,1,0:T(1,128)S(1)} %bitcast.25), channel_id=1, replica_groups=mesh['x'=4,'y'=4,'z'=8,'c'=2] {'y','z','x','c'}, dimensions={0} | all-to-all | bytes 262144 | tf_op jit(solution)/shard_map/all_to_all | solution.py:213
  118.6 1.7 %first_evaluation_1.1 = (f32[256,128]{1,0:T(8,128)S(1)}, f32[2,2]{1,0:T(2,128)S(1)}) custom-call(f32[256,128]{1,0:T(8,128)S(1)} %bitcast.23, f32[256,128]{1,0:T(8,128)S(1)} %bitcast.21, f32[2,2]{1,0:T(2,128)S(1)} %get-tuple-element.25.held, f32[1040,128]{1,0:T(8,128)S(1)} %get-tuple-element.17.refs_0_.load, f32[1040,128]{1,0:T(8,128)S(1)} %collective-permute-done.refs_1_, ...), custom_call_target="tpu_custom_call" | custom-call | tf_op jit(solution)/shard_map/first_evaluation_1/pallas_call | solution.py:201
  120.3 12.6 %all_to_all.67 = f32[32,8,128]{2,1,0:T(8,128)S(1)} all-to-all(f32[32,8,128]{2,1,0:T(8,128)S(1)} %bitcast.29), channel_id=1, replica_groups=mesh['x'=4,'y'=4,'z'=8,'c'=2] {'y','z'}, dimensions={0} | all-to-all | bytes 262144 | tf_op jit(solution)/shard_map/all_to_all | solution.py:217
  132.9 0.8 last_evaluation.1
  (11 shorter events, 0.0 us)
Async XLA Ops:
  0.6 41.1 %copy-start.4 = (f32[16,128]{1,0:T(8,128)S(1)}, f32[16,128]{1,0:T(8,128)}, u32[]{:S(2)}) copy-start(f32[16,128]{1,0:T(8,128)} %reward.3) | copy-start | bytes 24580
  0.6 10.1 %copy-start.5 = (f32[128]{0:T(128)S(1)}, f32[128]{0:T(128)}, u32[]{:S(2)}) copy-start(f32[128]{0:T(128)} %param.11) | copy-start | bytes 1540
  4.4 1.9 %copy-start = (f32[16,4,128,128]{3,2,1,0:T(8,128)}, f32[16,4,128,128]{3,2,1,0:T(8,128)S(1)}, u32[]{:S(2)}) copy-start(f32[16,4,128,128]{3,2,1,0:T(8,128)S(1)} %get-tuple-element.19.tiles) | copy-start | bytes 12582916
  6.3 34.1 %collective-permute-start.2 = (f32[1040,128]{1,0:T(8,128)S(1)}, f32[1040,128]{1,0:T(8,128)S(1)}, u32[]{:S(2)}, u32[]{:S(2)}) collective-permute-start(f32[1040,128]{1,0:T(8,128)S(1)} %get-tuple-element.17.refs_0_.load), channel_id=1, source_target_pairs={{0,192},{64,0},{128,64},{192,128},{1,193},{65,1},{129,65},{193,129... | collective-permute-start | bytes 1597448 | tf_op jit(solution)/shard_map/ppermute | solution.py:252
  9.6 30.8 %collective-permute-start.1 = (f32[1040,128]{1,0:T(8,128)S(1)}, f32[1040,128]{1,0:T(8,128)S(1)}, u32[]{:S(2)}, u32[]{:S(2)}) collective-permute-start(f32[1040,128]{1,0:T(8,128)S(1)} %get-tuple-element.17.refs_0_.load), channel_id=1, source_target_pairs={{0,128},{64,192},{128,0},{192,64},{1,129},{65,193},{129,1},{193,65... | collective-permute-start | bytes 1597448 | tf_op jit(solution)/shard_map/ppermute | solution.py:252
  10.1 30.3 %collective-permute-start = (f32[1040,128]{1,0:T(8,128)S(1)}, f32[1040,128]{1,0:T(8,128)S(1)}, u32[]{:S(2)}, u32[]{:S(2)}) collective-permute-start(f32[1040,128]{1,0:T(8,128)S(1)} %get-tuple-element.17.refs_0_.load), channel_id=1, source_target_pairs={{0,64},{64,128},{128,192},{192,0},{1,65},{65,129},{129,193},{193,1... | collective-permute-start | bytes 1597448 | tf_op jit(solution)/shard_map/ppermute | solution.py:252
  11.5 28.9 %all-to-all-start = ((f32[256,1,128]{2,1,0:T(1,128)}), f32[256,1,128]{2,1,0:T(1,128)S(1)}, u32[]{:S(2)}, u32[]{:S(2)}) async-start(f32[256,1,128]{2,1,0:T(1,128)} %broadcast_in_dim.2), calls=%async_computation | async-start | bytes 262144 | tf_op jit(solution)/shard_map/all_to_all | solution.py:213
  26.5 28.9 %collective-permute-start.3 = (f32[1040,128]{1,0:T(8,128)S(1)}, f32[1040,128]{1,0:T(8,128)S(1)}, u32[]{:S(2)}, u32[]{:S(2)}) collective-permute-start(f32[1040,128]{1,0:T(8,128)S(1)} %get-tuple-element.17.refs_0_.load), channel_id=1, source_target_pairs={{0,1},{1,0},{2,3},{3,2},{4,5},{5,4},{6,7},{7,6},{8,9},{9,8},{10,11... | collective-permute-start | bytes 1597448 | tf_op jit(solution)/shard_map/ppermute | solution.py:253
  40.4 27.7 %collective-permute-start.4 = (f32[1040,128]{1,0:T(8,128)S(1)}, f32[1040,128]{1,0:T(8,128)S(1)}, u32[]{:S(2)}, u32[]{:S(2)}) collective-permute-start(f32[1040,128]{1,0:T(8,128)S(1)} %collective-permute-done.refs_1_), channel_id=1, source_target_pairs={{0,1},{1,0},{2,3},{3,2},{4,5},{5,4},{6,7},{7,6},{8,9},{9,8},{10,11... | collective-permute-start | bytes 1597448 | tf_op jit(solution)/shard_map/ppermute | solution.py:255
  41.2 27.0 %collective-permute-start.5 = (f32[1040,128]{1,0:T(8,128)S(1)}, f32[1040,128]{1,0:T(8,128)}, u32[]{:S(2)}, u32[]{:S(2)}) collective-permute-start(f32[1040,128]{1,0:T(8,128)S(1)} %collective-permute-done.1.refs_2_), channel_id=1, source_target_pairs={{0,1},{1,0},{2,3},{3,2},{4,5},{5,4},{6,7},{7,6},{8,9},{9,8},{10,11... | collective-permute-start | bytes 1597448 | tf_op jit(solution)/shard_map/ppermute | solution.py:255
  41.3 26.9 %collective-permute-start.6 = (f32[1040,128]{1,0:T(8,128)S(1)}, f32[1040,128]{1,0:T(8,128)}, u32[]{:S(2)}, u32[]{:S(2)}) collective-permute-start(f32[1040,128]{1,0:T(8,128)S(1)} %collective-permute-done.2.refs_3_), channel_id=1, source_target_pairs={{0,1},{1,0},{2,3},{3,2},{4,5},{5,4},{6,7},{7,6},{8,9},{9,8},{10,11... | collective-permute-start | bytes 1597448 | tf_op jit(solution)/shard_map/ppermute | solution.py:255
  41.7 2.2 %copy-start.1 = (f32[16,4,128,128]{3,2,1,0:T(8,128)S(1)}, f32[16,4,128,128]{3,2,1,0:T(8,128)}, u32[]{:S(2)}) copy-start(f32[16,4,128,128]{3,2,1,0:T(8,128)} %copy-done) | copy-start | bytes 12582916
  44.6 0.7 copy-start.3
  45.2 22.9 %all-to-all-start.1 = ((f32[256,1,128]{2,1,0:T(1,128)}), f32[256,1,128]{2,1,0:T(1,128)S(1)}, u32[]{:S(2)}, u32[]{:S(2)}) async-start(f32[256,1,128]{2,1,0:T(1,128)} %bitcast.24), calls=%async_computation.1 | async-start | bytes 262144 | tf_op jit(solution)/shard_map/all_to_all | solution.py:213
  68.2 29.0 %copy-start.2 = (f32[16,4,128,128]{3,2,1,0:T(8,128)S(1)}, f32[16,4,128,128]{3,2,1,0:T(8,128)}, u32[]{:S(2)}) copy-start(f32[16,4,128,128]{3,2,1,0:T(8,128)} %copy-done) | copy-start | bytes 12582916

commit v12 on v11

--- a/solution.py
+++ b/solution.py
@@ -250,9 +250,8 @@
     )(counts, lax.axis_index(LINE).reshape(1, 1), *(pltpu.with_memory_space_constraint(x, pltpu.HBM) for x in given))
     far = lax.axis_size(LINE[0])
     loads = [load] + [lax.ppermute(load, LINE[0], [(i, (i + k) % far) for i in range(far)]) for k in range(1, far)]
-    near = lax.ppermute(load, LINE[1], [(0, 1), (1, 0)])
-    *others, gathered = lax.optimization_barrier((*loads[1:], gathered))
-    loads = [load, *others, near] + [lax.ppermute(held, LINE[1], [(0, 1), (1, 0)]) for held in others]
+    *loads, gathered = lax.optimization_barrier((*loads, gathered))
+    loads += [lax.ppermute(held, LINE[1], [(0, 1), (1, 0)]) for held in loads]
     bounds = jnp.zeros((SWEEPS, 2), jnp.float32)
     all_rows = shaped(devices, width)
     for j in range(SWEEPS):

time: 134 us -> 126 us (0.940)
  blocking collectives: 58.7 us -> 111 us
  starting transfers between devices: 33 us -> 5.86 us
  waiting for transfers between devices: 24.5 us -> 0.02 us
  local copies, waits for them, and re-layouts: 5.54 us -> 0.08 us
  Pallas kernels: 10.5 us -> 6.8 us
    all_to_all x1 -> x3, blocking collectives: 20.8 us -> 73.3 us  [over_all(): return lax.all_to_all(rows, ORDER, 0, 0, tiled=True)]
    all_to_all x2 -> x0, starting transfers between devices: 25.1 us -> none  [over_all(): return lax.all_to_all(rows, ORDER, 0, 0, tiled=True)]
    all_to_all x2 -> x0, waiting for transfers between devices: 24.5 us -> none  [over_all(): return lax.all_to_all(rows, ORDER, 0, 0, tiled=True)]
    unnamed x12 -> x4, local copies, waits for them, and re-layouts: 4.81 us -> 0.01 us
    pallas_call x6, Pallas kernels: 7.5 us -> 3.75 us  [called(): pl.pallas_call(body, out_shape=out_shape, in_specs=[VECTORS] * (len(given...]
    ppermute x4, starting transfers between devices: 3.48 us -> 1.35 us  [local(): loads += [lax.ppermute(held, LINE[1], [(0, 1), (1, 0)]) for held in loads]]
  transfers between devices with their start and end apart: 9 -> 7, of which waited for: 2 -> 0; matrix products, arithmetic and copies ran while one was open for 1% -> 0% of each run, Pallas kernels for 1% -> 1%
where the time goes in v12:
time: 126 us; the launch traced here: 125 us
  blocking collectives  111 us (88%)
  Pallas kernels  6.8 us (5%)
  starting transfers between devices  5.86 us (5%)
  between operations  1.39 us (1%)
    all_to_all x3, blocking collectives, over_all(): return lax.all_to_all(rows, ORDER, 0, 0, tiled=True)  73.3 us
    all_to_all x3, blocking collectives, over_plane(): return lax.all_to_all(rows, PLANE, 0, 0, tiled=True)  37.9 us
    ppermute x3, starting transfers between devices, local(): lax.ppermute(load, LINE[0], [(i, (i + k) % far) for i in range(far)])  4.51 us
    pallas_call x6, Pallas kernels, called(): pl.pallas_call(body, out_shape=out_shape, in_specs=[VECTORS] * (len(given...  3.75 us
    pallas_call x1, Pallas kernels, local(): pl.pallas_call(prepare, out_shape=(shaped(AUX, width), shaped(actions, wi...  3.05 us
  transfers between devices with their start and end apart: 7, of which 0 were waited for; matrix products, arithmetic and copies ran while one was open for 0% of the time, Pallas kernels for 1%

profile of v12, /device:TPU:1, one launch (start us, length us, event | category | flops | bytes accessed | tf_op | source)
XLA Modules:
  0.0 125.4 jit_solution(11842806467405780308)
XLA Ops:
  0.6 0.0 copy-start
  0.6 0.0 copy-start.1
  1.3 3.0 %prepare.1 = (f32[8,128]{1,0:T(8,128)S(1)}, f32[16,128]{1,0:T(8,128)S(1)}, f32[1040,128]{1,0:T(8,128)S(1)}, f32[16,4,128,128]{3,2,1,0:T(8,128)S(1)}) custom-call(s32[1]{0:T(128)S(6)} %copy.10.counts, s32[1,1]{1,0:T(1,128)} %bitcast.at, s32[1,4]{1,0:T(1,128)} %columns_in.1, s32[2,128]{1,0:T(2,128)} %policy_in.1, f32[16,128]{1,0:T(8,128)} %reward.3, ...), custom_call_target="tpu_custom_call" | custom-call | flops 4000000 | bytes 8000000 | tf_op jit(solution)/shard_map/prepare/pallas_call | solution.py:228
  4.4 3.4 %collective-permute-start.2 = (f32[1040,128]{1,0:T(8,128)S(1)}, f32[1040,128]{1,0:T(8,128)S(1)}, u32[]{:S(2)}, u32[]{:S(2)}) collective-permute-start(f32[1040,128]{1,0:T(8,128)S(1)} %get-tuple-element.22.refs_0_.load), channel_id=1, source_target_pairs={{0,192},{64,0},{128,64},{192,128},{1,193},{65,1},{129,65},{193,129... | collective-permute-start | bytes 1597448 | tf_op jit(solution)/shard_map/ppermute | solution.py:252
  7.8 0.5 collective-permute-start.1
  8.3 0.6 collective-permute-start
  8.9 0.0 copy-done.1
  8.9 0.1 broadcast_in_dim.2
  9.0 29.6 %all_to_all.64 = f32[256,1,128]{2,1,0:T(1,128)S(1)} all-to-all(f32[256,1,128]{2,1,0:T(1,128)S(1)} %broadcast_in_dim.2), channel_id=1, replica_groups=mesh['x'=4,'y'=4,'z'=8,'c'=2] {'y','z','x','c'}, dimensions={0} | all-to-all | bytes 262144 | tf_op jit(solution)/shard_map/all_to_all | solution.py:213
  38.5 0.0 collective-permute-done.2.refs_3_
  38.6 0.0 collective-permute-done.1.refs_2_
  38.6 0.0 collective-permute-done.refs_1_
  38.6 0.7 collective-permute-start.3
  39.3 0.1 collective-permute-start.4
  39.4 0.4 collective-permute-start.5
  39.8 0.1 collective-permute-start.6
  39.9 0.0 copy-done
  39.9 0.7 back_up_0.1
  40.6 23.0 %all_to_all.65 = f32[256,1,128]{2,1,0:T(1,128)S(1)} all-to-all(f32[256,1,128]{2,1,0:T(1,128)S(1)} %bitcast.27), channel_id=1, replica_groups=mesh['x'=4,'y'=4,'z'=8,'c'=2] {'y','z','x','c'}, dimensions={0} | all-to-all | bytes 262144 | tf_op jit(solution)/shard_map/all_to_all | solution.py:213
  63.6 0.0 collective-permute-done.3.refs_4_
  63.6 0.0 collective-permute-done.4.refs_5_
  63.6 0.0 collective-permute-done.5.refs_6_
  63.6 0.0 collective-permute-done.6.refs_7_
  63.6 0.5 first_evaluation_0.1
  64.2 12.6 %all_to_all.66 = f32[32,8,128]{2,1,0:T(8,128)S(1)} all-to-all(f32[32,8,128]{2,1,0:T(8,128)S(1)} %bitcast.30), channel_id=1, replica_groups=mesh['x'=4,'y'=4,'z'=8,'c'=2] {'y','z'}, dimensions={0} | all-to-all | bytes 262144 | tf_op jit(solution)/shard_map/all_to_all | solution.py:217
  76.7 0.5 next_evaluation_0.1
  77.3 12.8 %all_to_all.67 = f32[32,8,128]{2,1,0:T(8,128)S(1)} all-to-all(f32[32,8,128]{2,1,0:T(8,128)S(1)} %bitcast.26), channel_id=1, replica_groups=mesh['x'=4,'y'=4,'z'=8,'c'=2] {'y','z'}, dimensions={0} | all-to-all | bytes 262144 | tf_op jit(solution)/shard_map/all_to_all | solution.py:217
  90.1 0.7 back_up_1.1
  90.7 20.8 %all_to_all.68 = f32[256,1,128]{2,1,0:T(1,128)S(1)} all-to-all(f32[256,1,128]{2,1,0:T(1,128)S(1)} %bitcast.24), channel_id=1, replica_groups=mesh['x'=4,'y'=4,'z'=8,'c'=2] {'y','z','x','c'}, dimensions={0} | all-to-all | bytes 262144 | tf_op jit(solution)/shard_map/all_to_all | solution.py:213
  111.5 0.5 first_evaluation_1.1
  112.0 12.6 %all_to_all.69 = f32[32,8,128]{2,1,0:T(8,128)S(1)} all-to-all(f32[32,8,128]{2,1,0:T(8,128)S(1)} %bitcast.29), channel_id=1, replica_groups=mesh['x'=4,'y'=4,'z'=8,'c'=2] {'y','z'}, dimensions={0} | all-to-all | bytes 262144 | tf_op jit(solution)/shard_map/all_to_all | solution.py:217
  124.6 0.8 last_evaluation.1
  (1 shorter events, 0.0 us)
Async XLA Ops:
  0.6 39.3 %copy-start = (f32[16,128]{1,0:T(8,128)S(1)}, f32[16,128]{1,0:T(8,128)}, u32[]{:S(2)}) copy-start(f32[16,128]{1,0:T(8,128)} %reward.3) | copy-start | bytes 24580
  0.6 8.2 %copy-start.1 = (f32[128]{0:T(128)S(1)}, f32[128]{0:T(128)}, u32[]{:S(2)}) copy-start(f32[128]{0:T(128)} %param.11) | copy-start | bytes 1540
  4.4 34.2 %collective-permute-start.2 = (f32[1040,128]{1,0:T(8,128)S(1)}, f32[1040,128]{1,0:T(8,128)S(1)}, u32[]{:S(2)}, u32[]{:S(2)}) collective-permute-start(f32[1040,128]{1,0:T(8,128)S(1)} %get-tuple-element.22.refs_0_.load), channel_id=1, source_target_pairs={{0,192},{64,0},{128,64},{192,128},{1,193},{65,1},{129,65},{193,129... | collective-permute-start | bytes 1597448 | tf_op jit(solution)/shard_map/ppermute | solution.py:252
  7.8 30.8 %collective-permute-start.1 = (f32[1040,128]{1,0:T(8,128)S(1)}, f32[1040,128]{1,0:T(8,128)S(1)}, u32[]{:S(2)}, u32[]{:S(2)}) collective-permute-start(f32[1040,128]{1,0:T(8,128)S(1)} %get-tuple-element.22.refs_0_.load), channel_id=1, source_target_pairs={{0,128},{64,192},{128,0},{192,64},{1,129},{65,193},{129,1},{193,65... | collective-permute-start | bytes 1597448 | tf_op jit(solution)/shard_map/ppermute | solution.py:252
  8.3 30.3 %collective-permute-start = (f32[1040,128]{1,0:T(8,128)S(1)}, f32[1040,128]{1,0:T(8,128)S(1)}, u32[]{:S(2)}, u32[]{:S(2)}) collective-permute-start(f32[1040,128]{1,0:T(8,128)S(1)} %get-tuple-element.22.refs_0_.load), channel_id=1, source_target_pairs={{0,64},{64,128},{128,192},{192,0},{1,65},{65,129},{129,193},{193,1... | collective-permute-start | bytes 1597448 | tf_op jit(solution)/shard_map/ppermute | solution.py:252
  38.6 25.0 %collective-permute-start.3 = (f32[1040,128]{1,0:T(8,128)S(1)}, f32[1040,128]{1,0:T(8,128)S(1)}, u32[]{:S(2)}, u32[]{:S(2)}) collective-permute-start(f32[1040,128]{1,0:T(8,128)S(1)} %get-tuple-element.22.refs_0_.load), channel_id=1, source_target_pairs={{0,1},{1,0},{2,3},{3,2},{4,5},{5,4},{6,7},{7,6},{8,9},{9,8},{10,11... | collective-permute-start | bytes 1597448 | tf_op jit(solution)/shard_map/ppermute | solution.py:254
  39.3 24.3 %collective-permute-start.4 = (f32[1040,128]{1,0:T(8,128)S(1)}, f32[1040,128]{1,0:T(8,128)S(1)}, u32[]{:S(2)}, u32[]{:S(2)}) collective-permute-start(f32[1040,128]{1,0:T(8,128)S(1)} %collective-permute-done.refs_1_), channel_id=1, source_target_pairs={{0,1},{1,0},{2,3},{3,2},{4,5},{5,4},{6,7},{7,6},{8,9},{9,8},{10,11... | collective-permute-start | bytes 1597448 | tf_op jit(solution)/shard_map/ppermute | solution.py:254
  39.4 24.2 %collective-permute-start.5 = (f32[1040,128]{1,0:T(8,128)S(1)}, f32[1040,128]{1,0:T(8,128)S(1)}, u32[]{:S(2)}, u32[]{:S(2)}) collective-permute-start(f32[1040,128]{1,0:T(8,128)S(1)} %collective-permute-done.1.refs_2_), channel_id=1, source_target_pairs={{0,1},{1,0},{2,3},{3,2},{4,5},{5,4},{6,7},{7,6},{8,9},{9,8},{10,11... | collective-permute-start | bytes 1597448 | tf_op jit(solution)/shard_map/ppermute | solution.py:254
  39.8 23.8 %collective-permute-start.6 = (f32[1040,128]{1,0:T(8,128)S(1)}, f32[1040,128]{1,0:T(8,128)S(1)}, u32[]{:S(2)}, u32[]{:S(2)}) collective-permute-start(f32[1040,128]{1,0:T(8,128)S(1)} %collective-permute-done.2.refs_3_), channel_id=1, source_target_pairs={{0,1},{1,0},{2,3},{3,2},{4,5},{5,4},{6,7},{7,6},{8,9},{9,8},{10,11... | collective-permute-start | bytes 1597448 | tf_op jit(solution)/shard_map/ppermute | solution.py:254
